TPU v7x, 1024 devices: a whole 4x4x32 slice. The times are simulated.
1024 devices in a mesh: wide: 64 (over y, z_lo, core), narrow: 16 (over x, z_hi).
Axes of the slice: x: 4, y: 4, z: 32 (z_hi: 4, z_lo: 8; z = z_hi * 8 + z_lo), core: 2. Of those that a mesh axis runs over, the one named last changes fastest.
Arguments:
- kirchhoff: float32 [256, 512, 512], P('wide', 'narrow'), may hold values from -24 to 24
- adjoint: float32 [256, 512, 512], P('wide', 'narrow'), may hold values from -24 to 24
- penalty_slope: bfloat16 [256, 512, 512], P('wide', 'narrow'), may hold values from 0.29882812 to 3
- design: float32 [256, 128, 256], P('narrow', 'wide'), may hold values from 0 to 1
- solid_mask: int32 [256, 128, 256], P('narrow', 'wide'), may hold values 0 or 1
- void_mask: int32 [256, 128, 256], P('narrow', 'wide'), may hold values 0 or 1
Outputs:
- projected_density: float32 [256, 128, 256], P('narrow', 'wide')
- design_sens: float32 [256, 128, 256], P('narrow', 'wide')
All inputs are finite; a program needn't handle non-finite values. No bound on the sum of `solid_mask` or of `void_mask` on one device may be relied on, other than what follows from the above.
Results may differ from a plain program's by a relative error of at most 0.0003.
Values sent between devices are 32-bit elements; how exact they have to be, the bound alone decides.
No kernel may reach another device: no remote copies, remote signals or barrier semaphores. Data moves between devices by JAX's collectives and lax.ppermute only.
A program may use at most 64 MiB of HBM per device.

v0:
```python
import math

import jax
import jax.numpy as jnp
from jax import lax
from jax.sharding import PartitionSpec as P

RADIUS = 12


BETA = 32.0
ETA = 0.5
LOWER_TANH = math.tanh(BETA * ETA)
SPAN_TANH = math.tanh(BETA * ETA) + math.tanh(BETA * (1.0 - ETA))
HIGHEST = lax.Precision.HIGHEST


def padded_2(shard, sides, width):
    for axis, dim in sides:
        count, length = (lax.axis_size(axis), shard.shape[dim])
        up = [(i, (i + 1) % count) for i in range(count - 1)]
        down = [(j, i) for i, j in up]
        last = lax.slice_in_dim(shard, length - width, length, axis=dim)
        initial = lax.slice_in_dim(shard, 0, width, axis=dim)
        before = lax.ppermute(last, axis, up)
        after = lax.ppermute(initial, axis, down)
        shard = jnp.concatenate([before, shard, after], axis=dim)
    return shard


def heaviside(values):
    return (LOWER_TANH + jnp.tanh(BETA * (values - ETA))) / SPAN_TANH


def heaviside_slope(values):
    inner = jnp.tanh(BETA * (values - ETA))
    return BETA * (1.0 - inner * inner) / SPAN_TANH


def restrict(ghosted, coeffs):
    grad_x = ghosted[:, 2:, 1:-1, 1:-1] - ghosted[:, :-2, 1:-1, 1:-1]
    grad_y = ghosted[:, 1:-1, 2:, 1:-1] - ghosted[:, 1:-1, :-2, 1:-1]
    grad_z = ghosted[:, 1:-1, 1:-1, 2:] - ghosted[:, 1:-1, 1:-1, :-2]
    product = grad_x[0] * grad_x[1] + grad_y[0] * grad_y[1] + grad_z[0] * grad_z[1]
    sensed = -0.25 * coeffs * product
    x_cells, y_cells, z_cells = sensed.shape
    return sensed.reshape(x_cells // 2, 2, y_cells // 2, 2, z_cells // 2, 2).sum(axis=(1, 3, 5))


def band(rows_out, rows_in, offset):
    out_pos = lax.broadcasted_iota(jnp.int32, (rows_out, rows_in), 0)
    in_pos = lax.broadcasted_iota(jnp.int32, (rows_out, rows_in), 1)
    return jnp.maximum(RADIUS + 1 - jnp.abs(in_pos - offset - out_pos), 0).astype(jnp.float32)


def cover(positions, extent):
    shifts = lax.broadcasted_iota(jnp.int32, (positions.shape[0], 2 * RADIUS + 1), 1) - RADIUS
    target = positions[:, None] + shifts
    inside = (target >= 0) & (target < extent)
    weight = (RADIUS + 1 - jnp.abs(shifts)).astype(jnp.float32)
    return jnp.sum(jnp.where(inside, weight, 0.0), axis=1)


def along_x_local(slab_part):
    x_total = slab_part.shape[1]
    return jnp.einsum("ij,zjy->ziy", band(x_total, x_total, 0), slab_part, precision=HIGHEST)


def smooth(values):
    z_cells, x_cells, y_cells = values.shape
    along_y = jnp.einsum("zxj,ji->zxi", values, band(y_cells, y_cells, 0), precision=HIGHEST)
    padded = padded_2(along_y, (("narrow", 0),), RADIUS)
    along_z = jnp.einsum(
        "ij,jxy->ixy", band(z_cells, z_cells + 2 * RADIUS, RADIUS), padded, precision=HIGHEST
    )
    transposed = along_x_local(
        lax.all_to_all(along_z, "wide", split_axis=2, concat_axis=1, tiled=True)
    )
    return lax.all_to_all(transposed, "wide", split_axis=1, concat_axis=2, tiled=True)


def per_device(kirchhoff, adjoint, penalty_slope, design, solid_mask, void_mask):
    fields = jnp.pad(jnp.stack([kirchhoff, adjoint]), ((0, 0), (0, 0), (0, 0), (1, 1)))
    z_cells, x_cells, y_cells = design.shape
    z_pos = lax.axis_index("narrow") * z_cells + lax.iota(jnp.int32, z_cells)
    x_pos = lax.axis_index("wide") * x_cells + lax.iota(jnp.int32, x_cells)
    y_pos = lax.iota(jnp.int32, y_cells)
    normalizer = (
        cover(z_pos, z_cells * lax.axis_size("narrow"))[:, None, None]
        * cover(x_pos, x_cells * lax.axis_size("wide"))[None, :, None]
        * cover(y_pos, y_cells)[None, None, :]
    )
    is_solid = solid_mask.astype(jnp.float32)
    is_void = void_mask.astype(jnp.float32)
    live = (1.0 - is_solid) * (1.0 - is_void)
    filtered = smooth(design) / normalizer
    projected = heaviside(filtered) * live + is_solid * (1.0 - is_void)
    ghosted = padded_2(fields, (("wide", 1), ("narrow", 2)), 1)
    coarse = restrict(ghosted, penalty_slope.astype(jnp.float32))
    coarse = jnp.transpose(coarse, (2, 0, 1))
    arrived = lax.all_to_all(coarse, "narrow", split_axis=0, concat_axis=2, tiled=True)
    weighted = heaviside_slope(filtered) * arrived * live / normalizer
    design_sens = smooth(weighted) * live
    return (projected, design_sens)


def solution(mesh):
    placed = (
        P("wide", "narrow", None),
        P("wide", "narrow", None),
        P("wide", "narrow", None),
        P("narrow", "wide", None),
        P("narrow", "wide", None),
        P("narrow", "wide", None),
    )
    return jax.shard_map(
        per_device,
        mesh=mesh,
        in_specs=placed,
        out_specs=(P("narrow", "wide", None), P("narrow", "wide", None)),
        check_vma=False,
    )
```

profile of v0, /device:TPU:1, one launch (start us, length us, event | category | flops | bytes accessed | tf_op | source)
XLA Modules:
  0.0 223.6 jit_solution(12722983638943194320)
XLA Ops:
  0.6 1.3 select_maximum_fusion
  1.9 16.1 %collective-permute-start.2 = (f32[2,1,32,514]{3,2,1,0:T(8,128)S(1)}, f32[2,1,32,514]{3,2,1,0:T(8,128)S(1)}, u32[]{:S(2)}, u32[]{:S(2)}) collective-permute-start(f32[2,1,32,514]{3,2,1,0:T(8,128)S(1)} %get-tuple-element.18), channel_id=1, source_target_pairs={{16,0},{32,16},{48,32},{64,48},{80,64},{96,80},{112,96},{128,112},... | collective-permute-start | bytes 394760 | tf_op jit(solution)/shard_map/ppermute | solution.py:26
  18.0 1.9 collective-permute-start.3
  20.0 0.3 convolution_bitcast_fusion.2
  20.3 4.3 %collective-permute-start = (f32[12,2,256]{2,0,1:T(8,128)S(1)}, f32[12,2,256]{2,0,1:T(8,128)S(1)}, u32[]{:S(2)}, u32[]{:S(2)}) collective-permute-start(f32[12,2,256]{2,0,1:T(8,128)S(1)} %get-tuple-element.23), channel_id=1, source_target_pairs={{0,1},{1,2},{2,3},{3,4},{4,5},{5,6},{6,7},{7,8},{8,9},{9,10},{10,1... | collective-permute-start | bytes 73736 | tf_op jit(solution)/shard_map/ppermute | solution.py:25
  24.6 1.3 collective-permute-start.1
  25.9 0.2 fusion.66
  26.3 1.3 collective-permute-start.4
  27.6 16.2 %collective-permute-start.5 = (f32[2,6,1,514]{3,2,1,0:T(1,128)S(1)}, f32[2,6,1,514]{3,2,1,0:T(1,128)S(1)}, u32[]{:S(2)}, u32[]{:S(2)}) collective-permute-start(f32[2,6,1,514]{3,2,1,0:T(1,128)S(1)} %get-tuple-element.15), channel_id=1, source_target_pairs={{0,1},{1,2},{2,3},{3,4},{4,5},{5,6},{6,7},{7,8},{8,9},{9,10},{10,1... | collective-permute-start | bytes 74024 | tf_op jit(solution)/shard_map/ppermute | solution.py:25
  43.9 0.2 fusion.16
  44.2 1.0 reshape.57
  45.1 22.0 %all-to-all-start = ((f32[64,1,128]{2,1,0:T(1,128)}), f32[64,1,128]{2,1,0:T(1,128)S(1)}, u32[]{:S(2)}, u32[]{:S(2)}) async-start(f32[64,1,128]{2,1,0:T(1,128)} %reshape.57), calls=%async_computation | async-start | bytes 65536 | tf_op jit(solution)/shard_map/all_to_all | solution.py:77
  67.2 0.8 fusion.2
  68.0 1.1 fusion.5
  69.2 18.1 %reshape.53 = f32[2,2,16,2,256,2]{5,4,3,2,1,0:T(8,128)} reshape(f32[4,32,512]{2,1,0:T(8,128)S(1)} %fusion.5) | data formatting | bytes 524288 | tf_op jit(solution)/shard_map/reshape | solution.py:47
  87.3 7.0 %reduce_sum.39 = f32[2,16,256]{2,1,0:T(8,128)S(1)} reduce(f32[2,2,16,2,256,2]{5,4,3,2,1,0:T(8,128)} %reshape.53, f32[]{:T(128)} %constant.23.clone.1), dimensions={1,3,5}, to_apply=%region_3.4 | reduce | flops 57344 | bytes 294916 | tf_op jit(solution)/shard_map/reduce_sum | solution.py:47
  94.4 1.0 reshape.61
  95.4 17.7 %all-to-all-start.2 = ((f32[16,1,512]{2,1,0:T(1,128)}), f32[16,1,512]{2,1,0:T(1,128)S(1)}, u32[]{:S(2)}, u32[]{:S(2)}) async-start(f32[16,1,512]{2,1,0:T(1,128)} %reshape.61), calls=%async_computation.2 | async-start | bytes 65536 | tf_op jit(solution)/shard_map/all_to_all | solution.py:101
  113.1 0.6 broadcast.200
  113.7 0.8 reduce.1
  114.4 0.4 reshape.58
  114.8 0.2 copy.102
  115.0 0.6 convolution_bitcast_fusion.1
  115.8 0.8 reshape.59
  116.6 20.9 %all-to-all-done.2 = f32[16,1,512]{2,1,0:T(1,128)S(1)} async-done(((f32[16,1,512]{2,1,0:T(1,128)}), f32[16,1,512]{2,1,0:T(1,128)S(1)}, u32[]{:S(2)}, u32[]{:S(2)}) %all-to-all-start.2) | async-done | bytes 32800 | tf_op jit(solution)/shard_map/all_to_all | solution.py:101
  137.5 13.7 %all-to-all-start.1 = ((f32[64,1,128]{2,1,0:T(1,128)}), f32[64,1,128]{2,1,0:T(1,128)S(1)}, u32[]{:S(2)}, u32[]{:S(2)}) async-start(f32[64,1,128]{2,1,0:T(1,128)} %reshape.59), calls=%async_computation.1 | async-start | bytes 65536 | tf_op jit(solution)/shard_map/all_to_all | solution.py:79
  151.2 0.2 select_reduce_fusion.1
  151.5 0.8 reduce
  152.2 0.4 reshape.62
  152.9 10.4 %all-to-all-done.1 = f32[64,1,128]{2,1,0:T(1,128)S(1)} async-done(((f32[64,1,128]{2,1,0:T(1,128)}), f32[64,1,128]{2,1,0:T(1,128)S(1)}, u32[]{:S(2)}, u32[]{:S(2)}) %all-to-all-start.1) | async-done | bytes 32800 | tf_op jit(solution)/shard_map/all_to_all | solution.py:79
  163.4 0.8 reduce.2
  164.1 0.2 reshape.60
  164.7 0.3 fusion.7
  165.0 2.0 collective-permute-start.6
  167.0 1.3 collective-permute-start.7
  168.3 17.3 %collective-permute-done.7 = f32[12,2,256]{2,0,1:T(8,128)S(1)} collective-permute-done((f32[12,2,256]{2,0,1:T(8,128)S(1)}, f32[12,2,256]{2,0,1:T(8,128)S(1)}, u32[]{:S(2)}, u32[]{:S(2)}) %collective-permute-start.7) | collective-permute-done | bytes 24608 | tf_op jit(solution)/shard_map/ppermute | solution.py:26
  185.9 0.3 reshape.63
  186.2 16.1 %all_to_all.90 = f32[64,1,128]{2,1,0:T(1,128)S(1)} all-to-all(f32[64,1,128]{2,1,0:T(1,128)S(1)} %reshape.63), channel_id=1, replica_groups=mesh['wide'=64,'narrow'=16] {'wide'}, dimensions={0} | all-to-all | bytes 65536 | tf_op jit(solution)/shard_map/all_to_all | solution.py:77
  202.3 0.8 reduce.3
  203.1 0.4 reshape.64
  203.5 0.2 copy.115
  203.7 0.6 convolution_bitcast_fusion
  204.4 0.2 reshape.65
  204.6 16.2 %all_to_all.91 = f32[64,1,128]{2,1,0:T(1,128)S(1)} all-to-all(f32[64,1,128]{2,1,0:T(1,128)S(1)} %reshape.65), channel_id=1, replica_groups=mesh['wide'=64,'narrow'=16] {'wide'}, dimensions={0} | all-to-all | bytes 65536 | tf_op jit(solution)/shard_map/all_to_all | solution.py:79
  220.9 0.8 reduce.4
  221.7 0.2 reshape.66
  222.3 0.6 copy.121
  222.9 0.6 copy.122
  (41 shorter events, 2.3 us)
Async XLA Ops:
  0.6 19.3 %copy-start = (f32[16,2,256]{2,1,0:T(2,128)S(1)}, f32[16,2,256]{2,1,0:T(2,128)}, u32[]{:S(2)}) copy-start(f32[16,2,256]{2,1,0:T(2,128)} %param.9) | copy-start | bytes 98308
  1.9 24.3 %collective-permute-start.2 = (f32[2,1,32,514]{3,2,1,0:T(8,128)S(1)}, f32[2,1,32,514]{3,2,1,0:T(8,128)S(1)}, u32[]{:S(2)}, u32[]{:S(2)}) collective-permute-start(f32[2,1,32,514]{3,2,1,0:T(8,128)S(1)} %get-tuple-element.18), channel_id=1, source_target_pairs={{16,0},{32,16},{48,32},{64,48},{80,64},{96,80},{112,96},{128,112},... | collective-permute-start | bytes 394760 | tf_op jit(solution)/shard_map/ppermute | solution.py:26
  18.0 8.2 %collective-permute-start.3 = (f32[2,1,32,514]{3,2,1,0:T(8,128)S(1)}, f32[2,1,32,514]{3,2,1,0:T(8,128)S(1)}, u32[]{:S(2)}, u32[]{:S(2)}) collective-permute-start(f32[2,1,32,514]{3,2,1,0:T(8,128)S(1)} %get-tuple-element.17), channel_id=1, source_target_pairs={{0,16},{16,32},{32,48},{48,64},{64,80},{80,96},{96,112},{112,128},... | collective-permute-start | bytes 394760 | tf_op jit(solution)/shard_map/ppermute | solution.py:25
  20.3 23.6 %collective-permute-start = (f32[12,2,256]{2,0,1:T(8,128)S(1)}, f32[12,2,256]{2,0,1:T(8,128)S(1)}, u32[]{:S(2)}, u32[]{:S(2)}) collective-permute-start(f32[12,2,256]{2,0,1:T(8,128)S(1)} %get-tuple-element.23), channel_id=1, source_target_pairs={{0,1},{1,2},{2,3},{3,4},{4,5},{5,6},{6,7},{7,8},{8,9},{9,10},{10,1... | collective-permute-start | bytes 73736 | tf_op jit(solution)/shard_map/ppermute | solution.py:25
  24.6 19.2 %collective-permute-start.1 = (f32[12,2,256]{2,0,1:T(8,128)S(1)}, f32[12,2,256]{2,0,1:T(8,128)S(1)}, u32[]{:S(2)}, u32[]{:S(2)}) collective-permute-start(f32[12,2,256]{2,0,1:T(8,128)S(1)} %get-tuple-element.24), channel_id=1, source_target_pairs={{1,0},{2,1},{3,2},{4,3},{5,4},{6,5},{7,6},{8,7},{9,8},{10,9},{11,1... | collective-permute-start | bytes 73736 | tf_op jit(solution)/shard_map/ppermute | solution.py:26
  26.3 40.9 %collective-permute-start.4 = (f32[2,6,1,514]{3,2,1,0:T(1,128)S(1)}, f32[2,6,1,514]{3,2,1,0:T(1,128)S(1)}, u32[]{:S(2)}, u32[]{:S(2)}) collective-permute-start(f32[2,6,1,514]{3,2,1,0:T(1,128)S(1)} %get-tuple-element.14), channel_id=1, source_target_pairs={{1,0},{2,1},{3,2},{4,3},{5,4},{6,5},{7,6},{8,7},{9,8},{10,9},{11,1... | collective-permute-start | bytes 74024 | tf_op jit(solution)/shard_map/ppermute | solution.py:26
  27.6 39.6 %collective-permute-start.5 = (f32[2,6,1,514]{3,2,1,0:T(1,128)S(1)}, f32[2,6,1,514]{3,2,1,0:T(1,128)S(1)}, u32[]{:S(2)}, u32[]{:S(2)}) collective-permute-start(f32[2,6,1,514]{3,2,1,0:T(1,128)S(1)} %get-tuple-element.15), channel_id=1, source_target_pairs={{0,1},{1,2},{2,3},{3,4},{4,5},{5,6},{6,7},{7,8},{8,9},{9,10},{10,1... | collective-permute-start | bytes 74024 | tf_op jit(solution)/shard_map/ppermute | solution.py:25
  45.1 50.2 %all-to-all-start = ((f32[64,1,128]{2,1,0:T(1,128)}), f32[64,1,128]{2,1,0:T(1,128)S(1)}, u32[]{:S(2)}, u32[]{:S(2)}) async-start(f32[64,1,128]{2,1,0:T(1,128)} %reshape.57), calls=%async_computation | async-start | bytes 65536 | tf_op jit(solution)/shard_map/all_to_all | solution.py:77
  69.1 95.5 %copy-start.1 = (s32[16,2,256]{2,1,0:T(2,128)S(1)}, s32[16,2,256]{2,1,0:T(2,128)}, u32[]{:S(2)}) copy-start(s32[16,2,256]{2,1,0:T(2,128)} %param.10) | copy-start | bytes 98308
  69.1 95.5 %copy-start.2 = (s32[16,2,256]{2,1,0:T(2,128)S(1)}, s32[16,2,256]{2,1,0:T(2,128)}, u32[]{:S(2)}) copy-start(s32[16,2,256]{2,1,0:T(2,128)} %param.11) | copy-start | bytes 98308
  95.4 42.1 %all-to-all-start.2 = ((f32[16,1,512]{2,1,0:T(1,128)}), f32[16,1,512]{2,1,0:T(1,128)S(1)}, u32[]{:S(2)}, u32[]{:S(2)}) async-start(f32[16,1,512]{2,1,0:T(1,128)} %reshape.61), calls=%async_computation.2 | async-start | bytes 65536 | tf_op jit(solution)/shard_map/all_to_all | solution.py:101
  137.5 25.9 %all-to-all-start.1 = ((f32[64,1,128]{2,1,0:T(1,128)}), f32[64,1,128]{2,1,0:T(1,128)S(1)}, u32[]{:S(2)}, u32[]{:S(2)}) async-start(f32[64,1,128]{2,1,0:T(1,128)} %reshape.59), calls=%async_computation.1 | async-start | bytes 65536 | tf_op jit(solution)/shard_map/all_to_all | solution.py:79
  165.0 3.3 %collective-permute-start.6 = (f32[12,2,256]{2,0,1:T(8,128)S(1)}, f32[12,2,256]{2,0,1:T(8,128)S(1)}, u32[]{:S(2)}, u32[]{:S(2)}) collective-permute-start(f32[12,2,256]{2,0,1:T(8,128)S(1)} %get-tuple-element.21), channel_id=1, source_target_pairs={{0,1},{1,2},{2,3},{3,4},{4,5},{5,6},{6,7},{7,8},{8,9},{9,10},{10,1... | collective-permute-start | bytes 73736 | tf_op jit(solution)/shard_map/ppermute | solution.py:25
  167.0 18.6 %collective-permute-start.7 = (f32[12,2,256]{2,0,1:T(8,128)S(1)}, f32[12,2,256]{2,0,1:T(8,128)S(1)}, u32[]{:S(2)}, u32[]{:S(2)}) collective-permute-start(f32[12,2,256]{2,0,1:T(8,128)S(1)} %get-tuple-element.22), channel_id=1, source_target_pairs={{1,0},{2,1},{3,2},{4,3},{5,4},{6,5},{7,6},{8,7},{9,8},{10,9},{11,1... | collective-permute-start | bytes 73736 | tf_op jit(solution)/shard_map/ppermute | solution.py:26
where the time goes:
time: 224 us
  starting transfers between devices  97.8 us (44%)
  waiting for transfers between devices  48.6 us (22%)
  blocking collectives  32.3 us (14%)
  local copies, waits for them, and re-layouts  27 us (12%)
  other arithmetic  14.7 us (7%)
    ppermute x4, starting transfers between devices, padded_2(): before = lax.ppermute(last, axis, up)  24.4 us
    all_to_all x1, starting transfers between devices, smooth(): lax.all_to_all(along_z, 'wide', split_axis=2, concat_axis=1, tiled=True)  22 us
    all_to_all x1, waiting for transfers between devices, per_device(): lax.all_to_all(coarse, 'narrow', split_axis=0, concat_axis=2, tiled=True)  20.9 us
    ppermute x4, starting transfers between devices, padded_2(): after = lax.ppermute(initial, axis, down)  19.9 us
    reshape x1, local copies, waits for them, and re-layouts, restrict(): sensed.reshape(x_cells // 2, 2, y_cells // 2, 2, z_cells // 2, 2)  18.1 us
    all_to_all x1, starting transfers between devices, per_device(): lax.all_to_all(coarse, 'narrow', split_axis=0, concat_axis=2, tiled=True)  17.7 us
    ppermute x4, waiting for transfers between devices, padded_2(): after = lax.ppermute(initial, axis, down)  17.3 us
    all_to_all x1, blocking collectives, smooth(): lax.all_to_all(transposed, 'wide', split_axis=1, concat_axis=2, tiled=True)  16.2 us
  transfers between devices with their start and end apart: 11, of which 3 were waited for; matrix products, arithmetic and copies ran while one was open for 16% of the time, Pallas kernels for 0%

commit v1 on v0

v1 whole, which is shorter than its diff:
```python
import math

import jax
import jax.numpy as jnp
from jax import lax
from jax.sharding import PartitionSpec as P

RADIUS = 12
BETA = 32.0
ETA = 0.5
LOWER_TANH = math.tanh(BETA * ETA)
SPAN_TANH = math.tanh(BETA * ETA) + math.tanh(BETA * (1.0 - ETA))
HIGHEST = lax.Precision.HIGHEST


def neighbours(shard, axis, dim):
    count, length = lax.axis_size(axis), shard.shape[dim]
    up = [(i, i + 1) for i in range(count - 1)]
    down = [(j, i) for i, j in up]
    before = lax.ppermute(lax.slice_in_dim(shard, length - 1, length, axis=dim), axis, up)
    after = lax.ppermute(lax.slice_in_dim(shard, 0, 1, axis=dim), axis, down)
    return before, after


def restrict(fields, coeffs, x_sides, y_sides):
    padded = jnp.concatenate([x_sides[0], fields, x_sides[1]], axis=1)
    grad_x = padded[:, 2:] - padded[:, :-2]
    padded = jnp.concatenate([y_sides[0], fields, y_sides[1]], axis=2)
    grad_y = padded[:, :, 2:] - padded[:, :, :-2]
    padded = jnp.pad(fields, ((0, 0), (0, 0), (0, 0), (1, 1)))
    grad_z = padded[..., 2:] - padded[..., :-2]
    product = grad_x[0] * grad_x[1] + grad_y[0] * grad_y[1] + grad_z[0] * grad_z[1]
    sensed = -0.25 * coeffs * product
    x_cells, y_cells, z_cells = sensed.shape
    sensed = sensed.reshape(x_cells // 2, 2, y_cells, z_cells).sum(axis=1)
    rows = lax.broadcasted_iota(jnp.int32, (z_cells, z_cells // 2), 0)
    cols = lax.broadcasted_iota(jnp.int32, (z_cells, z_cells // 2), 1)
    pairs = (rows // 2 == cols).astype(jnp.float32)
    sensed = jnp.einsum("xyz,zk->xyk", sensed, pairs, precision=HIGHEST)
    return sensed.reshape(x_cells // 2, y_cells // 2, 2, z_cells // 2).sum(axis=2)


def band(extent):
    out_pos = lax.broadcasted_iota(jnp.int32, (extent, extent), 0)
    in_pos = lax.broadcasted_iota(jnp.int32, (extent, extent), 1)
    return jnp.maximum(RADIUS + 1 - jnp.abs(in_pos - out_pos), 0).astype(jnp.float32)


def cover(positions, extent):
    low = jnp.maximum(RADIUS - positions, 0)
    high = jnp.maximum(RADIUS - (extent - 1 - positions), 0)
    total = (RADIUS + 1) ** 2
    return (total - low * (low + 1) // 2 - high * (high + 1) // 2).astype(jnp.float32)


def per_device(kirchhoff, adjoint, penalty_slope, design, solid_mask, void_mask):
    wide, narrow = lax.axis_size("wide"), lax.axis_size("narrow")
    zc, xc, y_all = design.shape
    z_all, x_all = zc * narrow, xc * wide
    yc, zw = y_all // narrow, z_all // wide

    is_solid = solid_mask.astype(jnp.float32)
    is_void = void_mask.astype(jnp.float32)
    live = (1.0 - is_solid) * (1.0 - is_void)

    along_y = jnp.einsum("zxj,ij->zxi", design, band(y_all), precision=HIGHEST)
    sent = jnp.stack([along_y, live], axis=1).reshape(zc, 2, xc, narrow, yc)
    sent = sent.transpose(3, 0, 1, 2, 4).reshape(narrow, 1, -1)
    got = lax.all_to_all(sent, "narrow", split_axis=0, concat_axis=0, tiled=True)
    got = got.reshape(z_all, 2, xc, yc)
    along_z = jnp.einsum("kz,zxy->kxy", band(z_all), got[:, 0], precision=HIGHEST)

    fields = jnp.stack([kirchhoff, adjoint])
    y_sides = neighbours(fields, "narrow", 2)
    x_sides = neighbours(fields, "wide", 1)
    coarse = restrict(fields, penalty_slope.astype(jnp.float32), x_sides, y_sides)
    coarse = coarse.transpose(2, 0, 1)

    sent = jnp.stack([along_z, got[:, 1], coarse], axis=1).reshape(wide, zw, 3, xc, yc)
    sent = sent.transpose(0, 3, 2, 1, 4).reshape(wide, 1, -1)
    got = lax.all_to_all(sent, "wide", split_axis=0, concat_axis=0, tiled=True)
    got = got.reshape(x_all, 3, zw * yc)

    along_x = jnp.dot(band(x_all), got[:, 0], precision=HIGHEST)
    z_pos = lax.axis_index("wide") * zw + lax.iota(jnp.int32, zw)
    y_pos = lax.axis_index("narrow") * yc + lax.iota(jnp.int32, yc)
    cover_zy = (cover(z_pos, z_all)[:, None] * cover(y_pos, y_all)[None, :]).reshape(-1)
    normalizer = cover(lax.iota(jnp.int32, x_all), x_all)[:, None] * cover_zy[None, :]
    filtered = along_x / normalizer
    inner = jnp.tanh(BETA * (filtered - ETA))
    slope = BETA * (1.0 - inner * inner) / SPAN_TANH
    density = (LOWER_TANH + inner) / SPAN_TANH
    weighted = slope * got[:, 2] * got[:, 1] / normalizer
    weighted = jnp.dot(band(x_all), weighted, precision=HIGHEST)

    sent = jnp.stack([density, weighted], axis=1).reshape(wide, 1, -1)
    got = lax.all_to_all(sent, "wide", split_axis=0, concat_axis=0, tiled=True)
    got = got.reshape(wide, xc, 2, zw, yc).transpose(0, 3, 2, 1, 4).reshape(z_all, 2, xc, yc)
    along_z = jnp.einsum("kz,zxy->kxy", band(z_all), got[:, 1], precision=HIGHEST)
    sent = jnp.stack([got[:, 0], along_z], axis=1).reshape(narrow, 1, -1)
    got = lax.all_to_all(sent, "narrow", split_axis=0, concat_axis=0, tiled=True)
    got = got.reshape(narrow, zc, 2, xc, yc).transpose(2, 1, 3, 0, 4).reshape(2, zc, xc, y_all)
    projected = got[0] * live + is_solid * (1.0 - is_void)
    design_sens = jnp.einsum("zxj,ij->zxi", got[1], band(y_all), precision=HIGHEST) * live
    return (projected, design_sens)


def solution(mesh):
    fields = P("wide", "narrow", None)
    cells = P("narrow", "wide", None)
    return jax.shard_map(
        per_device,
        mesh=mesh,
        in_specs=(fields, fields, fields, cells, cells, cells),
        out_specs=(cells, cells),
        check_vma=False,
    )
```

time: 224 us -> 168 us (0.75)
  starting transfers between devices: 97.8 us -> 65.9 us
  local copies, waits for them, and re-layouts: 27 us -> 10.5 us
  blocking collectives: 32.3 us -> 46.9 us
  waiting for transfers between devices: 48.6 us -> 35.5 us
  other arithmetic: 14.7 us -> 2.8 us
    all_to_all x3 -> x2, starting transfers between devices: 53.5 us -> 33.9 us  [the longest x1 19 us: per_device(): lax.all_to_all(sent, 'narrow', split_axis=0, concat_axis=0, tiled=True)]
    ppermute x8 -> x4, waiting for transfers between devices: 17.3 us -> 0.01 us  [the longest x2 0.01 us: neighbours(): after = lax.ppermute(lax.slice_in_dim(shard, 0, 1, axis=dim), axis, down)]
    all_to_all x2, blocking collectives: 32.3 us -> 46.9 us  [the longest x1 28.6 us: per_device(): lax.all_to_all(sent, 'narrow', split_axis=0, concat_axis=0, tiled=True)]
    reshape x1 -> x7, local copies, waits for them, and re-layouts: 18.1 us -> 4.52 us  [the longest x1 1.35 us: per_device(): sent = sent.transpose(3, 0, 1, 2, 4).reshape(narrow, 1, -1)]
    ppermute x8 -> x4, starting transfers between devices: 44.4 us -> 32 us  [the longest x2 17.4 us: neighbours(): after = lax.ppermute(lax.slice_in_dim(shard, 0, 1, axis=dim), axis, down)]
    reduce_sum x4 -> x1, other arithmetic: 7.44 us -> 0.19 us  [restrict(): sensed = sensed.reshape(x_cells // 2, 2, y_cells, z_cells).sum(axis=1)]
    all_to_all x3 -> x2, waiting for transfers between devices: 31.3 us -> 35.5 us  [the longest x1 22.2 us: per_device(): lax.all_to_all(sent, 'narrow', split_axis=0, concat_axis=0, tiled=True)]
    unnamed x18 -> x19, local copies, waits for them, and re-layouts: 6.13 us -> 2.85 us
  transfers between devices with their start and end apart: 11 -> 6, of which waited for: 3 -> 2; matrix products, arithmetic and copies ran while one was open for 16% -> 3% of each run, Pallas kernels for 0% -> 0%
where the time goes in v1:
time: 168 us; the launch traced here: 166 us
  starting transfers between devices  65.9 us (39%)
  blocking collectives  46.9 us (28%)
  waiting for transfers between devices  35.5 us (21%)
  local copies, waits for them, and re-layouts  10.5 us (6%)
  other arithmetic  2.8 us (2%)
  matrix products  2.78 us (2%)
    all_to_all x1, blocking collectives, per_device(): lax.all_to_all(sent, 'narrow', split_axis=0, concat_axis=0, tiled=True)  28.6 us
    all_to_all x1, waiting for transfers between devices, per_device(): lax.all_to_all(sent, 'narrow', split_axis=0, concat_axis=0, tiled=True)  22.2 us
    all_to_all x1, starting transfers between devices, per_device(): lax.all_to_all(sent, 'narrow', split_axis=0, concat_axis=0, tiled=True)  19 us
    all_to_all x1, blocking collectives, per_device(): got = lax.all_to_all(sent, 'wide', split_axis=0, concat_axis=0, tiled=True)  18.3 us
    ppermute x2, starting transfers between devices, neighbours(): after = lax.ppermute(lax.slice_in_dim(shard, 0, 1, axis=dim), axis, down)  17.4 us
    all_to_all x1, starting transfers between devices, per_device(): got = lax.all_to_all(sent, 'wide', split_axis=0, concat_axis=0, tiled=True)  14.9 us
    ppermute x2, starting transfers between devices, neighbours(): lax.ppermute(lax.slice_in_dim(shard, length - 1, length, axis=dim), axis,...  14.6 us
    all_to_all x1, waiting for transfers between devices, per_device(): got = lax.all_to_all(sent, 'wide', split_axis=0, concat_axis=0, tiled=True)  13.3 us
  transfers between devices with their start and end apart: 6, of which 2 were waited for; matrix products, arithmetic and copies ran while one was open for 3% of the time, Pallas kernels for 0%

profile of v1, /device:TPU:1, one launch (start us, length us, event | category | flops | bytes accessed | tf_op | source)
XLA Modules:
  0.0 165.5 jit_solution(14658938074513492989)
XLA Ops:
  0.7 1.0 fusion.28
  1.7 16.1 %collective-permute-start = (f32[2,1,32,512]{3,2,1,0:T(8,128)S(1)}, f32[2,1,32,512]{3,2,1,0:T(8,128)S(1)}, u32[]{:S(2)}, u32[]{:S(2)}) collective-permute-start(f32[2,1,32,512]{3,2,1,0:T(8,128)S(1)} %get-tuple-element.17), channel_id=1, source_target_pairs={{16,0},{32,16},{48,32},{64,48},{80,64},{96,80},{112,96},{128,112},... | collective-permute-start | bytes 393224 | tf_op jit(solution)/shard_map/ppermute | solution.py:21
  17.7 1.9 %collective-permute-start.1 = (f32[2,1,32,512]{3,2,1,0:T(8,128)S(1)}, f32[2,1,32,512]{3,2,1,0:T(8,128)S(1)}, u32[]{:S(2)}, u32[]{:S(2)}) collective-permute-start(f32[2,1,32,512]{3,2,1,0:T(8,128)S(1)} %get-tuple-element.18), channel_id=1, source_target_pairs={{0,16},{16,32},{32,48},{48,64},{64,80},{80,96},{96,112},{112,128},... | collective-permute-start | bytes 393224 | tf_op jit(solution)/shard_map/ppermute | solution.py:20
  19.7 1.3 collective-permute-start.2
  21.0 12.7 %collective-permute-start.3 = (f32[2,4,1,512]{3,2,1,0:T(1,128)S(1)}, f32[2,4,1,512]{3,2,1,0:T(1,128)S(1)}, u32[]{:S(2)}, u32[]{:S(2)}) collective-permute-start(f32[2,4,1,512]{3,2,1,0:T(1,128)S(1)} %get-tuple-element.20), channel_id=1, source_target_pairs={{0,1},{1,2},{2,3},{3,4},{4,5},{5,6},{6,7},{7,8},{8,9},{9,10},{10,1... | collective-permute-start | bytes 49160 | tf_op jit(solution)/shard_map/ppermute | solution.py:20
  33.8 0.4 convolution_bitcast_fusion.2
  34.3 0.2 copy.41
  34.5 0.5 copy-done.4
  35.2 0.2 copy.42
  35.4 0.3 maximum_bitcast_fusion
  35.7 1.4 reshape.248
  37.0 19.0 %all-to-all-start = ((f32[16,1,1024]{2,1,0:T(1,128)}), f32[16,1,1024]{2,1,0:T(1,128)S(1)}, u32[]{:S(2)}, u32[]{:S(2)}) async-start(f32[16,1,1024]{2,1,0:T(1,128)} %reshape.248), calls=%async_computation | async-start | bytes 131072 | tf_op jit(solution)/shard_map/all_to_all | solution.py:69
  56.2 0.2 fusion.5
  56.4 0.3 fusion.3
  56.7 0.6 copy-done.3
  57.3 0.2 bitcast_reduce_fusion
  57.6 0.5 convolution_reduce_fusion
  58.2 0.1 copy.50
  58.3 22.2 %all-to-all-done = f32[16,1,1024]{2,1,0:T(1,128)S(1)} async-done(((f32[16,1,1024]{2,1,0:T(1,128)}), f32[16,1,1024]{2,1,0:T(1,128)S(1)}, u32[]{:S(2)}, u32[]{:S(2)}) %all-to-all-start) | async-done | bytes 65568 | tf_op jit(solution)/shard_map/all_to_all | solution.py:69
  80.5 0.2 reduce
  80.6 0.7 reshape.233
  81.4 0.2 fusion.80
  81.8 0.6 convolution_bitcast_fusion
  82.5 0.8 copy.52
  83.2 14.9 %all-to-all-start.1 = ((f32[64,1,384]{2,1,0:T(1,128)}), f32[64,1,384]{2,1,0:T(1,128)S(1)}, u32[]{:S(2)}, u32[]{:S(2)}) async-start(f32[64,1,384]{2,1,0:T(1,128)} %copy.52), calls=%async_computation.1 | async-start | bytes 196608 | tf_op jit(solution)/shard_map/all_to_all | solution.py:81
  98.3 13.3 %all-to-all-done.1 = f32[64,1,384]{2,1,0:T(1,128)S(1)} async-done(((f32[64,1,384]{2,1,0:T(1,128)}), f32[64,1,384]{2,1,0:T(1,128)S(1)}, u32[]{:S(2)}, u32[]{:S(2)}) %all-to-all-start.1) | async-done | bytes 98336 | tf_op jit(solution)/shard_map/all_to_all | solution.py:81
  111.6 0.2 reduce.1
  111.9 0.1 reshape.236
  112.0 0.1 fusion.81
  112.3 0.3 fusion.2
  112.6 0.3 convolution_bitcast_fusion.1
  113.1 0.1 reshape.249
  113.2 18.3 %all_to_all.20 = f32[64,1,256]{2,1,0:T(1,128)S(1)} all-to-all(f32[64,1,256]{2,1,0:T(1,128)S(1)} %reshape.249), channel_id=1, replica_groups=mesh['wide'=64,'narrow'=16] {'wide'}, dimensions={0} | all-to-all | bytes 131072 | tf_op jit(solution)/shard_map/all_to_all | solution.py:97
  131.6 0.2 copy.58
  132.0 0.4 fusion.18
  132.5 0.3 copy.61
  132.8 0.7 reshape.250
  133.6 28.6 %all_to_all.21 = f32[16,1,1024]{2,1,0:T(1,128)S(1)} all-to-all(f32[16,1,1024]{2,1,0:T(1,128)S(1)} %reshape.250), channel_id=1, replica_groups=mesh['wide'=64,'narrow'=16] {'narrow'}, dimensions={0} | all-to-all | bytes 131072 | tf_op jit(solution)/shard_map/all_to_all | solution.py:101
  162.2 0.2 reduce.2
  162.3 0.7 reshape.241
  163.0 0.2 fusion.78
  163.2 0.2 copy.63
  163.4 0.1 squeeze.32
  163.6 0.6 copy.65
  164.2 0.2 copy.64
  164.4 0.1 squeeze.33
  164.5 0.3 convolution_multiply_fusion
  164.9 0.6 copy.66
  (43 shorter events, 1.7 us)
Async XLA Ops:
  0.6 33.1 %copy-start = (f32[16,2,256]{2,1,0:T(2,128)S(1)}, f32[16,2,256]{2,1,0:T(2,128)}, u32[]{:S(2)}) copy-start(f32[16,2,256]{2,1,0:T(2,128)} %param.9) | copy-start | bytes 98308
  0.6 19.0 %copy-start.1 = (f32[4,32,512]{2,1,0:T(8,128)S(1)}, f32[4,32,512]{2,1,0:T(8,128)}, u32[]{:S(2)}) copy-start(f32[4,32,512]{2,1,0:T(8,128)} %param.6) | copy-start | bytes 786436
  0.7 19.0 %copy-start.2 = (f32[4,32,512]{2,1,0:T(8,128)S(1)}, f32[4,32,512]{2,1,0:T(8,128)}, u32[]{:S(2)}) copy-start(f32[4,32,512]{2,1,0:T(8,128)} %param.7) | copy-start | bytes 786436
  1.7 54.5 %collective-permute-start = (f32[2,1,32,512]{3,2,1,0:T(8,128)S(1)}, f32[2,1,32,512]{3,2,1,0:T(8,128)S(1)}, u32[]{:S(2)}, u32[]{:S(2)}) collective-permute-start(f32[2,1,32,512]{3,2,1,0:T(8,128)S(1)} %get-tuple-element.17), channel_id=1, source_target_pairs={{16,0},{32,16},{48,32},{64,48},{80,64},{96,80},{112,96},{128,112},... | collective-permute-start | bytes 393224 | tf_op jit(solution)/shard_map/ppermute | solution.py:21
  17.7 38.4 %collective-permute-start.1 = (f32[2,1,32,512]{3,2,1,0:T(8,128)S(1)}, f32[2,1,32,512]{3,2,1,0:T(8,128)S(1)}, u32[]{:S(2)}, u32[]{:S(2)}) collective-permute-start(f32[2,1,32,512]{3,2,1,0:T(8,128)S(1)} %get-tuple-element.18), channel_id=1, source_target_pairs={{0,16},{16,32},{32,48},{48,64},{64,80},{80,96},{96,112},{112,128},... | collective-permute-start | bytes 393224 | tf_op jit(solution)/shard_map/ppermute | solution.py:20
  19.7 36.4 %collective-permute-start.2 = (f32[2,4,1,512]{3,2,1,0:T(1,128)S(1)}, f32[2,4,1,512]{3,2,1,0:T(1,128)S(1)}, u32[]{:S(2)}, u32[]{:S(2)}) collective-permute-start(f32[2,4,1,512]{3,2,1,0:T(1,128)S(1)} %get-tuple-element.19), channel_id=1, source_target_pairs={{1,0},{2,1},{3,2},{4,3},{5,4},{6,5},{7,6},{8,7},{9,8},{10,9},{11,1... | collective-permute-start | bytes 49160 | tf_op jit(solution)/shard_map/ppermute | solution.py:21
  21.0 35.1 %collective-permute-start.3 = (f32[2,4,1,512]{3,2,1,0:T(1,128)S(1)}, f32[2,4,1,512]{3,2,1,0:T(1,128)S(1)}, u32[]{:S(2)}, u32[]{:S(2)}) collective-permute-start(f32[2,4,1,512]{3,2,1,0:T(1,128)S(1)} %get-tuple-element.20), channel_id=1, source_target_pairs={{0,1},{1,2},{2,3},{3,4},{4,5},{5,6},{6,7},{7,8},{8,9},{9,10},{10,1... | collective-permute-start | bytes 49160 | tf_op jit(solution)/shard_map/ppermute | solution.py:20
  34.3 0.8 copy-start.4
  34.3 0.8 copy-start.5
  37.0 43.5 %all-to-all-start = ((f32[16,1,1024]{2,1,0:T(1,128)}), f32[16,1,1024]{2,1,0:T(1,128)S(1)}, u32[]{:S(2)}, u32[]{:S(2)}) async-start(f32[16,1,1024]{2,1,0:T(1,128)} %reshape.248), calls=%async_computation | async-start | bytes 131072 | tf_op jit(solution)/shard_map/all_to_all | solution.py:69
  56.4 0.9 copy-start.3
  83.2 28.4 %all-to-all-start.1 = ((f32[64,1,384]{2,1,0:T(1,128)}), f32[64,1,384]{2,1,0:T(1,128)S(1)}, u32[]{:S(2)}, u32[]{:S(2)}) async-start(f32[64,1,384]{2,1,0:T(1,128)} %copy.52), calls=%async_computation.1 | async-start | bytes 196608 | tf_op jit(solution)/shard_map/all_to_all | solution.py:81

commit v2 on v1

v2 whole, which is shorter than its diff:
```python
import math

import jax
import jax.numpy as jnp
from jax import lax
from jax.experimental import pallas as pl
from jax.experimental.pallas import tpu as pltpu
from jax.sharding import PartitionSpec as P

RADIUS = 12
BETA = 32.0
ETA = 0.5
LOWER_TANH = math.tanh(BETA * ETA)
SPAN_TANH = math.tanh(BETA * ETA) + math.tanh(BETA * (1.0 - ETA))
F32, BF16 = jnp.float32, jnp.bfloat16
LANES = 128
XC, ZC, YC, ZW = 2, 16, 16, 4


def iota(shape, dim):
    return lax.broadcasted_iota(jnp.int32, shape, dim)


def tri(distance):
    return jnp.maximum(RADIUS + 1 - jnp.abs(distance), 0).astype(F32).astype(BF16)


def pieces(values):
    high = values.astype(BF16)
    rest = values - high.astype(F32)
    middle = rest.astype(BF16)
    return high, middle, (rest - middle.astype(F32)).astype(BF16)


def left_mul(weights, values):
    return sum(jnp.dot(weights, p, preferred_element_type=F32) for p in pieces(values))


def right_mul(values, weights):
    return sum(jnp.dot(p, weights, preferred_element_type=F32) for p in pieces(values))


def right_mul_t(weights, values):
    dims = (((1,), (1,)), ((), ()))
    return sum(lax.dot_general(weights, p, dims, preferred_element_type=F32) for p in pieces(values))


def roll_lanes(values, shift):
    shift %= values.shape[1]
    return pltpu.roll(values, shift, 1) if shift else values


def block_transpose(tile):
    block = iota((8, LANES), 1) // YC
    rolled = [roll_lanes(tile, YC * s) for s in range(8)]
    result = []
    for j in range(8):
        made = rolled[-j % 8][:8]
        for i in range(1, 8):
            made = jnp.where(block == i, rolled[(i - j) % 8][8 * i : 8 * i + 8], made)
        result.append(made)
    return result


def band_right(extent):
    return tri(iota((extent, extent), 0) - iota((extent, extent), 1))


def filter_y_kernel(design, solid, void, out):
    y_all = design.shape[2]
    cells = jnp.concatenate([design[:, x, :] for x in range(XC)], axis=0)
    along_y = right_mul(cells, band_right(y_all))
    live = jnp.concatenate(
        [(1.0 - solid[:, x, :].astype(F32)) * (1.0 - void[:, x, :].astype(F32)) for x in range(XC)], axis=0
    )
    both = jnp.concatenate([along_y, live], axis=0)
    for t in range(y_all // LANES):
        for m, tile in enumerate(block_transpose(both[:, LANES * t : LANES * (t + 1)])):
            out[64 * t + 8 * m : 64 * t + 8 * m + 8, :] = tile


def restrict_kernel(kirchhoff, adjoint, slope, x_before, x_after, y_before, y_after, out):
    x_fine, y_fine, z_fine = kirchhoff.shape
    row = iota((y_fine, z_fine), 0)
    lane = iota((y_fine, z_fine), 1)

    def diffs(f, field, x):
        centre = field[x]
        before = x_before[f, 0] if x == 0 else field[x - 1]
        after = x_after[f, 0] if x == x_fine - 1 else field[x + 1]
        grad_x = after - before
        up = jnp.where(row == 0, y_before[f, x], pltpu.roll(centre, 1, 0))
        down = jnp.where(row == y_fine - 1, y_after[f, x], pltpu.roll(centre, y_fine - 1, 0))
        left = jnp.where(lane == 0, 0.0, pltpu.roll(centre, 1, 1))
        right = jnp.where(lane == z_fine - 1, 0.0, pltpu.roll(centre, z_fine - 1, 1))
        return grad_x, down - up, right - left

    sensed = []
    for x in range(x_fine):
        k, a = diffs(0, kirchhoff, x), diffs(1, adjoint, x)
        product = k[0] * a[0] + k[1] * a[1] + k[2] * a[2]
        sensed.append(-0.25 * slope[x].astype(F32) * product)
    pairs = jnp.concatenate([sensed[2 * x] + sensed[2 * x + 1] for x in range(XC)], axis=0)
    rows_in, rows_out = XC * y_fine, XC * YC
    fold = (iota((rows_out, rows_in), 1) // 2 == iota((rows_out, rows_in), 0)).astype(F32).astype(BF16)
    pairs = left_mul(fold, pairs)
    z_quarter = iota((YC, z_fine), 1) // 2 % ZW
    spread = jnp.concatenate(
        [jnp.where(z_quarter == q, pairs[YC * x : YC * x + YC], 0.0) for x in range(XC) for q in range(ZW)], axis=0
    )
    wide = out.shape[0]
    gather = (iota((wide, z_fine), 1) // (2 * ZW) == iota((wide, z_fine), 0)).astype(F32).astype(BF16)
    out[...] = right_mul_t(gather, spread)


def filter_z_kernel(got, coarse, out, held, slots):
    rows = got.shape[0]
    narrow = rows // 8
    grid = got[...]
    lane = iota((rows, LANES), 1)
    half = lane // YC % 2
    after = jnp.where(half == 0, roll_lanes(grid, -YC), 0.0)
    before = jnp.where(half == 1, roll_lanes(grid, YC), 0.0)

    def base(dim):
        position = iota((rows, rows), dim)
        return ZC * (position // 8) + position % 8

    step = base(0) - base(1)
    weights = jnp.concatenate([tri(step), tri(step - 8), tri(step + 8)], axis=1)
    along_z = left_mul(weights, jnp.concatenate([grid, after, before], axis=0))
    held[...] = jnp.where(lane < LANES // 2, along_z, grid)
    block = iota((narrow, LANES), 1) // YC
    for low in range(2):
        picked = [held[pl.ds(4 * low + q, narrow, 8), :] for q in range(ZW)]
        for high in range(2):
            for a in range(2):
                made = None
                for x in range(XC):
                    for q in range(ZW):
                        target, source = ZW * x + q, 4 * a + 2 * x + high
                        moved = roll_lanes(picked[q], YC * (target - source))
                        made = moved if made is None else jnp.where(block == target, moved, made)
                slots.at[a][pl.ds(2 * high + low, narrow, 4), :] = made
    for a in range(2):
        out[:, LANES * a : LANES * (a + 1)] = slots[a]
    out[:, 2 * LANES :] = coarse[...]


def cover(positions, extent):
    low = jnp.maximum(RADIUS - positions, 0)
    high = jnp.maximum(RADIUS - (extent - 1 - positions), 0)
    return ((RADIUS + 1) ** 2 - low * (low + 1) // 2 - high * (high + 1) // 2).astype(F32)


def weigh_kernel(z_all, y_all, place, got, out):
    wide = got.shape[0]
    lane, row = iota((wide, LANES), 1), iota((wide, LANES), 0)
    step = 2 * (iota((wide, wide), 0) - iota((wide, wide), 1))
    weights = jnp.concatenate([tri(step), tri(step - 1), tri(step + 1)], axis=1)
    first = lane < LANES // 2

    def along_x(values):
        swapped = roll_lanes(values, LANES // 2)
        three = [values, jnp.where(first, swapped, 0.0), jnp.where(first, 0.0, swapped)]
        return left_mul(weights, jnp.concatenate(three, axis=0))

    cover_x = cover(XC * row + lane // (ZW * YC), XC * wide)
    cover_z = cover(place[0] * ZW + lane // YC % ZW, z_all)
    cover_y = cover(place[1] * YC + lane % YC, y_all)
    normalizer = cover_z * cover_x * cover_y
    filtered = along_x(got[:, :LANES]) / normalizer
    inner = jnp.tanh(BETA * (filtered - ETA))
    out[:, :LANES] = (LOWER_TANH + inner) / SPAN_TANH
    slope = BETA * (1.0 - inner * inner) / SPAN_TANH
    weighted = slope * got[:, 2 * LANES :] * got[:, LANES : 2 * LANES] / normalizer
    out[:, LANES:] = along_x(weighted)


def filter_z_back_kernel(got, out):
    wide = got.shape[0]
    density, weighted = got[:, :LANES], got[:, LANES:]
    quarter = iota((wide, LANES), 1) // YC % ZW
    step = ZW * (iota((wide, wide), 1) - iota((wide, wide), 0))
    weights, moved = [], []
    for d in range(1 - ZW, ZW):
        weights.append(tri(step + d))
        inside = (quarter + d >= 0) & (quarter + d < ZW)
        moved.append(jnp.where(inside, roll_lanes(weighted, -YC * d), 0.0))
    along_z = left_mul(jnp.concatenate(weights, axis=1), jnp.concatenate(moved, axis=0))
    per = ZC // ZW
    for n in range(wide // per):
        out[8 * n : 8 * n + per, :] = density[per * n : per * (n + 1)]
        out[8 * n + per : 8 * n + 2 * per, :] = along_z[per * n : per * (n + 1)]


def filter_y_back_kernel(got, solid, void, projected, sens, held):
    y_all = projected.shape[2]
    tiles = [block_transpose(got[64 * t : 64 * (t + 1), :]) for t in range(y_all // LANES)]
    lines = jnp.concatenate([jnp.concatenate(column, axis=0) for column in tiles], axis=1)
    along_y = right_mul(lines, band_right(y_all))
    per = ZC // ZW
    for x in range(XC):
        for q in range(ZW):
            at = 8 * (ZW * x + q)
            for t in range(y_all // LANES):
                lanes = slice(LANES * t, LANES * (t + 1))
                held[0, x, t, pl.ds(q, per, ZW), :] = lines[at : at + per, lanes]
                held[1, x, t, pl.ds(q, per, ZW), :] = along_y[at + per : at + 2 * per, lanes]
    for x in range(XC):
        is_solid, is_void = solid[:, x, :].astype(F32), void[:, x, :].astype(F32)
        live = (1.0 - is_solid) * (1.0 - is_void)
        density = jnp.concatenate([held[0, x, t] for t in range(y_all // LANES)], axis=1)
        smoothed = jnp.concatenate([held[1, x, t] for t in range(y_all // LANES)], axis=1)
        projected[:, x, :] = density * live + is_solid * (1.0 - is_void)
        sens[:, x, :] = smoothed * live


def call(kernel, shape, scratch=(), smem=()):
    def run(*args):
        specs = [pl.BlockSpec(memory_space=pltpu.SMEM if i in smem else pltpu.VMEM) for i in range(len(args))]
        out_shape = jax.tree.map(lambda s: jax.ShapeDtypeStruct(s, F32), shape, is_leaf=lambda s: isinstance(s[0], int))
        return pl.pallas_call(
            kernel,
            out_shape=out_shape,
            in_specs=specs,
            out_specs=jax.tree.map(lambda _: pl.BlockSpec(memory_space=pltpu.VMEM), out_shape),
            scratch_shapes=[pltpu.VMEM(s, F32) for s in scratch],
            compiler_params=pltpu.CompilerParams(vmem_limit_bytes=32 << 20),
        )(*args)

    return run


def neighbours(shards, axis, dim):
    count, length = lax.axis_size(axis), shards[0].shape[dim]
    up = [(i, i + 1) for i in range(count - 1)]
    down = [(j, i) for i, j in up]
    last = jnp.stack([lax.slice_in_dim(s, length - 1, length, axis=dim) for s in shards])
    initial = jnp.stack([lax.slice_in_dim(s, 0, 1, axis=dim) for s in shards])
    return lax.ppermute(last, axis, up), lax.ppermute(initial, axis, down)


def exchange(values, axis):
    return lax.all_to_all(values, axis, split_axis=0, concat_axis=0, tiled=True)


def exchange_rows(values, axis):
    rows, lanes = values.shape
    return exchange(values.reshape(rows, 1, lanes), axis).reshape(rows, lanes)


def per_device(kirchhoff, adjoint, penalty_slope, design, solid_mask, void_mask):
    wide, narrow = lax.axis_size("wide"), lax.axis_size("narrow")
    z_all, y_all = ZC * narrow, design.shape[2]

    sent = call(filter_y_kernel, (8 * narrow, LANES))(design, solid_mask, void_mask)
    got = exchange(sent, "narrow")

    y_before, y_after = neighbours((kirchhoff, adjoint), "narrow", 1)
    x_before, x_after = neighbours((kirchhoff, adjoint), "wide", 0)
    coarse = call(restrict_kernel, (wide, LANES))(
        kirchhoff, adjoint, penalty_slope, x_before, x_after, y_before, y_after
    )

    sent = call(filter_z_kernel, (wide, 3 * LANES), [(8 * narrow, LANES), (2, wide, LANES)])(got, coarse)
    place = jnp.stack([lax.axis_index("wide"), lax.axis_index("narrow")]).astype(jnp.int32)
    place, sent = lax.optimization_barrier((place, sent))
    got = exchange_rows(sent, "wide")

    def weigh(*refs):
        weigh_kernel(z_all, y_all, *refs)

    sent = call(weigh, (wide, 2 * LANES), smem=(0,))(place, got)
    got = exchange_rows(sent, "wide")
    sent = call(filter_z_back_kernel, (8 * narrow, LANES))(got)
    got = exchange(sent, "narrow")
    held = (2, XC, y_all // LANES, ZC, LANES)
    return call(filter_y_back_kernel, (design.shape, design.shape), [held])(got, solid_mask, void_mask)


def solution(mesh):
    fields = P("wide", "narrow", None)
    cells = P("narrow", "wide", None)
    return jax.shard_map(
        per_device,
        mesh=mesh,
        in_specs=(fields, fields, fields, cells, cells, cells),
        out_specs=(cells, cells),
        check_vma=False,
    )
```

time: 168 us -> 157 us (0.935)
  blocking collectives: 46.9 us -> 84.6 us
  waiting for transfers between devices: 35.5 us -> 11.8 us
  starting transfers between devices: 65.9 us -> 50.6 us
  local copies, waits for them, and re-layouts: 10.5 us -> 1.22 us
  Pallas kernels: 0 us -> 4.61 us
  matrix products: 2.78 us -> 0 us
  other arithmetic: 2.8 us -> 0.13 us
    all_to_all x2 -> x3, blocking collectives: 46.9 us -> 84.6 us  [exchange(): return lax.all_to_all(values, axis, split_axis=0, concat_axis=0, tiled=True)]
    all_to_all x2 -> x1, waiting for transfers between devices: 35.5 us -> 0.01 us  [exchange(): return lax.all_to_all(values, axis, split_axis=0, concat_axis=0, tiled=True)]
    all_to_all x2 -> x1, starting transfers between devices: 33.9 us -> 19.2 us  [exchange(): return lax.all_to_all(values, axis, split_axis=0, concat_axis=0, tiled=True)]
    ppermute x4, waiting for transfers between devices: 0.01 us -> 11.8 us  [neighbours(): return (lax.ppermute(last, axis, up), lax.ppermute(initial, axis, down))]
    pallas_call x0 -> x6, Pallas kernels: none -> 4.61 us  [run(): pl.pallas_call(kernel, out_shape=out_shape, in_specs=specs, out_specs=jax...]
    reshape x7 -> x2, local copies, waits for them, and re-layouts: 4.52 us -> 0.19 us  [exchange_rows(): return exchange(values.reshape(rows, 1, lanes), axis).reshape(rows, lanes)]
    unnamed x19 -> x14, local copies, waits for them, and re-layouts: 2.85 us -> 0.05 us
    dot_general x6 -> x0, matrix products: 2.4 us -> none  [the longest x1 0.6 us: per_device(): jnp.einsum('kz,zxy->kxy', band(z_all), got[:, 0], precision=HIGHEST)]
  transfers between devices with their start and end apart: 6 -> 5, of which waited for: 2 -> 1; matrix products, arithmetic and copies ran while one was open for 3% -> 0% of each run, Pallas kernels for 0% -> 1%
where the time goes in v2:
time: 157 us; the launch traced here: 154 us
  blocking collectives  84.6 us (54%)
  starting transfers between devices  50.6 us (32%)
  waiting for transfers between devices  11.8 us (8%)
  Pallas kernels  4.61 us (3%)
    all_to_all x3, blocking collectives, exchange(): return lax.all_to_all(values, axis, split_axis=0, concat_axis=0, tiled=True)  84.6 us
    ppermute x4, starting transfers between devices, neighbours(): return (lax.ppermute(last, axis, up), lax.ppermute(initial, axis, down))  31.4 us
    all_to_all x1, starting transfers between devices, exchange(): return lax.all_to_all(values, axis, split_axis=0, concat_axis=0, tiled=True)  19.2 us
    ppermute x4, waiting for transfers between devices, neighbours(): return (lax.ppermute(last, axis, up), lax.ppermute(initial, axis, down))  11.8 us
    pallas_call x6, Pallas kernels, run(): pl.pallas_call(kernel, out_shape=out_shape, in_specs=specs, out_specs=jax...  4.61 us
  transfers between devices with their start and end apart: 5, of which 1 were waited for; matrix products, arithmetic and copies ran while one was open for 0% of the time, Pallas kernels for 1%

profile of v2, /device:TPU:1, one launch (start us, length us, event | category | flops | bytes accessed | tf_op | source)
XLA Modules:
  0.0 153.8 jit_solution(6055404530034387337)
XLA Ops:
  0.6 1.0 slice_bitcast_fusion
  1.6 0.0 copy-start.3
  1.6 0.0 copy-start.4
  1.6 0.0 copy-start.5
  1.6 16.1 %collective-permute-start.1 = (f32[2,1,32,512]{3,2,1,0:T(8,128)S(1)}, f32[2,1,32,512]{3,2,1,0:T(8,128)S(1)}, u32[]{:S(2)}, u32[]{:S(2)}) collective-permute-start(f32[2,1,32,512]{3,2,1,0:T(8,128)S(1)} %pad_maximum_fusion.1), channel_id=1, source_target_pairs={{16,0},{32,16},{48,32},{64,48},{80,64},{96,80},{112,96},{128,112},... | collective-permute-start | bytes 393224 | tf_op jit(solution)/shard_map/ppermute | solution.py:241
  17.7 0.0 copy-start
  17.7 0.0 copy-start.1
  17.8 2.1 %collective-permute-start = (f32[2,1,32,512]{3,2,1,0:T(8,128)S(1)}, f32[2,1,32,512]{3,2,1,0:T(8,128)S(1)}, u32[]{:S(2)}, u32[]{:S(2)}) collective-permute-start(f32[2,1,32,512]{3,2,1,0:T(8,128)S(1)} %pad_maximum_fusion), channel_id=1, source_target_pairs={{0,16},{16,32},{32,48},{48,64},{64,80},{80,96},{96,112},{112,128},... | collective-permute-start | bytes 393224 | tf_op jit(solution)/shard_map/ppermute | solution.py:241
  19.8 0.0 copy-done.3
  19.8 0.0 copy-done.4
  19.8 0.0 copy-done.5
  19.9 1.0 shard_map.77
  20.8 0.0 copy-start.2
  20.8 19.2 %all-to-all-start = ((f32[16,8,128]{2,1,0:T(8,128)}), f32[16,8,128]{2,1,0:T(8,128)S(1)}, u32[]{:S(2)}, u32[]{:S(2)}) async-start(f32[16,8,128]{2,1,0:T(8,128)} %bitcast.2), calls=%async_computation | async-start | bytes 131072 | tf_op jit(solution)/shard_map/all_to_all | solution.py:245
  40.0 0.0 copy-done
  40.0 0.0 copy-done.1
  40.1 12.0 %collective-permute-start.2 = (f32[2,4,1,512]{3,2,1,0:T(1,128)S(1)}, f32[2,4,1,512]{3,2,1,0:T(1,128)S(1)}, u32[]{:S(2)}, u32[]{:S(2)}) collective-permute-start(f32[2,4,1,512]{3,2,1,0:T(1,128)S(1)} %pad_maximum_fusion.2), channel_id=1, source_target_pairs={{0,1},{1,2},{2,3},{3,4},{4,5},{5,6},{6,7},{7,8},{8,9},{9,10},{10,1... | collective-permute-start | bytes 49160 | tf_op jit(solution)/shard_map/ppermute | solution.py:241
  52.1 1.3 collective-permute-start.3
  53.4 0.1 pad_add_fusion.refs_0_
  53.5 0.0 collective-permute-done.2.y_before
  53.5 11.8 %collective-permute-done.3.y_after = f32[2,4,1,512]{3,2,1,0:T(1,128)S(1)} collective-permute-done((f32[2,4,1,512]{3,2,1,0:T(1,128)S(1)}, f32[2,4,1,512]{3,2,1,0:T(1,128)S(1)}, u32[]{:S(2)}, u32[]{:S(2)}) %collective-permute-start.3) | collective-permute-done | bytes 16416 | tf_op jit(solution)/shard_map/ppermute | solution.py:241
  65.3 0.0 collective-permute-done.1.x_after
  65.3 0.0 collective-permute-done.x_before
  65.3 0.0 copy-done.2
  65.3 0.8 shard_map.78.coarse
  66.1 0.0 all-to-all-done
  66.1 0.5 shard_map.79
  66.6 0.1 copy.8
  66.7 29.4 %all_to_all.32 = f32[64,1,384]{2,1,0:T(1,128)S(1)} all-to-all(f32[64,1,384]{2,1,0:T(1,128)S(1)} %copy.8), channel_id=1, replica_groups=mesh['wide'=64,'narrow'=16] {'wide'}, dimensions={0} | all-to-all | bytes 196608 | tf_op jit(solution)/shard_map/all_to_all | solution.py:245
  96.1 1.1 shard_map.80
  97.2 0.1 copy.9
  97.3 18.3 %all_to_all.33 = f32[64,1,256]{2,1,0:T(1,128)S(1)} all-to-all(f32[64,1,256]{2,1,0:T(1,128)S(1)} %copy.9), channel_id=1, replica_groups=mesh['wide'=64,'narrow'=16] {'wide'}, dimensions={0} | all-to-all | bytes 131072 | tf_op jit(solution)/shard_map/all_to_all | solution.py:245
  115.6 0.3 shard_map.81
  115.9 36.9 %all_to_all.34 = f32[16,8,128]{2,1,0:T(8,128)S(1)} all-to-all(f32[16,8,128]{2,1,0:T(8,128)S(1)} %bitcast.36), channel_id=1, replica_groups=mesh['wide'=64,'narrow'=16] {'narrow'}, dimensions={0} | all-to-all | bytes 131072 | tf_op jit(solution)/shard_map/all_to_all | solution.py:245
  152.8 1.0 shard_map.82
  (7 shorter events, 0.1 us)
Async XLA Ops:
  1.6 18.2 %copy-start.3 = (s32[16,2,256]{2,1,0:T(2,128)S(1)}, s32[16,2,256]{2,1,0:T(2,128)}, u32[]{:S(2)}) copy-start(s32[16,2,256]{2,1,0:T(2,128)} %solid.3) | copy-start | bytes 98308
  1.6 18.2 %copy-start.4 = (s32[16,2,256]{2,1,0:T(2,128)S(1)}, s32[16,2,256]{2,1,0:T(2,128)}, u32[]{:S(2)}) copy-start(s32[16,2,256]{2,1,0:T(2,128)} %void.3) | copy-start | bytes 98308
  1.6 18.2 %copy-start.5 = (f32[16,2,256]{2,1,0:T(2,128)S(1)}, f32[16,2,256]{2,1,0:T(2,128)}, u32[]{:S(2)}) copy-start(f32[16,2,256]{2,1,0:T(2,128)} %design.1) | copy-start | bytes 98308
  1.6 63.7 %collective-permute-start.1 = (f32[2,1,32,512]{3,2,1,0:T(8,128)S(1)}, f32[2,1,32,512]{3,2,1,0:T(8,128)S(1)}, u32[]{:S(2)}, u32[]{:S(2)}) collective-permute-start(f32[2,1,32,512]{3,2,1,0:T(8,128)S(1)} %pad_maximum_fusion.1), channel_id=1, source_target_pairs={{16,0},{32,16},{48,32},{64,48},{80,64},{96,80},{112,96},{128,112},... | collective-permute-start | bytes 393224 | tf_op jit(solution)/shard_map/ppermute | solution.py:241
  17.7 22.3 %copy-start = (f32[4,32,512]{2,1,0:T(8,128)S(1)}, f32[4,32,512]{2,1,0:T(8,128)}, u32[]{:S(2)}) copy-start(f32[4,32,512]{2,1,0:T(8,128)} %kirchhoff.1) | copy-start | bytes 786436
  17.7 22.3 %copy-start.1 = (f32[4,32,512]{2,1,0:T(8,128)S(1)}, f32[4,32,512]{2,1,0:T(8,128)}, u32[]{:S(2)}) copy-start(f32[4,32,512]{2,1,0:T(8,128)} %adjoint.1) | copy-start | bytes 786436
  17.8 47.5 %collective-permute-start = (f32[2,1,32,512]{3,2,1,0:T(8,128)S(1)}, f32[2,1,32,512]{3,2,1,0:T(8,128)S(1)}, u32[]{:S(2)}, u32[]{:S(2)}) collective-permute-start(f32[2,1,32,512]{3,2,1,0:T(8,128)S(1)} %pad_maximum_fusion), channel_id=1, source_target_pairs={{0,16},{16,32},{32,48},{48,64},{64,80},{80,96},{96,112},{112,128},... | collective-permute-start | bytes 393224 | tf_op jit(solution)/shard_map/ppermute | solution.py:241
  20.8 44.5 %copy-start.2 = (bf16[4,32,512]{2,1,0:T(8,128)(2,1)S(1)}, bf16[4,32,512]{2,1,0:T(8,128)(2,1)}, u32[]{:S(2)}) copy-start(bf16[4,32,512]{2,1,0:T(8,128)(2,1)} %slope.1) | copy-start | bytes 393220
  20.8 45.3 %all-to-all-start = ((f32[16,8,128]{2,1,0:T(8,128)}), f32[16,8,128]{2,1,0:T(8,128)S(1)}, u32[]{:S(2)}, u32[]{:S(2)}) async-start(f32[16,8,128]{2,1,0:T(8,128)} %bitcast.2), calls=%async_computation | async-start | bytes 131072 | tf_op jit(solution)/shard_map/all_to_all | solution.py:245
  40.1 13.4 %collective-permute-start.2 = (f32[2,4,1,512]{3,2,1,0:T(1,128)S(1)}, f32[2,4,1,512]{3,2,1,0:T(1,128)S(1)}, u32[]{:S(2)}, u32[]{:S(2)}) collective-permute-start(f32[2,4,1,512]{3,2,1,0:T(1,128)S(1)} %pad_maximum_fusion.2), channel_id=1, source_target_pairs={{0,1},{1,2},{2,3},{3,4},{4,5},{5,6},{6,7},{7,8},{8,9},{9,10},{10,1... | collective-permute-start | bytes 49160 | tf_op jit(solution)/shard_map/ppermute | solution.py:241
  52.1 13.2 %collective-permute-start.3 = (f32[2,4,1,512]{3,2,1,0:T(1,128)S(1)}, f32[2,4,1,512]{3,2,1,0:T(1,128)S(1)}, u32[]{:S(2)}, u32[]{:S(2)}) collective-permute-start(f32[2,4,1,512]{3,2,1,0:T(1,128)S(1)} %pad_maximum_fusion.3), channel_id=1, source_target_pairs={{1,0},{2,1},{3,2},{4,3},{5,4},{6,5},{7,6},{8,7},{9,8},{10,9},{11,1... | collective-permute-start | bytes 49160 | tf_op jit(solution)/shard_map/ppermute | solution.py:241

commit v3 on v2

v3 whole, which is shorter than its diff:
```python
import math

import jax
import jax.numpy as jnp
from jax import lax
from jax.experimental import pallas as pl
from jax.experimental.pallas import tpu as pltpu
from jax.sharding import PartitionSpec as P

RADIUS = 12
BETA = 32.0
ETA = 0.5
LOWER_TANH = math.tanh(BETA * ETA)
SPAN_TANH = math.tanh(BETA * ETA) + math.tanh(BETA * (1.0 - ETA))
F32, BF16 = jnp.float32, jnp.bfloat16
LANES = 128
XC, ZC, YC, YW = 2, 16, 16, 4


def iota(shape, dim):
    return lax.broadcasted_iota(jnp.int32, shape, dim)


def tri(distance):
    return jnp.maximum(RADIUS + 1 - jnp.abs(distance), 0).astype(F32).astype(BF16)


def pieces(values):
    high = values.astype(BF16)
    rest = values - high.astype(F32)
    middle = rest.astype(BF16)
    return high, middle, (rest - middle.astype(F32)).astype(BF16)


def left_mul(weights, values):
    return sum(jnp.dot(weights, p, preferred_element_type=F32) for p in pieces(values))


def right_mul(values, weights):
    return sum(jnp.dot(p, weights, preferred_element_type=F32) for p in pieces(values))


def right_mul_t(weights, values):
    dims = (((1,), (1,)), ((), ()))
    return sum(lax.dot_general(weights, p, dims, preferred_element_type=F32) for p in pieces(values))


def roll_lanes(values, shift):
    shift %= values.shape[1]
    return pltpu.roll(values, shift, 1) if shift else values


def block_transpose(tile):
    r = tile.shape[0] // 8
    block = iota((r, LANES), 1) // ZC
    rolled = [roll_lanes(tile, ZC * s) for s in range(8)]
    result = []
    for j in range(8):
        made = rolled[-j % 8][:r]
        for i in range(1, 8):
            made = jnp.where(block == i, rolled[(i - j) % 8][r * i : r * (i + 1)], made)
        result.append(made)
    return result


def pack_kernel(kirchhoff, adjoint, design, y_last, y_first, x_last, x_first):
    x_fine, y_fine, _ = kirchhoff.shape
    y_all = design.shape[2]
    for out, y, x in ((y_last, y_fine - 1, x_fine - 1), (y_first, 0, 0)):
        for f, field in enumerate((kirchhoff, adjoint)):
            for k in range(x_fine):
                out[x_fine * f + k : x_fine * f + k + 1, :] = field[k, y : y + 1, :]
        for k in range(XC):
            out[2 * x_fine :, y_all * k : y_all * (k + 1)] = design[:, k, :]
    for out, x in ((x_last, x_fine - 1), (x_first, 0)):
        out[0] = kirchhoff[x]
        out[1] = adjoint[x]


def restrict_kernel(kirchhoff, adjoint, slope, x_before, x_after, n_before, n_after, out):
    x_fine, y_fine, z_fine = kirchhoff.shape
    row = iota((y_fine, z_fine), 0)
    lane = iota((y_fine, z_fine), 1)

    def diffs(f, field, x):
        centre = field[x]
        before = x_before[f] if x == 0 else field[x - 1]
        after = x_after[f] if x == x_fine - 1 else field[x + 1]
        grad_x = after - before
        at = x_fine * f + x
        up = jnp.where(row == 0, n_before[at : at + 1, :], pltpu.roll(centre, 1, 0))
        down = jnp.where(row == y_fine - 1, n_after[at : at + 1, :], pltpu.roll(centre, y_fine - 1, 0))
        left = jnp.where(lane == 0, 0.0, pltpu.roll(centre, 1, 1))
        right = jnp.where(lane == z_fine - 1, 0.0, pltpu.roll(centre, z_fine - 1, 1))
        return grad_x, down - up, right - left

    sensed = []
    for x in range(x_fine):
        k, a = diffs(0, kirchhoff, x), diffs(1, adjoint, x)
        product = k[0] * a[0] + k[1] * a[1] + k[2] * a[2]
        sensed.append(-0.25 * slope[x].astype(F32) * product)
    pairs = jnp.concatenate([sensed[2 * x] + sensed[2 * x + 1] for x in range(XC)], axis=0)
    shape = (XC * YC, XC * y_fine)
    made, given = iota(shape, 0), iota(shape, 1)
    y_made = YW * (made % YW) + made // YW % YW
    fold = (made // YC == given // y_fine) & (given % y_fine // 2 == y_made)
    pairs = left_mul(fold.astype(F32).astype(BF16), pairs)
    shape = (z_fine, z_fine // 2)
    pairs = right_mul(pairs, (iota(shape, 0) // 2 == iota(shape, 1)).astype(F32).astype(BF16))
    count = pairs.shape[1] // LANES
    parts = [pairs[YW * i : YW * (i + 1), LANES * t : LANES * (t + 1)] for i in range(8) for t in range(count)]
    for m, tile in enumerate(block_transpose(jnp.concatenate(parts, axis=0))):
        for t in range(count):
            at = YW * (8 * t + m)
            out[at : at + YW, :] = tile[YW * t : YW * (t + 1)]


def lines_of(values, wide):
    part = iota((wide, LANES), 1) // ZC % YW
    made = values[:wide]
    for r in range(1, YW):
        made = jnp.where(part == r, values[wide * r : wide * (r + 1)], made)
    return made


def design_kernel(design, solid, void, n_before, n_after, out):
    wide = out.shape[0]
    y_all = design.shape[2]
    skip = n_before.shape[0] - ZC
    shape = (ZC, 3 * ZC)
    weights = tri(iota(shape, 1) - iota(shape, 0) - ZC)
    along_z, live = [], []
    for x in range(XC):
        lanes = slice(y_all * x, y_all * (x + 1))
        planes = jnp.concatenate([n_before[skip:, lanes], design[:, x, :], n_after[skip:, lanes]], axis=0)
        along_z += [left_mul(weights, planes)] * YW
        is_live = (1.0 - solid[:, x, :].astype(F32)) * (1.0 - void[:, x, :].astype(F32))
        live += [is_live] * YW
    shape = (y_all, y_all)
    step = YW * (iota(shape, 0) % wide) + iota(shape, 0) // wide - iota(shape, 1)
    out[:, :LANES] = lines_of(right_mul_t(tri(step), jnp.concatenate(along_z, axis=0)), wide)
    place = (step == 0).astype(F32).astype(BF16)
    moved = lax.dot_general(
        place, jnp.concatenate(live, axis=0).astype(BF16), (((1,), (1,)), ((), ())), preferred_element_type=F32
    )
    out[:, LANES:] = lines_of(moved, wide)


def cover(positions, extent):
    low = jnp.maximum(RADIUS - positions, 0)
    high = jnp.maximum(RADIUS - (extent - 1 - positions), 0)
    return ((RADIUS + 1) ** 2 - low * (low + 1) // 2 - high * (high + 1) // 2).astype(F32)


def weigh_kernel(z_all, y_all, place, got, out):
    wide = got.shape[0]
    lane, row = iota((wide, LANES), 1), iota((wide, LANES), 0)
    step = 2 * (iota((wide, wide), 0) - iota((wide, wide), 1))
    weights = jnp.concatenate([tri(step), tri(step - 1), tri(step + 1)], axis=1)
    first = lane < LANES // 2

    def along_x(values):
        swapped = roll_lanes(values, LANES // 2)
        three = [values, jnp.where(first, swapped, 0.0), jnp.where(first, 0.0, swapped)]
        return left_mul(weights, jnp.concatenate(three, axis=0))

    cover_x = cover(XC * row + lane // (LANES // XC), XC * wide)
    cover_z = cover(place[1] * ZC + lane % ZC, z_all)
    cover_y = cover(place[0] * YW + lane // ZC % YW, y_all)
    normalizer = cover_z * cover_x * cover_y
    filtered = along_x(got[:, :LANES]) / normalizer
    inner = jnp.tanh(BETA * (filtered - ETA))
    out[:, :LANES] = (LOWER_TANH + inner) / SPAN_TANH
    slope = BETA * (1.0 - inner * inner) / SPAN_TANH
    weighted = slope * got[:, 2 * LANES :] * got[:, LANES : 2 * LANES] / normalizer
    out[:, LANES:] = along_x(weighted)


def along_lanes(values):
    turned = values.T
    rows = [[turned[ZC * (YW * x + r) : ZC * (YW * x + r + 1), :] for r in range(YW)] for x in range(XC)]
    return [jnp.concatenate(r, axis=1) for r in rows]


def y_steps(wide, y_all):
    shape = (YW * wide, y_all)
    return YW * (iota(shape, 0) % wide) + iota(shape, 0) // wide - iota(shape, 1)


def density_kernel(density, solid, void, projected):
    wide, y_all = density.shape[0], projected.shape[2]
    place = (y_steps(wide, y_all) == 0).astype(F32).astype(BF16)
    for x, lines in enumerate(along_lanes(density[...])):
        is_solid, is_void = solid[:, x, :].astype(F32), void[:, x, :].astype(F32)
        live = (1.0 - is_solid) * (1.0 - is_void)
        projected[:, x, :] = right_mul(lines, place) * live + is_solid * (1.0 - is_void)


def sens_kernel(before, own, after, solid, void, sens):
    wide, y_all = own.shape[0], sens.shape[2]
    given, made = iota((LANES, LANES), 0), iota((LANES, LANES), 1)
    step = jnp.where(given // ZC == made // ZC, given % ZC - made % ZC, 4 * ZC)
    weights = jnp.concatenate([tri(step - ZC), tri(step), tri(step + ZC)], axis=0)
    along_z = right_mul(jnp.concatenate([before[...], own[...], after[...]], axis=1), weights)
    weights = tri(y_steps(wide, y_all))
    for x, lines in enumerate(along_lanes(along_z)):
        live = (1.0 - solid[:, x, :].astype(F32)) * (1.0 - void[:, x, :].astype(F32))
        sens[:, x, :] = right_mul(lines, weights) * live


def call(kernel, shape, scratch=(), smem=()):
    def run(*args):
        specs = [pl.BlockSpec(memory_space=pltpu.SMEM if i in smem else pltpu.VMEM) for i in range(len(args))]
        out_shape = jax.tree.map(lambda s: jax.ShapeDtypeStruct(s, F32), shape, is_leaf=lambda s: isinstance(s[0], int))
        return pl.pallas_call(
            kernel,
            out_shape=out_shape,
            in_specs=specs,
            out_specs=jax.tree.map(lambda _: pl.BlockSpec(memory_space=pltpu.VMEM), out_shape),
            scratch_shapes=[pltpu.VMEM(s, F32) for s in scratch],
            compiler_params=pltpu.CompilerParams(vmem_limit_bytes=32 << 20),
        )(*args)

    return run


def to_sides(last, first, axis):
    up = [(i, i + 1) for i in range(lax.axis_size(axis) - 1)]
    return lax.ppermute(last, axis, up), lax.ppermute(first, axis, [(j, i) for i, j in up])


def exchange(values, axis):
    return lax.all_to_all(values, axis, split_axis=0, concat_axis=0, tiled=True)


def exchange_rows(values, axis):
    rows, lanes = values.shape
    return exchange(values.reshape(rows, 1, lanes), axis).reshape(rows, lanes)


def per_device(kirchhoff, adjoint, penalty_slope, design, solid_mask, void_mask):
    wide, narrow = lax.axis_size("wide"), lax.axis_size("narrow")
    z_all, y_all = ZC * narrow, design.shape[2]
    x_fine, y_fine, z_fine = kirchhoff.shape

    n_shape, x_shape = (2 * x_fine + ZC, z_fine), (2, y_fine, z_fine)
    packed = call(pack_kernel, (n_shape, n_shape, x_shape, x_shape))(kirchhoff, adjoint, design)
    n_before, n_after = to_sides(packed[0], packed[1], "narrow")
    x_before, x_after = to_sides(packed[2], packed[3], "wide")
    coarse = call(restrict_kernel, (YW * narrow, LANES))(
        kirchhoff, adjoint, penalty_slope, x_before, x_after, n_before, n_after
    )
    coarse = exchange(coarse, "narrow")
    lines = call(design_kernel, (wide, 2 * LANES))(design, solid_mask, void_mask, n_before, n_after)
    sent = jnp.concatenate([lines, coarse], axis=1)

    place = jnp.stack([lax.axis_index("wide"), lax.axis_index("narrow")]).astype(jnp.int32)
    place, sent = lax.optimization_barrier((place, sent))
    got = exchange_rows(sent, "wide")

    def weigh(*refs):
        weigh_kernel(z_all, y_all, *refs)

    sent = call(weigh, (wide, 2 * LANES), smem=(0,))(place, got)
    got = exchange_rows(sent, "wide")
    weighted = got[:, LANES:]
    before, after = to_sides(weighted, weighted, "narrow")
    projected = call(density_kernel, design.shape)(got[:, :LANES], solid_mask, void_mask)
    sens = call(sens_kernel, design.shape)(before, weighted, after, solid_mask, void_mask)
    return projected, sens


def solution(mesh):
    fields = P("wide", "narrow", None)
    cells = P("narrow", "wide", None)
    return jax.shard_map(
        per_device,
        mesh=mesh,
        in_specs=(fields, fields, fields, cells, cells, cells),
        out_specs=(cells, cells),
        check_vma=False,
    )
```

time: 157 us -> 156 us (level); the launches traced: 154 us -> 156 us
  waiting for transfers between devices: 11.8 us -> 53.7 us
  blocking collectives: 84.6 us -> 47.5 us
  starting transfers between devices: 50.6 us -> 45.5 us
  local copies, waits for them, and re-layouts: 1.22 us -> 2.88 us
    all_to_all x3 -> x2, blocking collectives: 84.6 us -> 47.5 us  [exchange(): return lax.all_to_all(values, axis, split_axis=0, concat_axis=0, tiled=True)]
    all_to_all x1, waiting for transfers between devices: 0.01 us -> 22.8 us  [exchange(): return lax.all_to_all(values, axis, split_axis=0, concat_axis=0, tiled=True)]
    ppermute x4 -> x6, waiting for transfers between devices: 11.8 us -> 30.9 us  [the longest x3 30.8 us: to_sides(): lax.ppermute(first, axis, [(j, i) for i, j in up])]
    ppermute x4 -> x6, starting transfers between devices: 31.4 us -> 27.2 us  [the longest x3 15 us: to_sides(): lax.ppermute(first, axis, [(j, i) for i, j in up])]
    unnamed x14 -> x16, local copies, waits for them, and re-layouts: 0.05 us -> 2.68 us
  transfers between devices with their start and end apart: 5 -> 7, of which waited for: 1 -> 3; matrix products, arithmetic and copies ran while one was open for 0% -> 0% of each run, Pallas kernels for 1% -> 1%
where the time goes in v3:
time: 156 us
  waiting for transfers between devices  53.7 us (34%)
  blocking collectives  47.5 us (30%)
  starting transfers between devices  45.5 us (29%)
  Pallas kernels  5.25 us (3%)
  local copies, waits for them, and re-layouts  2.88 us (2%)
    all_to_all x2, blocking collectives, exchange(): return lax.all_to_all(values, axis, split_axis=0, concat_axis=0, tiled=True)  47.5 us
    ppermute x3, waiting for transfers between devices, to_sides(): lax.ppermute(first, axis, [(j, i) for i, j in up])  30.8 us
    all_to_all x1, waiting for transfers between devices, exchange(): return lax.all_to_all(values, axis, split_axis=0, concat_axis=0, tiled=True)  22.8 us
    all_to_all x1, starting transfers between devices, exchange(): return lax.all_to_all(values, axis, split_axis=0, concat_axis=0, tiled=True)  18.3 us
    ppermute x3, starting transfers between devices, to_sides(): lax.ppermute(first, axis, [(j, i) for i, j in up])  15 us
    ppermute x3, starting transfers between devices, to_sides(): lax.ppermute(last, axis, up)  12.2 us
    pallas_call x6, Pallas kernels, run(): pl.pallas_call(kernel, out_shape=out_shape, in_specs=specs, out_specs=jax...  5.25 us
  transfers between devices with their start and end apart: 7, of which 3 were waited for; matrix products, arithmetic and copies ran while one was open for 0% of the time, Pallas kernels for 1%

profile of v3, /device:TPU:1, one launch (start us, length us, event | category | flops | bytes accessed | tf_op | source)
XLA Modules:
  0.0 155.7 jit_solution(5052703523056316931)
XLA Ops:
  0.6 0.0 copy-start
  0.6 0.9 copy-done
  1.6 0.0 copy-start.1
  1.6 0.9 copy-done.1
  2.5 0.0 copy-start.4
  2.5 0.8 copy-done.4
  3.3 0.0 copy-start.6
  3.3 5.1 %collective-permute-start.2 = (f32[2,32,512]{2,1,0:T(8,128)S(1)}, f32[2,32,512]{2,1,0:T(8,128)S(1)}, u32[]{:S(2)}, u32[]{:S(2)}) collective-permute-start(f32[2,32,512]{2,1,0:T(8,128)S(1)} %get-tuple-element.10), channel_id=1, source_target_pairs={{0,16},{16,32},{32,48},{48,64},{64,80},{80,96},{96,112},{112,128},... | collective-permute-start | bytes 393224 | tf_op jit(solution)/shard_map/ppermute | solution.py:229
  8.4 12.4 %collective-permute-start.3 = (f32[2,32,512]{2,1,0:T(8,128)S(1)}, f32[2,32,512]{2,1,0:T(8,128)S(1)}, u32[]{:S(2)}, u32[]{:S(2)}) collective-permute-start(f32[2,32,512]{2,1,0:T(8,128)S(1)} %get-tuple-element.11), channel_id=1, source_target_pairs={{16,0},{32,16},{48,32},{64,48},{80,64},{96,80},{112,96},{128,112},... | collective-permute-start | bytes 393224 | tf_op jit(solution)/shard_map/ppermute | solution.py:229
  20.8 4.9 %collective-permute-start = (f32[24,512]{1,0:T(8,128)S(1)}, f32[24,512]{1,0:T(8,128)S(1)}, u32[]{:S(2)}, u32[]{:S(2)}) collective-permute-start(f32[24,512]{1,0:T(8,128)S(1)} %get-tuple-element.8), channel_id=1, source_target_pairs={{0,1},{1,2},{2,3},{3,4},{4,5},{5,6},{6,7},{7,8},{8,9},{9,10},{10,1... | collective-permute-start | bytes 147464 | tf_op jit(solution)/shard_map/ppermute | solution.py:229
  25.8 1.3 collective-permute-start.1
  27.1 0.0 collective-permute-done.n_before
  27.1 14.7 %collective-permute-done.1.n_after = f32[24,512]{1,0:T(8,128)S(1)} collective-permute-done((f32[24,512]{1,0:T(8,128)S(1)}, f32[24,512]{1,0:T(8,128)S(1)}, u32[]{:S(2)}, u32[]{:S(2)}) %collective-permute-start.1) | collective-permute-done | bytes 49184 | tf_op jit(solution)/shard_map/ppermute | solution.py:229
  41.8 0.0 collective-permute-done.2.x_before
  41.8 0.0 collective-permute-done.3.x_after
  41.8 0.0 copy-done.6
  41.8 0.0 copy-start.5
  41.8 1.5 shard_map.79
  43.3 0.0 copy-start.2
  43.3 0.0 copy-start.3
  43.3 18.3 %all-to-all-start = ((f32[16,4,128]{2,1,0:T(4,128)}), f32[16,4,128]{2,1,0:T(4,128)S(1)}, u32[]{:S(2)}, u32[]{:S(2)}) async-start(f32[16,4,128]{2,1,0:T(4,128)} %bitcast.2), calls=%async_computation | async-start | bytes 65536 | tf_op jit(solution)/shard_map/all_to_all | solution.py:233
  61.6 0.1 pad_add_fusion.refs_0_
  61.7 0.0 copy-done.5
  61.7 0.0 copy-done.2
  61.7 0.0 copy-done.3
  61.7 0.5 shard_map.78
  62.2 22.8 %all-to-all-done = f32[16,4,128]{2,1,0:T(4,128)S(1)} async-done(((f32[16,4,128]{2,1,0:T(4,128)}), f32[16,4,128]{2,1,0:T(4,128)S(1)}, u32[]{:S(2)}, u32[]{:S(2)}) %all-to-all-start) | async-done | bytes 32800 | tf_op jit(solution)/shard_map/all_to_all | solution.py:233
  85.0 0.1 copy.8
  85.1 29.2 %all_to_all.22 = f32[64,1,384]{2,1,0:T(1,128)S(1)} all-to-all(f32[64,1,384]{2,1,0:T(1,128)S(1)} %copy.8), channel_id=1, replica_groups=mesh['wide'=64,'narrow'=16] {'wide'}, dimensions={0} | all-to-all | bytes 196608 | tf_op jit(solution)/shard_map/all_to_all | solution.py:233
  114.4 1.1 shard_map.80
  115.4 0.1 copy.9
  115.5 18.3 %all_to_all.23 = f32[64,1,256]{2,1,0:T(1,128)S(1)} all-to-all(f32[64,1,256]{2,1,0:T(1,128)S(1)} %copy.9), channel_id=1, replica_groups=mesh['wide'=64,'narrow'=16] {'wide'}, dimensions={0} | all-to-all | bytes 131072 | tf_op jit(solution)/shard_map/all_to_all | solution.py:233
  133.9 2.2 %collective-permute-start.4 = (f32[64,128]{1,0:T(8,128)S(1)}, f32[64,128]{1,0:T(8,128)S(1)}, u32[]{:S(2)}, u32[]{:S(2)}) collective-permute-start(f32[64,128]{1,0:T(8,128)S(1)} %get-tuple-element.14.own), channel_id=1, source_target_pairs={{0,1},{1,2},{2,3},{3,4},{4,5},{5,6},{6,7},{7,8},{8,9},{9,10},{10,1... | collective-permute-start | bytes 98312 | tf_op jit(solution)/shard_map/ppermute | solution.py:229
  136.1 1.3 collective-permute-start.5
  137.4 1.0 shard_map.81
  138.4 0.0 collective-permute-done.4.before
  138.4 16.1 %collective-permute-done.5.after = f32[64,128]{1,0:T(8,128)S(1)} collective-permute-done((f32[64,128]{1,0:T(8,128)S(1)}, f32[64,128]{1,0:T(8,128)S(1)}, u32[]{:S(2)}, u32[]{:S(2)}) %collective-permute-start.5) | collective-permute-done | bytes 32800 | tf_op jit(solution)/shard_map/ppermute | solution.py:229
  154.5 1.2 shard_map.82
  (5 shorter events, 0.1 us)
Async XLA Ops:
  0.6 1.0 copy-start
  1.6 0.9 copy-start.1
  2.5 0.8 copy-start.4
  3.3 38.5 %copy-start.6 = (bf16[4,32,512]{2,1,0:T(8,128)(2,1)S(1)}, bf16[4,32,512]{2,1,0:T(8,128)(2,1)}, u32[]{:S(2)}) copy-start(bf16[4,32,512]{2,1,0:T(8,128)(2,1)} %slope.1) | copy-start | bytes 393220
  3.3 38.5 %collective-permute-start.2 = (f32[2,32,512]{2,1,0:T(8,128)S(1)}, f32[2,32,512]{2,1,0:T(8,128)S(1)}, u32[]{:S(2)}, u32[]{:S(2)}) collective-permute-start(f32[2,32,512]{2,1,0:T(8,128)S(1)} %get-tuple-element.10), channel_id=1, source_target_pairs={{0,16},{16,32},{32,48},{48,64},{64,80},{80,96},{96,112},{112,128},... | collective-permute-start | bytes 393224 | tf_op jit(solution)/shard_map/ppermute | solution.py:229
  8.4 33.4 %collective-permute-start.3 = (f32[2,32,512]{2,1,0:T(8,128)S(1)}, f32[2,32,512]{2,1,0:T(8,128)S(1)}, u32[]{:S(2)}, u32[]{:S(2)}) collective-permute-start(f32[2,32,512]{2,1,0:T(8,128)S(1)} %get-tuple-element.11), channel_id=1, source_target_pairs={{16,0},{32,16},{48,32},{64,48},{80,64},{96,80},{112,96},{128,112},... | collective-permute-start | bytes 393224 | tf_op jit(solution)/shard_map/ppermute | solution.py:229
  20.8 6.2 %collective-permute-start = (f32[24,512]{1,0:T(8,128)S(1)}, f32[24,512]{1,0:T(8,128)S(1)}, u32[]{:S(2)}, u32[]{:S(2)}) collective-permute-start(f32[24,512]{1,0:T(8,128)S(1)} %get-tuple-element.8), channel_id=1, source_target_pairs={{0,1},{1,2},{2,3},{3,4},{4,5},{5,6},{6,7},{7,8},{8,9},{9,10},{10,1... | collective-permute-start | bytes 147464 | tf_op jit(solution)/shard_map/ppermute | solution.py:229
  25.8 16.0 %collective-permute-start.1 = (f32[24,512]{1,0:T(8,128)S(1)}, f32[24,512]{1,0:T(8,128)S(1)}, u32[]{:S(2)}, u32[]{:S(2)}) collective-permute-start(f32[24,512]{1,0:T(8,128)S(1)} %get-tuple-element.9), channel_id=1, source_target_pairs={{1,0},{2,1},{3,2},{4,3},{5,4},{6,5},{7,6},{8,7},{9,8},{10,9},{11,1... | collective-permute-start | bytes 147464 | tf_op jit(solution)/shard_map/ppermute | solution.py:229
  41.8 19.8 %copy-start.5 = (f32[16,2,256]{2,1,0:T(2,128)S(1)}, f32[16,2,256]{2,1,0:T(2,128)}, u32[]{:S(2)}) copy-start(f32[16,2,256]{2,1,0:T(2,128)} %design.3) | copy-start | bytes 98308
  43.3 18.4 %copy-start.2 = (s32[16,2,256]{2,1,0:T(2,128)S(1)}, s32[16,2,256]{2,1,0:T(2,128)}, u32[]{:S(2)}) copy-start(s32[16,2,256]{2,1,0:T(2,128)} %solid.5) | copy-start | bytes 98308
  43.3 18.4 %copy-start.3 = (s32[16,2,256]{2,1,0:T(2,128)S(1)}, s32[16,2,256]{2,1,0:T(2,128)}, u32[]{:S(2)}) copy-start(s32[16,2,256]{2,1,0:T(2,128)} %void.5) | copy-start | bytes 98308
  43.3 41.7 %all-to-all-start = ((f32[16,4,128]{2,1,0:T(4,128)}), f32[16,4,128]{2,1,0:T(4,128)S(1)}, u32[]{:S(2)}, u32[]{:S(2)}) async-start(f32[16,4,128]{2,1,0:T(4,128)} %bitcast.2), calls=%async_computation | async-start | bytes 65536 | tf_op jit(solution)/shard_map/all_to_all | solution.py:233
  133.9 4.5 %collective-permute-start.4 = (f32[64,128]{1,0:T(8,128)S(1)}, f32[64,128]{1,0:T(8,128)S(1)}, u32[]{:S(2)}, u32[]{:S(2)}) collective-permute-start(f32[64,128]{1,0:T(8,128)S(1)} %get-tuple-element.14.own), channel_id=1, source_target_pairs={{0,1},{1,2},{2,3},{3,4},{4,5},{5,6},{6,7},{7,8},{8,9},{9,10},{10,1... | collective-permute-start | bytes 98312 | tf_op jit(solution)/shard_map/ppermute | solution.py:229
  136.1 18.4 %collective-permute-start.5 = (f32[64,128]{1,0:T(8,128)S(1)}, f32[64,128]{1,0:T(8,128)S(1)}, u32[]{:S(2)}, u32[]{:S(2)}) collective-permute-start(f32[64,128]{1,0:T(8,128)S(1)} %get-tuple-element.14.own), channel_id=1, source_target_pairs={{1,0},{2,1},{3,2},{4,3},{5,4},{6,5},{7,6},{8,7},{9,8},{10,9},{11,1... | collective-permute-start | bytes 98312 | tf_op jit(solution)/shard_map/ppermute | solution.py:229

commit v4 on v3

--- a/solution.py
+++ b/solution.py
@@ -63,18 +63,18 @@
     return result
 
 
-def pack_kernel(kirchhoff, adjoint, design, y_last, y_first, x_last, x_first):
+def pack_kernel(kirchhoff, adjoint, design, y_last, y_first):
     x_fine, y_fine, _ = kirchhoff.shape
     y_all = design.shape[2]
-    for out, y, x in ((y_last, y_fine - 1, x_fine - 1), (y_first, 0, 0)):
+    for out, y, z in ((y_last, y_fine - 1, ZC - RADIUS), (y_first, 0, 0)):
         for f, field in enumerate((kirchhoff, adjoint)):
             for k in range(x_fine):
-                out[x_fine * f + k : x_fine * f + k + 1, :] = field[k, y : y + 1, :]
+                for h in range(2):
+                    at = 2 * (x_fine * f + k) + h
+                    out[at : at + 1, :] = field[k, y : y + 1, y_all * h : y_all * (h + 1)]
         for k in range(XC):
-            out[2 * x_fine :, y_all * k : y_all * (k + 1)] = design[:, k, :]
-    for out, x in ((x_last, x_fine - 1), (x_first, 0)):
-        out[0] = kirchhoff[x]
-        out[1] = adjoint[x]
+            at = 4 * x_fine + RADIUS * k
+            out[at : at + RADIUS, :] = design[:, k, :][z : z + RADIUS]
 
 
 def restrict_kernel(kirchhoff, adjoint, slope, x_before, x_after, n_before, n_after, out):
@@ -87,9 +87,10 @@
         before = x_before[f] if x == 0 else field[x - 1]
         after = x_after[f] if x == x_fine - 1 else field[x + 1]
         grad_x = after - before
-        at = x_fine * f + x
-        up = jnp.where(row == 0, n_before[at : at + 1, :], pltpu.roll(centre, 1, 0))
-        down = jnp.where(row == y_fine - 1, n_after[at : at + 1, :], pltpu.roll(centre, y_fine - 1, 0))
+        at = 2 * (x_fine * f + x)
+        y_before, y_after = (jnp.concatenate([n[at : at + 1], n[at + 1 : at + 2]], axis=1) for n in (n_before, n_after))
+        up = jnp.where(row == 0, y_before, pltpu.roll(centre, 1, 0))
+        down = jnp.where(row == y_fine - 1, y_after, pltpu.roll(centre, y_fine - 1, 0))
         left = jnp.where(lane == 0, 0.0, pltpu.roll(centre, 1, 1))
         right = jnp.where(lane == z_fine - 1, 0.0, pltpu.roll(centre, z_fine - 1, 1))
         return grad_x, down - up, right - left
@@ -126,13 +127,13 @@
 def design_kernel(design, solid, void, n_before, n_after, out):
     wide = out.shape[0]
     y_all = design.shape[2]
-    skip = n_before.shape[0] - ZC
-    shape = (ZC, 3 * ZC)
-    weights = tri(iota(shape, 1) - iota(shape, 0) - ZC)
+    skip = n_before.shape[0] - XC * RADIUS
+    shape = (ZC, ZC + 2 * RADIUS)
+    weights = tri(iota(shape, 1) - iota(shape, 0) - RADIUS)
     along_z, live = [], []
     for x in range(XC):
-        lanes = slice(y_all * x, y_all * (x + 1))
-        planes = jnp.concatenate([n_before[skip:, lanes], design[:, x, :], n_after[skip:, lanes]], axis=0)
+        rows = slice(skip + RADIUS * x, skip + RADIUS * (x + 1))
+        planes = jnp.concatenate([n_before[rows, :], design[:, x, :], n_after[rows, :]], axis=0)
         along_z += [left_mul(weights, planes)] * YW
         is_live = (1.0 - solid[:, x, :].astype(F32)) * (1.0 - void[:, x, :].astype(F32))
         live += [is_live] * YW
@@ -187,21 +188,47 @@
     return YW * (iota(shape, 0) % wide) + iota(shape, 0) // wide - iota(shape, 1)
 
 
-def density_kernel(density, solid, void, projected):
-    wide, y_all = density.shape[0], projected.shape[2]
+def pack_planes_kernel(got, last, first):
+    rows = got.shape[0] // 4
+    z = iota((rows, LANES), 1) % ZC
+    skip = ZC - RADIUS
+    values = got[:, LANES:]
+    spare = values[3 * rows :]
+    for g in range(3):
+        own, at = values[rows * g : rows * (g + 1)], slice(rows * g, rows * (g + 1))
+        last[at, :] = jnp.where(z >= skip, own, roll_lanes(spare, -skip * (g + 1)))
+        first[at, :] = jnp.where(z < RADIUS, own, roll_lanes(spare, RADIUS - skip * g))
+
+
+def unpack_planes(packed, is_last):
+    rows = packed.shape[0] // 3
+    z = iota((rows, LANES), 1) % ZC
+    skip = ZC - RADIUS
+    values = packed[...]
+    spare = None
+    for g in range(3):
+        shift, start = (skip * (g + 1), skip * (g + 1)) if is_last else (skip * g - RADIUS, skip * g)
+        moved = roll_lanes(values[rows * g : rows * (g + 1)], shift)
+        spare = moved if spare is None else jnp.where((z >= start) & (z < start + skip), moved, spare)
+    return jnp.concatenate([values, spare], axis=0)
+
+
+def density_kernel(got, solid, void, projected):
+    wide, y_all = got.shape[0], projected.shape[2]
     place = (y_steps(wide, y_all) == 0).astype(F32).astype(BF16)
-    for x, lines in enumerate(along_lanes(density[...])):
+    for x, lines in enumerate(along_lanes(got[:, :LANES])):
         is_solid, is_void = solid[:, x, :].astype(F32), void[:, x, :].astype(F32)
         live = (1.0 - is_solid) * (1.0 - is_void)
         projected[:, x, :] = right_mul(lines, place) * live + is_solid * (1.0 - is_void)
 
 
-def sens_kernel(before, own, after, solid, void, sens):
-    wide, y_all = own.shape[0], sens.shape[2]
+def sens_kernel(before, got, after, solid, void, sens):
+    wide, y_all = got.shape[0], sens.shape[2]
     given, made = iota((LANES, LANES), 0), iota((LANES, LANES), 1)
     step = jnp.where(given // ZC == made // ZC, given % ZC - made % ZC, 4 * ZC)
     weights = jnp.concatenate([tri(step - ZC), tri(step), tri(step + ZC)], axis=0)
-    along_z = right_mul(jnp.concatenate([before[...], own[...], after[...]], axis=1), weights)
+    three = [unpack_planes(before, True), got[:, LANES:], unpack_planes(after, False)]
+    along_z = right_mul(jnp.concatenate(three, axis=1), weights)
     weights = tri(y_steps(wide, y_all))
     for x, lines in enumerate(along_lanes(along_z)):
         live = (1.0 - solid[:, x, :].astype(F32)) * (1.0 - void[:, x, :].astype(F32))
@@ -241,21 +268,21 @@
 def per_device(kirchhoff, adjoint, penalty_slope, design, solid_mask, void_mask):
     wide, narrow = lax.axis_size("wide"), lax.axis_size("narrow")
     z_all, y_all = ZC * narrow, design.shape[2]
-    x_fine, y_fine, z_fine = kirchhoff.shape
-
-    n_shape, x_shape = (2 * x_fine + ZC, z_fine), (2, y_fine, z_fine)
-    packed = call(pack_kernel, (n_shape, n_shape, x_shape, x_shape))(kirchhoff, adjoint, design)
-    n_before, n_after = to_sides(packed[0], packed[1], "narrow")
-    x_before, x_after = to_sides(packed[2], packed[3], "wide")
+    x_fine = kirchhoff.shape[0]
+
+    x_last, x_first = (jnp.stack([kirchhoff[x], adjoint[x]]) for x in (x_fine - 1, 0))
+    x_before, x_after = to_sides(x_last, x_first, "wide")
+    packed = (4 * x_fine + XC * RADIUS, y_all)
+    n_before, n_after = to_sides(*call(pack_kernel, (packed, packed))(kirchhoff, adjoint, design), "narrow")
     coarse = call(restrict_kernel, (YW * narrow, LANES))(
         kirchhoff, adjoint, penalty_slope, x_before, x_after, n_before, n_after
     )
+    lines = call(design_kernel, (wide, 2 * LANES))(design, solid_mask, void_mask, n_before, n_after)
+    place = jnp.stack([lax.axis_index("wide"), lax.axis_index("narrow")]).astype(jnp.int32)
+    lines, coarse, place = lax.optimization_barrier((lines, coarse, place))
     coarse = exchange(coarse, "narrow")
-    lines = call(design_kernel, (wide, 2 * LANES))(design, solid_mask, void_mask, n_before, n_after)
     sent = jnp.concatenate([lines, coarse], axis=1)
 
-    place = jnp.stack([lax.axis_index("wide"), lax.axis_index("narrow")]).astype(jnp.int32)
-    place, sent = lax.optimization_barrier((place, sent))
     got = exchange_rows(sent, "wide")
 
     def weigh(*refs):
@@ -263,10 +290,10 @@
 
     sent = call(weigh, (wide, 2 * LANES), smem=(0,))(place, got)
     got = exchange_rows(sent, "wide")
-    weighted = got[:, LANES:]
-    before, after = to_sides(weighted, weighted, "narrow")
-    projected = call(density_kernel, design.shape)(got[:, :LANES], solid_mask, void_mask)
-    sens = call(sens_kernel, design.shape)(before, weighted, after, solid_mask, void_mask)
+    packed = (3 * wide // 4, LANES)
+    before, after = to_sides(*call(pack_planes_kernel, (packed, packed))(got), "narrow")
+    projected = call(density_kernel, design.shape)(got, solid_mask, void_mask)
+    sens = call(sens_kernel, design.shape)(before, got, after, solid_mask, void_mask)
     return projected, sens
 
 

time: 156 us -> 153 us (0.981)
  blocking collectives: 47.5 us -> 87.2 us
  waiting for transfers between devices: 53.7 us -> 30.7 us
  starting transfers between devices: 45.5 us -> 27.4 us
  local copies, waits for them, and re-layouts: 2.88 us -> 1.2 us
    all_to_all x2 -> x3, blocking collectives: 47.5 us -> 87.2 us  [exchange(): return lax.all_to_all(values, axis, split_axis=0, concat_axis=0, tiled=True)]
    all_to_all x1 -> x0, waiting for transfers between devices: 22.8 us -> none  [exchange(): return lax.all_to_all(values, axis, split_axis=0, concat_axis=0, tiled=True)]
    all_to_all x1 -> x0, starting transfers between devices: 18.3 us -> none  [exchange(): return lax.all_to_all(values, axis, split_axis=0, concat_axis=0, tiled=True)]
    ppermute x3, starting transfers between devices: 15 us -> 18.8 us  [to_sides(): lax.ppermute(first, axis, [(j, i) for i, j in up])]
    ppermute x3, starting transfers between devices: 12.2 us -> 8.59 us  [to_sides(): lax.ppermute(last, axis, up)]
    unnamed x16 -> x14, local copies, waits for them, and re-layouts: 2.68 us -> 0.05 us
    pallas_call x6 -> x7, Pallas kernels: 5.25 us -> 4.74 us  [run(): pl.pallas_call(kernel, out_shape=out_shape, in_specs=specs, out_specs=jax...]
  transfers between devices with their start and end apart: 7 -> 6, of which waited for: 3 -> 2; matrix products, arithmetic and copies ran while one was open for 0% -> 0% of each run, Pallas kernels for 1% -> 1%
where the time goes in v4:
time: 153 us; the launch traced here: 152 us
  blocking collectives  87.2 us (57%)
  waiting for transfers between devices  30.7 us (20%)
  starting transfers between devices  27.4 us (18%)
  Pallas kernels  4.74 us (3%)
    all_to_all x3, blocking collectives, exchange(): return lax.all_to_all(values, axis, split_axis=0, concat_axis=0, tiled=True)  87.2 us
    ppermute x3, waiting for transfers between devices, to_sides(): lax.ppermute(first, axis, [(j, i) for i, j in up])  30.7 us
    ppermute x3, starting transfers between devices, to_sides(): lax.ppermute(first, axis, [(j, i) for i, j in up])  18.8 us
    ppermute x3, starting transfers between devices, to_sides(): lax.ppermute(last, axis, up)  8.59 us
    pallas_call x7, Pallas kernels, run(): pl.pallas_call(kernel, out_shape=out_shape, in_specs=specs, out_specs=jax...  4.74 us
  transfers between devices with their start and end apart: 6, of which 2 were waited for; matrix products, arithmetic and copies ran while one was open for 0% of the time, Pallas kernels for 1%

profile of v4, /device:TPU:1, one launch (start us, length us, event | category | flops | bytes accessed | tf_op | source)
XLA Modules:
  0.0 152.2 jit_solution(10271924441037138053)
XLA Ops:
  0.6 0.0 copy-start.4
  0.6 1.0 fusion
  1.6 0.0 copy-start
  1.6 0.0 copy-start.1
  1.6 16.2 %collective-permute-start.3 = (f32[2,32,512]{2,1,0:T(8,128)S(1)}, f32[2,32,512]{2,1,0:T(8,128)S(1)}, u32[]{:S(2)}, u32[]{:S(2)}) collective-permute-start(f32[2,32,512]{2,1,0:T(8,128)S(1)} %pad_maximum_fusion.1), channel_id=1, source_target_pairs={{16,0},{32,16},{48,32},{64,48},{80,64},{96,80},{112,96},{128,112},... | collective-permute-start | bytes 393224 | tf_op jit(solution)/shard_map/ppermute | solution.py:256
  17.9 1.9 %collective-permute-start.2 = (f32[2,32,512]{2,1,0:T(8,128)S(1)}, f32[2,32,512]{2,1,0:T(8,128)S(1)}, u32[]{:S(2)}, u32[]{:S(2)}) collective-permute-start(f32[2,32,512]{2,1,0:T(8,128)S(1)} %pad_maximum_fusion), channel_id=1, source_target_pairs={{0,16},{16,32},{32,48},{48,64},{64,80},{80,96},{96,112},{112,128},... | collective-permute-start | bytes 393224 | tf_op jit(solution)/shard_map/ppermute | solution.py:256
  19.8 0.0 copy-done.4
  19.8 0.0 copy-done
  19.8 0.0 copy-done.1
  19.8 0.0 copy-start.2
  19.8 0.0 copy-start.3
  19.9 4.3 %collective-permute-start = (f32[40,256]{1,0:T(8,128)S(1)}, f32[40,256]{1,0:T(8,128)S(1)}, u32[]{:S(2)}, u32[]{:S(2)}) collective-permute-start(f32[40,256]{1,0:T(8,128)S(1)} %get-tuple-element.9), channel_id=1, source_target_pairs={{0,1},{1,2},{2,3},{3,4},{4,5},{5,6},{6,7},{7,8},{8,9},{9,10},{10,1... | collective-permute-start | bytes 122888 | tf_op jit(solution)/shard_map/ppermute | solution.py:256
  24.2 1.3 collective-permute-start.1
  25.5 0.0 copy-start.5
  25.5 0.1 pad_add_fusion.refs_0_
  25.6 0.0 collective-permute-done.n_before
  25.6 16.0 %collective-permute-done.1.n_after = f32[40,256]{1,0:T(8,128)S(1)} collective-permute-done((f32[40,256]{1,0:T(8,128)S(1)}, f32[40,256]{1,0:T(8,128)S(1)}, u32[]{:S(2)}, u32[]{:S(2)}) %collective-permute-start.1) | collective-permute-done | bytes 40992 | tf_op jit(solution)/shard_map/ppermute | solution.py:256
  41.6 0.0 copy-done.2
  41.6 0.0 copy-done.3
  41.6 0.5 shard_map.78
  42.1 0.0 collective-permute-done.3.x_after
  42.1 0.0 collective-permute-done.2.x_before
  42.1 0.0 copy-done.5
  42.1 0.9 shard_map.79
  43.0 45.5 %all_to_all.22 = f32[16,4,128]{2,1,0:T(4,128)S(1)} all-to-all(f32[16,4,128]{2,1,0:T(4,128)S(1)} %bitcast.18), channel_id=1, replica_groups=mesh['wide'=64,'narrow'=16] {'narrow'}, dimensions={0} | all-to-all | bytes 65536 | tf_op jit(solution)/shard_map/all_to_all | solution.py:260
  88.5 0.1 copy.8
  88.6 23.4 %all_to_all.23 = f32[64,1,384]{2,1,0:T(1,128)S(1)} all-to-all(f32[64,1,384]{2,1,0:T(1,128)S(1)} %copy.8), channel_id=1, replica_groups=mesh['wide'=64,'narrow'=16] {'wide'}, dimensions={0} | all-to-all | bytes 196608 | tf_op jit(solution)/shard_map/all_to_all | solution.py:260
  112.0 1.1 shard_map.80
  113.1 0.1 copy.9
  113.2 18.3 %all_to_all.24 = f32[64,1,256]{2,1,0:T(1,128)S(1)} all-to-all(f32[64,1,256]{2,1,0:T(1,128)S(1)} %copy.9), channel_id=1, replica_groups=mesh['wide'=64,'narrow'=16] {'wide'}, dimensions={0} | all-to-all | bytes 131072 | tf_op jit(solution)/shard_map/all_to_all | solution.py:260
  131.5 0.1 shard_map.82
  131.6 2.4 %collective-permute-start.4 = (f32[48,128]{1,0:T(8,128)S(1)}, f32[48,128]{1,0:T(8,128)S(1)}, u32[]{:S(2)}, u32[]{:S(2)}) collective-permute-start(f32[48,128]{1,0:T(8,128)S(1)} %get-tuple-element.14), channel_id=1, source_target_pairs={{0,1},{1,2},{2,3},{3,4},{4,5},{5,6},{6,7},{7,8},{8,9},{9,10},{10,1... | collective-permute-start | bytes 73736 | tf_op jit(solution)/shard_map/ppermute | solution.py:256
  134.0 1.3 collective-permute-start.5
  135.3 1.0 shard_map.81
  136.2 0.0 collective-permute-done.4.before
  136.2 14.7 %collective-permute-done.5.after = f32[48,128]{1,0:T(8,128)S(1)} collective-permute-done((f32[48,128]{1,0:T(8,128)S(1)}, f32[48,128]{1,0:T(8,128)S(1)}, u32[]{:S(2)}, u32[]{:S(2)}) %collective-permute-start.5) | collective-permute-done | bytes 24608 | tf_op jit(solution)/shard_map/ppermute | solution.py:256
  151.0 1.2 shard_map.83
  (6 shorter events, 0.1 us)
Async XLA Ops:
  0.6 19.2 %copy-start.4 = (f32[16,2,256]{2,1,0:T(2,128)S(1)}, f32[16,2,256]{2,1,0:T(2,128)}, u32[]{:S(2)}) copy-start(f32[16,2,256]{2,1,0:T(2,128)} %design.3) | copy-start | bytes 98308
  1.6 18.2 %copy-start = (f32[4,32,512]{2,1,0:T(8,128)S(1)}, f32[4,32,512]{2,1,0:T(8,128)}, u32[]{:S(2)}) copy-start(f32[4,32,512]{2,1,0:T(8,128)} %kirchhoff.3) | copy-start | bytes 786436
  1.6 18.2 %copy-start.1 = (f32[4,32,512]{2,1,0:T(8,128)S(1)}, f32[4,32,512]{2,1,0:T(8,128)}, u32[]{:S(2)}) copy-start(f32[4,32,512]{2,1,0:T(8,128)} %adjoint.3) | copy-start | bytes 786436
  1.6 40.5 %collective-permute-start.3 = (f32[2,32,512]{2,1,0:T(8,128)S(1)}, f32[2,32,512]{2,1,0:T(8,128)S(1)}, u32[]{:S(2)}, u32[]{:S(2)}) collective-permute-start(f32[2,32,512]{2,1,0:T(8,128)S(1)} %pad_maximum_fusion.1), channel_id=1, source_target_pairs={{16,0},{32,16},{48,32},{64,48},{80,64},{96,80},{112,96},{128,112},... | collective-permute-start | bytes 393224 | tf_op jit(solution)/shard_map/ppermute | solution.py:256
  17.9 24.2 %collective-permute-start.2 = (f32[2,32,512]{2,1,0:T(8,128)S(1)}, f32[2,32,512]{2,1,0:T(8,128)S(1)}, u32[]{:S(2)}, u32[]{:S(2)}) collective-permute-start(f32[2,32,512]{2,1,0:T(8,128)S(1)} %pad_maximum_fusion), channel_id=1, source_target_pairs={{0,16},{16,32},{32,48},{48,64},{64,80},{80,96},{96,112},{112,128},... | collective-permute-start | bytes 393224 | tf_op jit(solution)/shard_map/ppermute | solution.py:256
  19.8 21.8 %copy-start.2 = (s32[16,2,256]{2,1,0:T(2,128)S(1)}, s32[16,2,256]{2,1,0:T(2,128)}, u32[]{:S(2)}) copy-start(s32[16,2,256]{2,1,0:T(2,128)} %solid.5) | copy-start | bytes 98308
  19.8 21.8 %copy-start.3 = (s32[16,2,256]{2,1,0:T(2,128)S(1)}, s32[16,2,256]{2,1,0:T(2,128)}, u32[]{:S(2)}) copy-start(s32[16,2,256]{2,1,0:T(2,128)} %void.5) | copy-start | bytes 98308
  19.9 5.7 %collective-permute-start = (f32[40,256]{1,0:T(8,128)S(1)}, f32[40,256]{1,0:T(8,128)S(1)}, u32[]{:S(2)}, u32[]{:S(2)}) collective-permute-start(f32[40,256]{1,0:T(8,128)S(1)} %get-tuple-element.9), channel_id=1, source_target_pairs={{0,1},{1,2},{2,3},{3,4},{4,5},{5,6},{6,7},{7,8},{8,9},{9,10},{10,1... | collective-permute-start | bytes 122888 | tf_op jit(solution)/shard_map/ppermute | solution.py:256
  24.2 17.4 %collective-permute-start.1 = (f32[40,256]{1,0:T(8,128)S(1)}, f32[40,256]{1,0:T(8,128)S(1)}, u32[]{:S(2)}, u32[]{:S(2)}) collective-permute-start(f32[40,256]{1,0:T(8,128)S(1)} %get-tuple-element.10), channel_id=1, source_target_pairs={{1,0},{2,1},{3,2},{4,3},{5,4},{6,5},{7,6},{8,7},{9,8},{10,9},{11,1... | collective-permute-start | bytes 122888 | tf_op jit(solution)/shard_map/ppermute | solution.py:256
  25.5 16.6 %copy-start.5 = (bf16[4,32,512]{2,1,0:T(8,128)(2,1)S(1)}, bf16[4,32,512]{2,1,0:T(8,128)(2,1)}, u32[]{:S(2)}) copy-start(bf16[4,32,512]{2,1,0:T(8,128)(2,1)} %slope.1) | copy-start | bytes 393220
  131.6 4.6 %collective-permute-start.4 = (f32[48,128]{1,0:T(8,128)S(1)}, f32[48,128]{1,0:T(8,128)S(1)}, u32[]{:S(2)}, u32[]{:S(2)}) collective-permute-start(f32[48,128]{1,0:T(8,128)S(1)} %get-tuple-element.14), channel_id=1, source_target_pairs={{0,1},{1,2},{2,3},{3,4},{4,5},{5,6},{6,7},{7,8},{8,9},{9,10},{10,1... | collective-permute-start | bytes 73736 | tf_op jit(solution)/shard_map/ppermute | solution.py:256
  134.0 17.0 %collective-permute-start.5 = (f32[48,128]{1,0:T(8,128)S(1)}, f32[48,128]{1,0:T(8,128)S(1)}, u32[]{:S(2)}, u32[]{:S(2)}) collective-permute-start(f32[48,128]{1,0:T(8,128)S(1)} %get-tuple-element.15), channel_id=1, source_target_pairs={{1,0},{2,1},{3,2},{4,3},{5,4},{6,5},{7,6},{8,7},{9,8},{10,9},{11,1... | collective-permute-start | bytes 73736 | tf_op jit(solution)/shard_map/ppermute | solution.py:256

commit v5 on v4

--- a/solution.py
+++ b/solution.py
@@ -63,32 +63,50 @@
     return result
 
 
-def pack_kernel(kirchhoff, adjoint, design, y_last, y_first):
+def is_even(axis):
+    return lax.rem(lax.axis_index(axis), 2) == 0
+
+
+def by_side(even, of_first, of_second):
+    return jnp.where(even, of_second, of_first), jnp.where(even, of_first, of_second)
+
+
+def pack_kernel(kirchhoff, adjoint, design, to_first, to_second):
+    even = is_even("narrow")
     x_fine, y_fine, _ = kirchhoff.shape
     y_all = design.shape[2]
-    for out, y, z in ((y_last, y_fine - 1, ZC - RADIUS), (y_first, 0, 0)):
-        for f, field in enumerate((kirchhoff, adjoint)):
-            for k in range(x_fine):
-                for h in range(2):
-                    at = 2 * (x_fine * f + k) + h
-                    out[at : at + 1, :] = field[k, y : y + 1, y_all * h : y_all * (h + 1)]
-        for k in range(XC):
-            at = 4 * x_fine + RADIUS * k
-            out[at : at + RADIUS, :] = design[:, k, :][z : z + RADIUS]
-
-
-def restrict_kernel(kirchhoff, adjoint, slope, x_before, x_after, n_before, n_after, out):
+
+    def put(rows, before, after):
+        to_first[rows, :] = jnp.where(even, after, before)
+        to_second[rows, :] = jnp.where(even, before, after)
+
+    for f, field in enumerate((kirchhoff, adjoint)):
+        for k in range(x_fine):
+            for h in range(2):
+                at, lanes = 2 * (x_fine * f + k) + h, slice(y_all * h, y_all * (h + 1))
+                put(slice(at, at + 1), field[k, 0:1, lanes], field[k, y_fine - 1 : y_fine, lanes])
+    for k in range(XC):
+        at = 4 * x_fine + RADIUS * k
+        planes = design[:, k, :]
+        put(slice(at, at + RADIUS), planes[:RADIUS], planes[ZC - RADIUS :])
+
+
+def restrict_kernel(kirchhoff, adjoint, slope, x_first, x_second, n_first, n_second, out):
     x_fine, y_fine, z_fine = kirchhoff.shape
     row = iota((y_fine, z_fine), 0)
     lane = iota((y_fine, z_fine), 1)
+    x_even, n_even = is_even("wide"), is_even("narrow")
 
     def diffs(f, field, x):
         centre = field[x]
-        before = x_before[f] if x == 0 else field[x - 1]
-        after = x_after[f] if x == x_fine - 1 else field[x + 1]
+        x_before, x_after = by_side(x_even, x_first[f], x_second[f])
+        before = x_before if x == 0 else field[x - 1]
+        after = x_after if x == x_fine - 1 else field[x + 1]
         grad_x = after - before
         at = 2 * (x_fine * f + x)
-        y_before, y_after = (jnp.concatenate([n[at : at + 1], n[at + 1 : at + 2]], axis=1) for n in (n_before, n_after))
+        y_before, y_after = by_side(
+            n_even, *(jnp.concatenate([n[at : at + 1], n[at + 1 : at + 2]], axis=1) for n in (n_first, n_second))
+        )
         up = jnp.where(row == 0, y_before, pltpu.roll(centre, 1, 0))
         down = jnp.where(row == y_fine - 1, y_after, pltpu.roll(centre, y_fine - 1, 0))
         left = jnp.where(lane == 0, 0.0, pltpu.roll(centre, 1, 1))
@@ -124,16 +142,17 @@
     return made
 
 
-def design_kernel(design, solid, void, n_before, n_after, out):
+def design_kernel(design, solid, void, n_first, n_second, out):
     wide = out.shape[0]
     y_all = design.shape[2]
-    skip = n_before.shape[0] - XC * RADIUS
+    skip = n_first.shape[0] - XC * RADIUS
     shape = (ZC, ZC + 2 * RADIUS)
     weights = tri(iota(shape, 1) - iota(shape, 0) - RADIUS)
     along_z, live = [], []
     for x in range(XC):
         rows = slice(skip + RADIUS * x, skip + RADIUS * (x + 1))
-        planes = jnp.concatenate([n_before[rows, :], design[:, x, :], n_after[rows, :]], axis=0)
+        before, after = by_side(is_even("narrow"), n_first[rows, :], n_second[rows, :])
+        planes = jnp.concatenate([before, design[:, x, :], after], axis=0)
         along_z += [left_mul(weights, planes)] * YW
         is_live = (1.0 - solid[:, x, :].astype(F32)) * (1.0 - void[:, x, :].astype(F32))
         live += [is_live] * YW
@@ -188,23 +207,26 @@
     return YW * (iota(shape, 0) % wide) + iota(shape, 0) // wide - iota(shape, 1)
 
 
-def pack_planes_kernel(got, last, first):
+def pack_planes_kernel(got, to_first, to_second):
     rows = got.shape[0] // 4
     z = iota((rows, LANES), 1) % ZC
     skip = ZC - RADIUS
+    even = is_even("narrow")
     values = got[:, LANES:]
     spare = values[3 * rows :]
     for g in range(3):
         own, at = values[rows * g : rows * (g + 1)], slice(rows * g, rows * (g + 1))
-        last[at, :] = jnp.where(z >= skip, own, roll_lanes(spare, -skip * (g + 1)))
-        first[at, :] = jnp.where(z < RADIUS, own, roll_lanes(spare, RADIUS - skip * g))
+        after = jnp.where(z >= skip, own, roll_lanes(spare, -skip * (g + 1)))
+        before = jnp.where(z < RADIUS, own, roll_lanes(spare, RADIUS - skip * g))
+        to_first[at, :] = jnp.where(even, after, before)
+        to_second[at, :] = jnp.where(even, before, after)
 
 
 def unpack_planes(packed, is_last):
     rows = packed.shape[0] // 3
     z = iota((rows, LANES), 1) % ZC
     skip = ZC - RADIUS
-    values = packed[...]
+    values = packed
     spare = None
     for g in range(3):
         shift, start = (skip * (g + 1), skip * (g + 1)) if is_last else (skip * g - RADIUS, skip * g)
@@ -222,7 +244,8 @@
         projected[:, x, :] = right_mul(lines, place) * live + is_solid * (1.0 - is_void)
 
 
-def sens_kernel(before, got, after, solid, void, sens):
+def sens_kernel(first, got, second, solid, void, sens):
+    before, after = by_side(is_even("narrow"), first[...], second[...])
     wide, y_all = got.shape[0], sens.shape[2]
     given, made = iota((LANES, LANES), 0), iota((LANES, LANES), 1)
     step = jnp.where(given // ZC == made // ZC, given % ZC - made % ZC, 4 * ZC)
@@ -251,9 +274,11 @@
     return run
 
 
-def to_sides(last, first, axis):
-    up = [(i, i + 1) for i in range(lax.axis_size(axis) - 1)]
-    return lax.ppermute(last, axis, up), lax.ppermute(first, axis, [(j, i) for i, j in up])
+def swap(to_first, to_second, axis):
+    count = lax.axis_size(axis)
+    pairs = [[(i, i + 1) for i in range(start, count - 1, 2)] for start in (0, 1)]
+    both = [[*p, *((j, i) for i, j in p)] for p in pairs]
+    return lax.ppermute(to_first, axis, both[0]), lax.ppermute(to_second, axis, both[1])
 
 
 def exchange(values, axis):
@@ -270,14 +295,15 @@
     z_all, y_all = ZC * narrow, design.shape[2]
     x_fine = kirchhoff.shape[0]
 
-    x_last, x_first = (jnp.stack([kirchhoff[x], adjoint[x]]) for x in (x_fine - 1, 0))
-    x_before, x_after = to_sides(x_last, x_first, "wide")
+    sides = [jnp.stack([kirchhoff[x], adjoint[x]]) for x in (0, x_fine - 1)]
+    even = is_even("wide")
+    x_first, x_second = swap(jnp.where(even, sides[1], sides[0]), jnp.where(even, sides[0], sides[1]), "wide")
     packed = (4 * x_fine + XC * RADIUS, y_all)
-    n_before, n_after = to_sides(*call(pack_kernel, (packed, packed))(kirchhoff, adjoint, design), "narrow")
+    n_first, n_second = swap(*call(pack_kernel, (packed, packed))(kirchhoff, adjoint, design), "narrow")
     coarse = call(restrict_kernel, (YW * narrow, LANES))(
-        kirchhoff, adjoint, penalty_slope, x_before, x_after, n_before, n_after
+        kirchhoff, adjoint, penalty_slope, x_first, x_second, n_first, n_second
     )
-    lines = call(design_kernel, (wide, 2 * LANES))(design, solid_mask, void_mask, n_before, n_after)
+    lines = call(design_kernel, (wide, 2 * LANES))(design, solid_mask, void_mask, n_first, n_second)
     place = jnp.stack([lax.axis_index("wide"), lax.axis_index("narrow")]).astype(jnp.int32)
     lines, coarse, place = lax.optimization_barrier((lines, coarse, place))
     coarse = exchange(coarse, "narrow")
@@ -291,9 +317,9 @@
     sent = call(weigh, (wide, 2 * LANES), smem=(0,))(place, got)
     got = exchange_rows(sent, "wide")
     packed = (3 * wide // 4, LANES)
-    before, after = to_sides(*call(pack_planes_kernel, (packed, packed))(got), "narrow")
+    first, second = swap(*call(pack_planes_kernel, (packed, packed))(got), "narrow")
     projected = call(density_kernel, design.shape)(got, solid_mask, void_mask)
-    sens = call(sens_kernel, design.shape)(before, got, after, solid_mask, void_mask)
+    sens = call(sens_kernel, design.shape)(first, got, second, solid_mask, void_mask)
     return projected, sens
 
 

time: 153 us -> 150 us (0.980)
  waiting for transfers between devices: 30.7 us -> 21.8 us
  blocking collectives: 87.2 us -> 95 us
    ppermute x6, waiting for transfers between devices: 30.7 us -> 21.8 us  [the longest x3 21.7 us: swap(): lax.ppermute(to_first, axis, both[0])]
    all_to_all x3, blocking collectives: 87.2 us -> 95 us  [exchange(): return lax.all_to_all(values, axis, split_axis=0, concat_axis=0, tiled=True)]
where the time goes in v5:
time: 150 us
  blocking collectives  95 us (63%)
  starting transfers between devices  26.3 us (18%)
  waiting for transfers between devices  21.8 us (15%)
  Pallas kernels  4.78 us (3%)
    all_to_all x3, blocking collectives, exchange(): return lax.all_to_all(values, axis, split_axis=0, concat_axis=0, tiled=True)  95 us
    ppermute x3, starting transfers between devices, swap(): lax.ppermute(to_first, axis, both[0])  23 us
    ppermute x3, waiting for transfers between devices, swap(): lax.ppermute(to_first, axis, both[0])  21.7 us
    pallas_call x7, Pallas kernels, run(): pl.pallas_call(kernel, out_shape=out_shape, in_specs=specs, out_specs=jax...  4.78 us
    ppermute x3, starting transfers between devices, swap(): lax.ppermute(to_second, axis, both[1])  3.25 us
  transfers between devices with their start and end apart: 6, of which 2 were waited for; matrix products, arithmetic and copies ran while one was open for 0% of the time, Pallas kernels for 1%

profile of v5, /device:TPU:1, one launch (start us, length us, event | category | flops | bytes accessed | tf_op | source)
XLA Modules:
  0.0 150.0 jit_solution(14660433624191508343)
XLA Ops:
  0.6 0.0 copy-start.4
  0.6 1.0 fusion.2
  1.6 0.0 copy-start
  1.6 0.0 copy-start.1
  1.7 16.2 %collective-permute-start.2 = (f32[2,32,512]{2,1,0:T(8,128)S(1)}, f32[2,32,512]{2,1,0:T(8,128)S(1)}, u32[]{:S(2)}, u32[]{:S(2)}) collective-permute-start(f32[2,32,512]{2,1,0:T(8,128)S(1)} %get-tuple-element.17), channel_id=1, source_target_pairs={{0,16},{32,48},{64,80},{96,112},{128,144},{160,176},{192,208},{224... | collective-permute-start | bytes 393224 | tf_op jit(solution)/shard_map/ppermute | solution.py:281
  17.9 1.9 %collective-permute-start.3 = (f32[2,32,512]{2,1,0:T(8,128)S(1)}, f32[2,32,512]{2,1,0:T(8,128)S(1)}, u32[]{:S(2)}, u32[]{:S(2)}) collective-permute-start(f32[2,32,512]{2,1,0:T(8,128)S(1)} %get-tuple-element.16), channel_id=1, source_target_pairs={{16,32},{48,64},{80,96},{112,128},{144,160},{176,192},{208,224},{2... | collective-permute-start | bytes 393224 | tf_op jit(solution)/shard_map/ppermute | solution.py:281
  19.8 0.0 copy-done.4
  19.8 0.0 copy-done
  19.8 0.0 copy-done.1
  19.8 0.0 copy-start.2
  19.8 0.0 copy-start.3
  19.9 0.0 copy-start.5
  19.9 4.4 %collective-permute-start = (f32[40,256]{1,0:T(8,128)S(1)}, f32[40,256]{1,0:T(8,128)S(1)}, u32[]{:S(2)}, u32[]{:S(2)}) collective-permute-start(f32[40,256]{1,0:T(8,128)S(1)} %get-tuple-element.9), channel_id=1, source_target_pairs={{0,1},{2,3},{4,5},{6,7},{8,9},{10,11},{12,13},{14,15},{1,0},{3,2},... | collective-permute-start | bytes 122888 | tf_op jit(solution)/shard_map/ppermute | solution.py:281
  24.4 0.7 collective-permute-start.1
  25.0 0.1 pad_add_fusion.refs_0_
  25.1 8.8 %collective-permute-done.n_first = f32[40,256]{1,0:T(8,128)S(1)} collective-permute-done((f32[40,256]{1,0:T(8,128)S(1)}, f32[40,256]{1,0:T(8,128)S(1)}, u32[]{:S(2)}, u32[]{:S(2)}) %collective-permute-start) | collective-permute-done | bytes 40992 | tf_op jit(solution)/shard_map/ppermute | solution.py:281
  33.9 0.0 collective-permute-done.1.n_second
  33.9 0.0 copy-done.2
  33.9 0.0 copy-done.3
  33.9 0.5 shard_map.78
  34.4 0.0 collective-permute-done.2.x_first
  34.4 0.0 collective-permute-done.3.x_second
  34.4 0.0 copy-done.5
  34.4 0.9 shard_map.79
  35.3 47.8 %all_to_all.22 = f32[16,4,128]{2,1,0:T(4,128)S(1)} all-to-all(f32[16,4,128]{2,1,0:T(4,128)S(1)} %bitcast.18), channel_id=1, replica_groups=mesh['wide'=64,'narrow'=16] {'narrow'}, dimensions={0} | all-to-all | bytes 65536 | tf_op jit(solution)/shard_map/all_to_all | solution.py:285
  83.1 0.1 copy.8
  83.2 28.9 %all_to_all.23 = f32[64,1,384]{2,1,0:T(1,128)S(1)} all-to-all(f32[64,1,384]{2,1,0:T(1,128)S(1)} %copy.8), channel_id=1, replica_groups=mesh['wide'=64,'narrow'=16] {'wide'}, dimensions={0} | all-to-all | bytes 196608 | tf_op jit(solution)/shard_map/all_to_all | solution.py:285
  112.1 1.1 shard_map.80
  113.2 0.1 copy.9
  113.3 18.3 %all_to_all.24 = f32[64,1,256]{2,1,0:T(1,128)S(1)} all-to-all(f32[64,1,256]{2,1,0:T(1,128)S(1)} %copy.9), channel_id=1, replica_groups=mesh['wide'=64,'narrow'=16] {'wide'}, dimensions={0} | all-to-all | bytes 131072 | tf_op jit(solution)/shard_map/all_to_all | solution.py:285
  131.6 0.1 shard_map.82
  131.7 2.4 %collective-permute-start.4 = (f32[48,128]{1,0:T(8,128)S(1)}, f32[48,128]{1,0:T(8,128)S(1)}, u32[]{:S(2)}, u32[]{:S(2)}) collective-permute-start(f32[48,128]{1,0:T(8,128)S(1)} %get-tuple-element.14), channel_id=1, source_target_pairs={{0,1},{2,3},{4,5},{6,7},{8,9},{10,11},{12,13},{14,15},{1,0},{3,2},... | collective-permute-start | bytes 73736 | tf_op jit(solution)/shard_map/ppermute | solution.py:281
  134.1 0.7 collective-permute-start.5
  134.8 1.0 shard_map.81
  135.7 13.0 %collective-permute-done.4.first = f32[48,128]{1,0:T(8,128)S(1)} collective-permute-done((f32[48,128]{1,0:T(8,128)S(1)}, f32[48,128]{1,0:T(8,128)S(1)}, u32[]{:S(2)}, u32[]{:S(2)}) %collective-permute-start.4) | collective-permute-done | bytes 24608 | tf_op jit(solution)/shard_map/ppermute | solution.py:281
  148.7 0.0 collective-permute-done.5.second
  148.7 1.2 shard_map.83
  (5 shorter events, 0.1 us)
Async XLA Ops:
  0.6 19.2 %copy-start.4 = (f32[16,2,256]{2,1,0:T(2,128)S(1)}, f32[16,2,256]{2,1,0:T(2,128)}, u32[]{:S(2)}) copy-start(f32[16,2,256]{2,1,0:T(2,128)} %design.3) | copy-start | bytes 98308
  1.6 18.2 %copy-start = (f32[4,32,512]{2,1,0:T(8,128)S(1)}, f32[4,32,512]{2,1,0:T(8,128)}, u32[]{:S(2)}) copy-start(f32[4,32,512]{2,1,0:T(8,128)} %kirchhoff.3) | copy-start | bytes 786436
  1.6 18.2 %copy-start.1 = (f32[4,32,512]{2,1,0:T(8,128)S(1)}, f32[4,32,512]{2,1,0:T(8,128)}, u32[]{:S(2)}) copy-start(f32[4,32,512]{2,1,0:T(8,128)} %adjoint.3) | copy-start | bytes 786436
  1.7 32.7 %collective-permute-start.2 = (f32[2,32,512]{2,1,0:T(8,128)S(1)}, f32[2,32,512]{2,1,0:T(8,128)S(1)}, u32[]{:S(2)}, u32[]{:S(2)}) collective-permute-start(f32[2,32,512]{2,1,0:T(8,128)S(1)} %get-tuple-element.17), channel_id=1, source_target_pairs={{0,16},{32,48},{64,80},{96,112},{128,144},{160,176},{192,208},{224... | collective-permute-start | bytes 393224 | tf_op jit(solution)/shard_map/ppermute | solution.py:281
  17.9 16.5 %collective-permute-start.3 = (f32[2,32,512]{2,1,0:T(8,128)S(1)}, f32[2,32,512]{2,1,0:T(8,128)S(1)}, u32[]{:S(2)}, u32[]{:S(2)}) collective-permute-start(f32[2,32,512]{2,1,0:T(8,128)S(1)} %get-tuple-element.16), channel_id=1, source_target_pairs={{16,32},{48,64},{80,96},{112,128},{144,160},{176,192},{208,224},{2... | collective-permute-start | bytes 393224 | tf_op jit(solution)/shard_map/ppermute | solution.py:281
  19.8 14.1 %copy-start.2 = (s32[16,2,256]{2,1,0:T(2,128)S(1)}, s32[16,2,256]{2,1,0:T(2,128)}, u32[]{:S(2)}) copy-start(s32[16,2,256]{2,1,0:T(2,128)} %solid.5) | copy-start | bytes 98308
  19.8 14.1 %copy-start.3 = (s32[16,2,256]{2,1,0:T(2,128)S(1)}, s32[16,2,256]{2,1,0:T(2,128)}, u32[]{:S(2)}) copy-start(s32[16,2,256]{2,1,0:T(2,128)} %void.5) | copy-start | bytes 98308
  19.9 14.5 %copy-start.5 = (bf16[4,32,512]{2,1,0:T(8,128)(2,1)S(1)}, bf16[4,32,512]{2,1,0:T(8,128)(2,1)}, u32[]{:S(2)}) copy-start(bf16[4,32,512]{2,1,0:T(8,128)(2,1)} %slope.1) | copy-start | bytes 393220
  19.9 14.0 %collective-permute-start = (f32[40,256]{1,0:T(8,128)S(1)}, f32[40,256]{1,0:T(8,128)S(1)}, u32[]{:S(2)}, u32[]{:S(2)}) collective-permute-start(f32[40,256]{1,0:T(8,128)S(1)} %get-tuple-element.9), channel_id=1, source_target_pairs={{0,1},{2,3},{4,5},{6,7},{8,9},{10,11},{12,13},{14,15},{1,0},{3,2},... | collective-permute-start | bytes 122888 | tf_op jit(solution)/shard_map/ppermute | solution.py:281
  24.4 9.5 %collective-permute-start.1 = (f32[40,256]{1,0:T(8,128)S(1)}, f32[40,256]{1,0:T(8,128)S(1)}, u32[]{:S(2)}, u32[]{:S(2)}) collective-permute-start(f32[40,256]{1,0:T(8,128)S(1)} %get-tuple-element.10), channel_id=1, source_target_pairs={{1,2},{3,4},{5,6},{7,8},{9,10},{11,12},{13,14},{2,1},{4,3},{6,5},{... | collective-permute-start | bytes 122888 | tf_op jit(solution)/shard_map/ppermute | solution.py:281
  131.7 17.0 %collective-permute-start.4 = (f32[48,128]{1,0:T(8,128)S(1)}, f32[48,128]{1,0:T(8,128)S(1)}, u32[]{:S(2)}, u32[]{:S(2)}) collective-permute-start(f32[48,128]{1,0:T(8,128)S(1)} %get-tuple-element.14), channel_id=1, source_target_pairs={{0,1},{2,3},{4,5},{6,7},{8,9},{10,11},{12,13},{14,15},{1,0},{3,2},... | collective-permute-start | bytes 73736 | tf_op jit(solution)/shard_map/ppermute | solution.py:281
  134.1 14.6 %collective-permute-start.5 = (f32[48,128]{1,0:T(8,128)S(1)}, f32[48,128]{1,0:T(8,128)S(1)}, u32[]{:S(2)}, u32[]{:S(2)}) collective-permute-start(f32[48,128]{1,0:T(8,128)S(1)} %get-tuple-element.15), channel_id=1, source_target_pairs={{1,2},{3,4},{5,6},{7,8},{9,10},{11,12},{13,14},{2,1},{4,3},{6,5},{... | collective-permute-start | bytes 73736 | tf_op jit(solution)/shard_map/ppermute | solution.py:281

commit v6 on v5

--- a/solution.py
+++ b/solution.py
@@ -192,7 +192,7 @@
     inner = jnp.tanh(BETA * (filtered - ETA))
     out[:, :LANES] = (LOWER_TANH + inner) / SPAN_TANH
     slope = BETA * (1.0 - inner * inner) / SPAN_TANH
-    weighted = slope * got[:, 2 * LANES :] * got[:, LANES : 2 * LANES] / normalizer
+    weighted = slope * got[:, LANES:] / normalizer
     out[:, LANES:] = along_x(weighted)
 
 
@@ -307,7 +307,7 @@
     place = jnp.stack([lax.axis_index("wide"), lax.axis_index("narrow")]).astype(jnp.int32)
     lines, coarse, place = lax.optimization_barrier((lines, coarse, place))
     coarse = exchange(coarse, "narrow")
-    sent = jnp.concatenate([lines, coarse], axis=1)
+    sent = jnp.concatenate([lines[:, :LANES], lines[:, LANES:] * coarse], axis=1)
 
     got = exchange_rows(sent, "wide")
 

time: 150 us -> 149 us (level)
  no operation moved by 1% of the time
where the time goes in v6:
time: 149 us
  blocking collectives  93.6 us (63%)
  starting transfers between devices  26.3 us (18%)
  waiting for transfers between devices  21.8 us (15%)
  Pallas kernels  4.78 us (3%)
    all_to_all x3, blocking collectives, exchange(): return lax.all_to_all(values, axis, split_axis=0, concat_axis=0, tiled=True)  93.6 us
    ppermute x3, starting transfers between devices, swap(): lax.ppermute(to_first, axis, both[0])  23 us
    ppermute x3, waiting for transfers between devices, swap(): lax.ppermute(to_first, axis, both[0])  21.7 us
    pallas_call x7, Pallas kernels, run(): pl.pallas_call(kernel, out_shape=out_shape, in_specs=specs, out_specs=jax...  4.78 us
    ppermute x3, starting transfers between devices, swap(): lax.ppermute(to_second, axis, both[1])  3.25 us
  transfers between devices with their start and end apart: 6, of which 2 were waited for; matrix products, arithmetic and copies ran while one was open for 0% of the time, Pallas kernels for 1%

profile of v6, /device:TPU:1, one launch (start us, length us, event | category | flops | bytes accessed | tf_op | source)
XLA Modules:
  0.0 148.5 jit_solution(13243524109400606191)
XLA Ops:
  0.6 0.0 copy-start.4
  0.6 1.0 fusion.2
  1.6 0.0 copy-start
  1.6 0.0 copy-start.1
  1.7 16.2 %collective-permute-start.2 = (f32[2,32,512]{2,1,0:T(8,128)S(1)}, f32[2,32,512]{2,1,0:T(8,128)S(1)}, u32[]{:S(2)}, u32[]{:S(2)}) collective-permute-start(f32[2,32,512]{2,1,0:T(8,128)S(1)} %get-tuple-element.17), channel_id=1, source_target_pairs={{0,16},{32,48},{64,80},{96,112},{128,144},{160,176},{192,208},{224... | collective-permute-start | bytes 393224 | tf_op jit(solution)/shard_map/ppermute | solution.py:281
  17.9 1.9 %collective-permute-start.3 = (f32[2,32,512]{2,1,0:T(8,128)S(1)}, f32[2,32,512]{2,1,0:T(8,128)S(1)}, u32[]{:S(2)}, u32[]{:S(2)}) collective-permute-start(f32[2,32,512]{2,1,0:T(8,128)S(1)} %get-tuple-element.16), channel_id=1, source_target_pairs={{16,32},{48,64},{80,96},{112,128},{144,160},{176,192},{208,224},{2... | collective-permute-start | bytes 393224 | tf_op jit(solution)/shard_map/ppermute | solution.py:281
  19.8 0.0 copy-done.4
  19.8 0.0 copy-done
  19.8 0.0 copy-done.1
  19.8 0.0 copy-start.2
  19.8 0.0 copy-start.3
  19.9 0.0 copy-start.5
  19.9 4.4 %collective-permute-start = (f32[40,256]{1,0:T(8,128)S(1)}, f32[40,256]{1,0:T(8,128)S(1)}, u32[]{:S(2)}, u32[]{:S(2)}) collective-permute-start(f32[40,256]{1,0:T(8,128)S(1)} %get-tuple-element.9), channel_id=1, source_target_pairs={{0,1},{2,3},{4,5},{6,7},{8,9},{10,11},{12,13},{14,15},{1,0},{3,2},... | collective-permute-start | bytes 122888 | tf_op jit(solution)/shard_map/ppermute | solution.py:281
  24.4 0.7 collective-permute-start.1
  25.0 0.1 pad_add_fusion.refs_0_
  25.1 8.8 %collective-permute-done.n_first = f32[40,256]{1,0:T(8,128)S(1)} collective-permute-done((f32[40,256]{1,0:T(8,128)S(1)}, f32[40,256]{1,0:T(8,128)S(1)}, u32[]{:S(2)}, u32[]{:S(2)}) %collective-permute-start) | collective-permute-done | bytes 40992 | tf_op jit(solution)/shard_map/ppermute | solution.py:281
  33.9 0.0 collective-permute-done.1.n_second
  33.9 0.0 copy-done.2
  33.9 0.0 copy-done.3
  33.9 0.5 shard_map.78
  34.4 0.0 collective-permute-done.2.x_first
  34.4 0.0 collective-permute-done.3.x_second
  34.4 0.0 copy-done.5
  34.4 0.9 shard_map.79
  35.3 47.8 %all_to_all.22 = f32[16,4,128]{2,1,0:T(4,128)S(1)} all-to-all(f32[16,4,128]{2,1,0:T(4,128)S(1)} %bitcast.18), channel_id=1, replica_groups=mesh['wide'=64,'narrow'=16] {'narrow'}, dimensions={0} | all-to-all | bytes 65536 | tf_op jit(solution)/shard_map/all_to_all | solution.py:285
  83.1 0.1 copy.8
  83.2 28.2 %all_to_all.23 = f32[64,1,256]{2,1,0:T(1,128)S(1)} all-to-all(f32[64,1,256]{2,1,0:T(1,128)S(1)} %copy.8), channel_id=1, replica_groups=mesh['wide'=64,'narrow'=16] {'wide'}, dimensions={0} | all-to-all | bytes 131072 | tf_op jit(solution)/shard_map/all_to_all | solution.py:285
  111.4 1.1 shard_map.80
  112.4 0.1 copy.9
  112.5 17.7 %all_to_all.24 = f32[64,1,256]{2,1,0:T(1,128)S(1)} all-to-all(f32[64,1,256]{2,1,0:T(1,128)S(1)} %copy.9), channel_id=1, replica_groups=mesh['wide'=64,'narrow'=16] {'wide'}, dimensions={0} | all-to-all | bytes 131072 | tf_op jit(solution)/shard_map/all_to_all | solution.py:285
  130.2 0.1 shard_map.82
  130.3 2.4 %collective-permute-start.4 = (f32[48,128]{1,0:T(8,128)S(1)}, f32[48,128]{1,0:T(8,128)S(1)}, u32[]{:S(2)}, u32[]{:S(2)}) collective-permute-start(f32[48,128]{1,0:T(8,128)S(1)} %get-tuple-element.14), channel_id=1, source_target_pairs={{0,1},{2,3},{4,5},{6,7},{8,9},{10,11},{12,13},{14,15},{1,0},{3,2},... | collective-permute-start | bytes 73736 | tf_op jit(solution)/shard_map/ppermute | solution.py:281
  132.7 0.7 collective-permute-start.5
  133.3 1.0 shard_map.81
  134.3 13.0 %collective-permute-done.4.first = f32[48,128]{1,0:T(8,128)S(1)} collective-permute-done((f32[48,128]{1,0:T(8,128)S(1)}, f32[48,128]{1,0:T(8,128)S(1)}, u32[]{:S(2)}, u32[]{:S(2)}) %collective-permute-start.4) | collective-permute-done | bytes 24608 | tf_op jit(solution)/shard_map/ppermute | solution.py:281
  147.3 0.0 collective-permute-done.5.second
  147.3 1.2 shard_map.83
  (6 shorter events, 0.1 us)
Async XLA Ops:
  0.6 19.2 %copy-start.4 = (f32[16,2,256]{2,1,0:T(2,128)S(1)}, f32[16,2,256]{2,1,0:T(2,128)}, u32[]{:S(2)}) copy-start(f32[16,2,256]{2,1,0:T(2,128)} %design.3) | copy-start | bytes 98308
  1.6 18.2 %copy-start = (f32[4,32,512]{2,1,0:T(8,128)S(1)}, f32[4,32,512]{2,1,0:T(8,128)}, u32[]{:S(2)}) copy-start(f32[4,32,512]{2,1,0:T(8,128)} %kirchhoff.3) | copy-start | bytes 786436
  1.6 18.2 %copy-start.1 = (f32[4,32,512]{2,1,0:T(8,128)S(1)}, f32[4,32,512]{2,1,0:T(8,128)}, u32[]{:S(2)}) copy-start(f32[4,32,512]{2,1,0:T(8,128)} %adjoint.3) | copy-start | bytes 786436
  1.7 32.7 %collective-permute-start.2 = (f32[2,32,512]{2,1,0:T(8,128)S(1)}, f32[2,32,512]{2,1,0:T(8,128)S(1)}, u32[]{:S(2)}, u32[]{:S(2)}) collective-permute-start(f32[2,32,512]{2,1,0:T(8,128)S(1)} %get-tuple-element.17), channel_id=1, source_target_pairs={{0,16},{32,48},{64,80},{96,112},{128,144},{160,176},{192,208},{224... | collective-permute-start | bytes 393224 | tf_op jit(solution)/shard_map/ppermute | solution.py:281
  17.9 16.5 %collective-permute-start.3 = (f32[2,32,512]{2,1,0:T(8,128)S(1)}, f32[2,32,512]{2,1,0:T(8,128)S(1)}, u32[]{:S(2)}, u32[]{:S(2)}) collective-permute-start(f32[2,32,512]{2,1,0:T(8,128)S(1)} %get-tuple-element.16), channel_id=1, source_target_pairs={{16,32},{48,64},{80,96},{112,128},{144,160},{176,192},{208,224},{2... | collective-permute-start | bytes 393224 | tf_op jit(solution)/shard_map/ppermute | solution.py:281
  19.8 14.1 %copy-start.2 = (s32[16,2,256]{2,1,0:T(2,128)S(1)}, s32[16,2,256]{2,1,0:T(2,128)}, u32[]{:S(2)}) copy-start(s32[16,2,256]{2,1,0:T(2,128)} %solid.5) | copy-start | bytes 98308
  19.8 14.1 %copy-start.3 = (s32[16,2,256]{2,1,0:T(2,128)S(1)}, s32[16,2,256]{2,1,0:T(2,128)}, u32[]{:S(2)}) copy-start(s32[16,2,256]{2,1,0:T(2,128)} %void.5) | copy-start | bytes 98308
  19.9 14.5 %copy-start.5 = (bf16[4,32,512]{2,1,0:T(8,128)(2,1)S(1)}, bf16[4,32,512]{2,1,0:T(8,128)(2,1)}, u32[]{:S(2)}) copy-start(bf16[4,32,512]{2,1,0:T(8,128)(2,1)} %slope.1) | copy-start | bytes 393220
  19.9 14.0 %collective-permute-start = (f32[40,256]{1,0:T(8,128)S(1)}, f32[40,256]{1,0:T(8,128)S(1)}, u32[]{:S(2)}, u32[]{:S(2)}) collective-permute-start(f32[40,256]{1,0:T(8,128)S(1)} %get-tuple-element.9), channel_id=1, source_target_pairs={{0,1},{2,3},{4,5},{6,7},{8,9},{10,11},{12,13},{14,15},{1,0},{3,2},... | collective-permute-start | bytes 122888 | tf_op jit(solution)/shard_map/ppermute | solution.py:281
  24.4 9.5 %collective-permute-start.1 = (f32[40,256]{1,0:T(8,128)S(1)}, f32[40,256]{1,0:T(8,128)S(1)}, u32[]{:S(2)}, u32[]{:S(2)}) collective-permute-start(f32[40,256]{1,0:T(8,128)S(1)} %get-tuple-element.10), channel_id=1, source_target_pairs={{1,2},{3,4},{5,6},{7,8},{9,10},{11,12},{13,14},{2,1},{4,3},{6,5},{... | collective-permute-start | bytes 122888 | tf_op jit(solution)/shard_map/ppermute | solution.py:281
  130.3 17.0 %collective-permute-start.4 = (f32[48,128]{1,0:T(8,128)S(1)}, f32[48,128]{1,0:T(8,128)S(1)}, u32[]{:S(2)}, u32[]{:S(2)}) collective-permute-start(f32[48,128]{1,0:T(8,128)S(1)} %get-tuple-element.14), channel_id=1, source_target_pairs={{0,1},{2,3},{4,5},{6,7},{8,9},{10,11},{12,13},{14,15},{1,0},{3,2},... | collective-permute-start | bytes 73736 | tf_op jit(solution)/shard_map/ppermute | solution.py:281
  132.7 14.6 %collective-permute-start.5 = (f32[48,128]{1,0:T(8,128)S(1)}, f32[48,128]{1,0:T(8,128)S(1)}, u32[]{:S(2)}, u32[]{:S(2)}) collective-permute-start(f32[48,128]{1,0:T(8,128)S(1)} %get-tuple-element.15), channel_id=1, source_target_pairs={{1,2},{3,4},{5,6},{7,8},{9,10},{11,12},{13,14},{2,1},{4,3},{6,5},{... | collective-permute-start | bytes 73736 | tf_op jit(solution)/shard_map/ppermute | solution.py:281

commit v7 on v6

--- a/solution.py
+++ b/solution.py
@@ -71,24 +71,30 @@
     return jnp.where(even, of_second, of_first), jnp.where(even, of_first, of_second)
 
 
-def pack_kernel(kirchhoff, adjoint, design, to_first, to_second):
+def pack_kernel(k_low, k_high, a_low, a_high, design, to_first, to_second):
+    x_fine, y_all = k_low.shape[0], design.shape[2]
     even = is_even("narrow")
-    x_fine, y_fine, _ = kirchhoff.shape
-    y_all = design.shape[2]
 
     def put(rows, before, after):
         to_first[rows, :] = jnp.where(even, after, before)
         to_second[rows, :] = jnp.where(even, before, after)
 
-    for f, field in enumerate((kirchhoff, adjoint)):
+    for f, (low, high) in enumerate(((k_low, k_high), (a_low, a_high))):
         for k in range(x_fine):
             for h in range(2):
                 at, lanes = 2 * (x_fine * f + k) + h, slice(y_all * h, y_all * (h + 1))
-                put(slice(at, at + 1), field[k, 0:1, lanes], field[k, y_fine - 1 : y_fine, lanes])
+                put(slice(at, at + 1), low[k : k + 1, lanes], high[k : k + 1, lanes])
     for k in range(XC):
         at = 4 * x_fine + RADIUS * k
         planes = design[:, k, :]
         put(slice(at, at + RADIUS), planes[:RADIUS], planes[ZC - RADIUS :])
+
+
+def pack_wide_kernel(kirchhoff, adjoint, _, __, to_first, to_second):
+    even = is_even("wide")
+    for f, field in enumerate((kirchhoff, adjoint)):
+        to_first[f] = jnp.where(even, field[field.shape[0] - 1], field[0])
+        to_second[f] = jnp.where(even, field[0], field[field.shape[0] - 1])
 
 
 def restrict_kernel(kirchhoff, adjoint, slope, x_first, x_second, n_first, n_second, out):
@@ -258,7 +264,7 @@
         sens[:, x, :] = right_mul(lines, weights) * live
 
 
-def call(kernel, shape, scratch=(), smem=()):
+def call(kernel, shape, scratch=(), smem=(), flops=1 << 20):
     def run(*args):
         specs = [pl.BlockSpec(memory_space=pltpu.SMEM if i in smem else pltpu.VMEM) for i in range(len(args))]
         out_shape = jax.tree.map(lambda s: jax.ShapeDtypeStruct(s, F32), shape, is_leaf=lambda s: isinstance(s[0], int))
@@ -268,6 +274,7 @@
             in_specs=specs,
             out_specs=jax.tree.map(lambda _: pl.BlockSpec(memory_space=pltpu.VMEM), out_shape),
             scratch_shapes=[pltpu.VMEM(s, F32) for s in scratch],
+            cost_estimate=pl.CostEstimate(flops=flops, bytes_accessed=1 << 16, transcendentals=0),
             compiler_params=pltpu.CompilerParams(vmem_limit_bytes=32 << 20),
         )(*args)
 
@@ -295,15 +302,17 @@
     z_all, y_all = ZC * narrow, design.shape[2]
     x_fine = kirchhoff.shape[0]
 
-    sides = [jnp.stack([kirchhoff[x], adjoint[x]]) for x in (0, x_fine - 1)]
-    even = is_even("wide")
-    x_first, x_second = swap(jnp.where(even, sides[1], sides[0]), jnp.where(even, sides[0], sides[1]), "wide")
     packed = (4 * x_fine + XC * RADIUS, y_all)
-    n_first, n_second = swap(*call(pack_kernel, (packed, packed))(kirchhoff, adjoint, design), "narrow")
+    rows = [field[:, y] for field in (kirchhoff, adjoint) for y in (0, kirchhoff.shape[1] - 1)]
+    packed = call(pack_kernel, (packed, packed))(*rows, design)
+    n_first, n_second = swap(*packed, "narrow")
+    layers = (2, *kirchhoff.shape[1:])
+    layers = call(pack_wide_kernel, (layers, layers), flops=1 << 30)(kirchhoff, adjoint, *packed)
+    x_first, x_second = swap(*layers, "wide")
     coarse = call(restrict_kernel, (YW * narrow, LANES))(
         kirchhoff, adjoint, penalty_slope, x_first, x_second, n_first, n_second
     )
-    lines = call(design_kernel, (wide, 2 * LANES))(design, solid_mask, void_mask, n_first, n_second)
+    lines = call(design_kernel, (wide, 2 * LANES), flops=1 << 36)(design, solid_mask, void_mask, n_first, n_second)
     place = jnp.stack([lax.axis_index("wide"), lax.axis_index("narrow")]).astype(jnp.int32)
     lines, coarse, place = lax.optimization_barrier((lines, coarse, place))
     coarse = exchange(coarse, "narrow")

time: 149 us -> 147 us (0.987)
  waiting for transfers between devices: 21.8 us -> 15.6 us
  local copies, waits for them, and re-layouts: 1.16 us -> 4.6 us
    ppermute x3, waiting for transfers between devices: 21.7 us -> 13 us  [swap(): lax.ppermute(to_first, axis, both[0])]
    unnamed x14 -> x18, local copies, waits for them, and re-layouts: 0.05 us -> 2.65 us
    ppermute x3, waiting for transfers between devices: 0.01 us -> 2.58 us  [swap(): lax.ppermute(to_second, axis, both[1])]
    ppermute x3, starting transfers between devices: 23 us -> 21.5 us  [swap(): lax.ppermute(to_first, axis, both[0])]
    ppermute x3, starting transfers between devices: 3.25 us -> 4.77 us  [swap(): lax.ppermute(to_second, axis, both[1])]
    pallas_call x7 -> x8, Pallas kernels: 4.78 us -> 4.8 us  [run(): pl.pallas_call(kernel, out_shape=out_shape, in_specs=specs, out_specs=jax...]
where the time goes in v7:
time: 147 us; the launch traced here: 146 us
  blocking collectives  93.7 us (64%)
  starting transfers between devices  26.2 us (18%)
  waiting for transfers between devices  15.6 us (11%)
  Pallas kernels  4.8 us (3%)
  local copies, waits for them, and re-layouts  4.6 us (3%)
    all_to_all x3, blocking collectives, exchange(): return lax.all_to_all(values, axis, split_axis=0, concat_axis=0, tiled=True)  93.7 us
    ppermute x3, starting transfers between devices, swap(): lax.ppermute(to_first, axis, both[0])  21.5 us
    ppermute x3, waiting for transfers between devices, swap(): lax.ppermute(to_first, axis, both[0])  13 us
    pallas_call x8, Pallas kernels, run(): pl.pallas_call(kernel, out_shape=out_shape, in_specs=specs, out_specs=jax...  4.8 us
    ppermute x3, starting transfers between devices, swap(): lax.ppermute(to_second, axis, both[1])  4.77 us
  transfers between devices with their start and end apart: 6, of which 2 were waited for; matrix products, arithmetic and copies ran while one was open for 0% of the time, Pallas kernels for 1%

profile of v7, /device:TPU:1, one launch (start us, length us, event | category | flops | bytes accessed | tf_op | source)
XLA Modules:
  0.0 145.9 jit_solution(14815976912567200007)
XLA Ops:
  0.6 0.9 fusion
  1.5 0.9 fusion.1
  2.4 0.0 copy-start.7
  2.5 0.7 copy-done.7
  3.2 16.3 %collective-permute-start = (f32[40,256]{1,0:T(8,128)S(1)}, f32[40,256]{1,0:T(8,128)S(1)}, u32[]{:S(2)}, u32[]{:S(2)}) collective-permute-start(f32[40,256]{1,0:T(8,128)S(1)} %get-tuple-element.11._), channel_id=1, source_target_pairs={{0,1},{2,3},{4,5},{6,7},{8,9},{10,11},{12,13},{14,15},{1,0},{3,2},... | collective-permute-start | bytes 122888 | tf_op jit(solution)/shard_map/ppermute | solution.py:288
  19.5 0.7 collective-permute-start.1
  20.2 0.0 copy-start
  20.2 0.9 copy-done
  21.1 0.0 copy-start.2
  21.1 0.9 copy-done.2
  22.1 0.0 copy-start.4
  22.1 0.0 copy-start.5
  22.1 2.9 %collective-permute-start.2 = (f32[2,32,512]{2,1,0:T(8,128)S(1)}, f32[2,32,512]{2,1,0:T(8,128)S(1)}, u32[]{:S(2)}, u32[]{:S(2)}) collective-permute-start(f32[2,32,512]{2,1,0:T(8,128)S(1)} %get-tuple-element.13), channel_id=1, source_target_pairs={{0,16},{32,48},{64,80},{96,112},{128,144},{160,176},{192,208},{224... | collective-permute-start | bytes 393224 | tf_op jit(solution)/shard_map/ppermute | solution.py:288
  25.0 3.4 %collective-permute-start.3 = (f32[2,32,512]{2,1,0:T(8,128)S(1)}, f32[2,32,512]{2,1,0:T(8,128)S(1)}, u32[]{:S(2)}, u32[]{:S(2)}) collective-permute-start(f32[2,32,512]{2,1,0:T(8,128)S(1)} %get-tuple-element.14), channel_id=1, source_target_pairs={{16,32},{48,64},{80,96},{112,128},{144,160},{176,192},{208,224},{2... | collective-permute-start | bytes 393224 | tf_op jit(solution)/shard_map/ppermute | solution.py:288
  28.4 0.1 pad_add_fusion.refs_0_
  28.5 0.0 copy-start.1
  28.5 0.0 copy-start.3
  28.5 0.0 copy-start.6
  28.5 0.0 collective-permute-done.n_first
  28.5 0.0 collective-permute-done.1.n_second
  28.5 0.0 copy-done.4
  28.6 0.0 copy-done.5
  28.6 0.5 shard_map.78
  29.1 0.0 collective-permute-done.2.x_first
  29.1 2.6 %collective-permute-done.3.x_second = f32[2,32,512]{2,1,0:T(8,128)S(1)} collective-permute-done((f32[2,32,512]{2,1,0:T(8,128)S(1)}, f32[2,32,512]{2,1,0:T(8,128)S(1)}, u32[]{:S(2)}, u32[]{:S(2)}) %collective-permute-start.3) | collective-permute-done | bytes 131104 | tf_op jit(solution)/shard_map/ppermute | solution.py:288
  31.7 0.0 copy-done.1
  31.7 0.0 copy-done.3
  31.7 0.0 copy-done.6
  31.7 0.9 shard_map.80
  32.5 47.9 %all_to_all.22 = f32[16,4,128]{2,1,0:T(4,128)S(1)} all-to-all(f32[16,4,128]{2,1,0:T(4,128)S(1)} %bitcast.26), channel_id=1, replica_groups=mesh['wide'=64,'narrow'=16] {'narrow'}, dimensions={0} | all-to-all | bytes 65536 | tf_op jit(solution)/shard_map/all_to_all | solution.py:292
  80.5 0.1 copy.16
  80.6 28.1 %all_to_all.23 = f32[64,1,256]{2,1,0:T(1,128)S(1)} all-to-all(f32[64,1,256]{2,1,0:T(1,128)S(1)} %copy.16), channel_id=1, replica_groups=mesh['wide'=64,'narrow'=16] {'wide'}, dimensions={0} | all-to-all | bytes 131072 | tf_op jit(solution)/shard_map/all_to_all | solution.py:292
  108.7 1.1 shard_map.81
  109.8 0.1 copy.17
  109.9 17.7 %all_to_all.24 = f32[64,1,256]{2,1,0:T(1,128)S(1)} all-to-all(f32[64,1,256]{2,1,0:T(1,128)S(1)} %copy.17), channel_id=1, replica_groups=mesh['wide'=64,'narrow'=16] {'wide'}, dimensions={0} | all-to-all | bytes 131072 | tf_op jit(solution)/shard_map/all_to_all | solution.py:292
  127.6 0.1 shard_map.83
  127.6 2.3 %collective-permute-start.4 = (f32[48,128]{1,0:T(8,128)S(1)}, f32[48,128]{1,0:T(8,128)S(1)}, u32[]{:S(2)}, u32[]{:S(2)}) collective-permute-start(f32[48,128]{1,0:T(8,128)S(1)} %get-tuple-element.18), channel_id=1, source_target_pairs={{0,1},{2,3},{4,5},{6,7},{8,9},{10,11},{12,13},{14,15},{1,0},{3,2},... | collective-permute-start | bytes 73736 | tf_op jit(solution)/shard_map/ppermute | solution.py:288
  130.0 0.7 collective-permute-start.5
  130.6 1.0 shard_map.82
  131.6 13.0 %collective-permute-done.4.first = f32[48,128]{1,0:T(8,128)S(1)} collective-permute-done((f32[48,128]{1,0:T(8,128)S(1)}, f32[48,128]{1,0:T(8,128)S(1)}, u32[]{:S(2)}, u32[]{:S(2)}) %collective-permute-start.4) | collective-permute-done | bytes 24608 | tf_op jit(solution)/shard_map/ppermute | solution.py:288
  144.7 0.0 collective-permute-done.5.second
  144.7 1.2 shard_map.84
  (8 shorter events, 0.1 us)
Async XLA Ops:
  2.4 0.8 copy-start.7
  3.2 25.3 %collective-permute-start = (f32[40,256]{1,0:T(8,128)S(1)}, f32[40,256]{1,0:T(8,128)S(1)}, u32[]{:S(2)}, u32[]{:S(2)}) collective-permute-start(f32[40,256]{1,0:T(8,128)S(1)} %get-tuple-element.11._), channel_id=1, source_target_pairs={{0,1},{2,3},{4,5},{6,7},{8,9},{10,11},{12,13},{14,15},{1,0},{3,2},... | collective-permute-start | bytes 122888 | tf_op jit(solution)/shard_map/ppermute | solution.py:288
  19.5 9.0 %collective-permute-start.1 = (f32[40,256]{1,0:T(8,128)S(1)}, f32[40,256]{1,0:T(8,128)S(1)}, u32[]{:S(2)}, u32[]{:S(2)}) collective-permute-start(f32[40,256]{1,0:T(8,128)S(1)} %get-tuple-element.12.__), channel_id=1, source_target_pairs={{1,2},{3,4},{5,6},{7,8},{9,10},{11,12},{13,14},{2,1},{4,3},{6,5},{... | collective-permute-start | bytes 122888 | tf_op jit(solution)/shard_map/ppermute | solution.py:288
  20.2 1.0 copy-start
  21.1 0.9 copy-start.2
  22.1 6.5 %copy-start.4 = (s32[16,2,256]{2,1,0:T(2,128)S(1)}, s32[16,2,256]{2,1,0:T(2,128)}, u32[]{:S(2)}) copy-start(s32[16,2,256]{2,1,0:T(2,128)} %solid.5) | copy-start | bytes 98308
  22.1 6.5 %copy-start.5 = (s32[16,2,256]{2,1,0:T(2,128)S(1)}, s32[16,2,256]{2,1,0:T(2,128)}, u32[]{:S(2)}) copy-start(s32[16,2,256]{2,1,0:T(2,128)} %void.5) | copy-start | bytes 98308
  22.1 6.9 %collective-permute-start.2 = (f32[2,32,512]{2,1,0:T(8,128)S(1)}, f32[2,32,512]{2,1,0:T(8,128)S(1)}, u32[]{:S(2)}, u32[]{:S(2)}) collective-permute-start(f32[2,32,512]{2,1,0:T(8,128)S(1)} %get-tuple-element.13), channel_id=1, source_target_pairs={{0,16},{32,48},{64,80},{96,112},{128,144},{160,176},{192,208},{224... | collective-permute-start | bytes 393224 | tf_op jit(solution)/shard_map/ppermute | solution.py:288
  25.0 6.7 %collective-permute-start.3 = (f32[2,32,512]{2,1,0:T(8,128)S(1)}, f32[2,32,512]{2,1,0:T(8,128)S(1)}, u32[]{:S(2)}, u32[]{:S(2)}) collective-permute-start(f32[2,32,512]{2,1,0:T(8,128)S(1)} %get-tuple-element.14), channel_id=1, source_target_pairs={{16,32},{48,64},{80,96},{112,128},{144,160},{176,192},{208,224},{2... | collective-permute-start | bytes 393224 | tf_op jit(solution)/shard_map/ppermute | solution.py:288
  28.5 3.1 %copy-start.1 = (f32[4,32,512]{2,1,0:T(8,128)S(1)}, f32[4,32,512]{2,1,0:T(8,128)}, u32[]{:S(2)}) copy-start(f32[4,32,512]{2,1,0:T(8,128)} %kirchhoff.3) | copy-start | bytes 786436
  28.5 3.1 %copy-start.3 = (f32[4,32,512]{2,1,0:T(8,128)S(1)}, f32[4,32,512]{2,1,0:T(8,128)}, u32[]{:S(2)}) copy-start(f32[4,32,512]{2,1,0:T(8,128)} %adjoint.3) | copy-start | bytes 786436
  28.5 3.1 %copy-start.6 = (bf16[4,32,512]{2,1,0:T(8,128)(2,1)S(1)}, bf16[4,32,512]{2,1,0:T(8,128)(2,1)}, u32[]{:S(2)}) copy-start(bf16[4,32,512]{2,1,0:T(8,128)(2,1)} %slope.1) | copy-start | bytes 393220
  127.6 17.0 %collective-permute-start.4 = (f32[48,128]{1,0:T(8,128)S(1)}, f32[48,128]{1,0:T(8,128)S(1)}, u32[]{:S(2)}, u32[]{:S(2)}) collective-permute-start(f32[48,128]{1,0:T(8,128)S(1)} %get-tuple-element.18), channel_id=1, source_target_pairs={{0,1},{2,3},{4,5},{6,7},{8,9},{10,11},{12,13},{14,15},{1,0},{3,2},... | collective-permute-start | bytes 73736 | tf_op jit(solution)/shard_map/ppermute | solution.py:288
  130.0 14.7 %collective-permute-start.5 = (f32[48,128]{1,0:T(8,128)S(1)}, f32[48,128]{1,0:T(8,128)S(1)}, u32[]{:S(2)}, u32[]{:S(2)}) collective-permute-start(f32[48,128]{1,0:T(8,128)S(1)} %get-tuple-element.19), channel_id=1, source_target_pairs={{1,2},{3,4},{5,6},{7,8},{9,10},{11,12},{13,14},{2,1},{4,3},{6,5},{... | collective-permute-start | bytes 73736 | tf_op jit(solution)/shard_map/ppermute | solution.py:288

commit v8 on v7

--- a/solution.py
+++ b/solution.py
@@ -83,7 +83,7 @@
         for k in range(x_fine):
             for h in range(2):
                 at, lanes = 2 * (x_fine * f + k) + h, slice(y_all * h, y_all * (h + 1))
-                put(slice(at, at + 1), low[k : k + 1, lanes], high[k : k + 1, lanes])
+                put(slice(at, at + 1), low[k, 0:1, lanes], high[k, 7:8, lanes])
     for k in range(XC):
         at = 4 * x_fine + RADIUS * k
         planes = design[:, k, :]
@@ -281,6 +281,20 @@
     return run
 
 
+def pack_narrow(kirchhoff, adjoint, design, shape):
+    x_fine, y_fine, z_fine = kirchhoff.shape
+    low = pl.BlockSpec((x_fine, 8, z_fine), lambda i: (0, 0, 0))
+    high = pl.BlockSpec((x_fine, 8, z_fine), lambda i: (0, y_fine // 8 - 1, 0))
+    out = pl.BlockSpec(shape, lambda i: (0, 0))
+    return pl.pallas_call(
+        pack_kernel,
+        grid=(1,),
+        out_shape=[jax.ShapeDtypeStruct(shape, F32)] * 2,
+        in_specs=[low, high, low, high, pl.BlockSpec(design.shape, lambda i: (0, 0, 0))],
+        out_specs=[out, out],
+    )(kirchhoff, kirchhoff, adjoint, adjoint, design)
+
+
 def swap(to_first, to_second, axis):
     count = lax.axis_size(axis)
     pairs = [[(i, i + 1) for i in range(start, count - 1, 2)] for start in (0, 1)]
@@ -303,8 +317,7 @@
     x_fine = kirchhoff.shape[0]
 
     packed = (4 * x_fine + XC * RADIUS, y_all)
-    rows = [field[:, y] for field in (kirchhoff, adjoint) for y in (0, kirchhoff.shape[1] - 1)]
-    packed = call(pack_kernel, (packed, packed))(*rows, design)
+    packed = pack_narrow(kirchhoff, adjoint, design, packed)
     n_first, n_second = swap(*packed, "narrow")
     layers = (2, *kirchhoff.shape[1:])
     layers = call(pack_wide_kernel, (layers, layers), flops=1 << 30)(kirchhoff, adjoint, *packed)

time: 147 us -> 146 us (level)
  local copies, waits for them, and re-layouts: 4.6 us -> 1.75 us
  Pallas kernels: 4.8 us -> 6.44 us
    slice x2 -> x0, local copies, waits for them, and re-layouts: 1.78 us -> none  [per_device(): field[:, y]]
    pallas_call x0 -> x1, Pallas kernels: none -> 1.68 us  [pack_narrow(): pl.pallas_call(pack_kernel, grid=(1,), out_shape=[jax.ShapeDtypeStruct(sh...]
    pallas_call x8 -> x7, Pallas kernels: 4.8 us -> 4.75 us  [run(): pl.pallas_call(kernel, out_shape=out_shape, in_specs=specs, out_specs=jax...]
where the time goes in v8:
time: 146 us; the launch traced here: 145 us
  blocking collectives  94.3 us (65%)
  starting transfers between devices  26.4 us (18%)
  waiting for transfers between devices  15.5 us (11%)
  Pallas kernels  6.44 us (4%)
  local copies, waits for them, and re-layouts  1.75 us (1%)
    all_to_all x3, blocking collectives, exchange(): return lax.all_to_all(values, axis, split_axis=0, concat_axis=0, tiled=True)  94.3 us
    ppermute x3, starting transfers between devices, swap(): lax.ppermute(to_first, axis, both[0])  21.5 us
    ppermute x3, waiting for transfers between devices, swap(): lax.ppermute(to_first, axis, both[0])  13 us
    ppermute x3, starting transfers between devices, swap(): lax.ppermute(to_second, axis, both[1])  4.9 us
    pallas_call x7, Pallas kernels, run(): pl.pallas_call(kernel, out_shape=out_shape, in_specs=specs, out_specs=jax...  4.75 us
  transfers between devices with their start and end apart: 6, of which 2 were waited for; matrix products, arithmetic and copies ran while one was open for 0% of the time, Pallas kernels for 1%

profile of v8, /device:TPU:1, one launch (start us, length us, event | category | flops | bytes accessed | tf_op | source)
XLA Modules:
  0.0 145.3 jit_solution(15805307754171619697)
XLA Ops:
  0.6 0.0 copy-start
  0.6 0.0 copy-start.1
  0.6 1.7 %shard_map.77 = (f32[40,256]{1,0:T(8,128)}, f32[40,256]{1,0:T(8,128)}) custom-call(f32[4,32,512]{2,1,0:T(8,128)} %kirchhoff.3, f32[4,32,512]{2,1,0:T(8,128)} %kirchhoff.3, f32[4,32,512]{2,1,0:T(8,128)} %adjoint.3, f32[4,32,512]{2,1,0:T(8,128)} %adjoint.3, f32[16,2,256]{2,1,0:T(2,128)} %design.3), custom_call_target="tpu_custom_call" | custom-call | tf_op jit(solution)/shard_map/pallas_call | solution.py:289
  2.3 16.3 %collective-permute-start = (f32[40,256]{1,0:T(8,128)}, f32[40,256]{1,0:T(8,128)S(1)}, u32[]{:S(2)}, u32[]{:S(2)}) collective-permute-start(f32[40,256]{1,0:T(8,128)} %get-tuple-element.11._), channel_id=1, source_target_pairs={{0,1},{2,3},{4,5},{6,7},{8,9},{10,11},{12,13},{14,15},{1,0},{3,2},... | collective-permute-start | bytes 122888 | tf_op jit(solution)/shard_map/ppermute | solution.py:302
  18.6 0.0 copy-start.2
  18.6 0.0 copy-start.3
  18.6 0.0 copy-start.5
  18.6 0.8 collective-permute-start.1
  19.4 0.0 copy-done
  19.4 0.0 copy-done.1
  19.5 0.0 copy-start.6
  19.5 0.8 copy-done.6
  20.2 0.0 copy-start.7
  20.2 0.8 copy-done.7
  21.0 2.9 %collective-permute-start.2 = (f32[2,32,512]{2,1,0:T(8,128)S(1)}, f32[2,32,512]{2,1,0:T(8,128)S(1)}, u32[]{:S(2)}, u32[]{:S(2)}) collective-permute-start(f32[2,32,512]{2,1,0:T(8,128)S(1)} %get-tuple-element.13), channel_id=1, source_target_pairs={{0,16},{32,48},{64,80},{96,112},{128,144},{160,176},{192,208},{224... | collective-permute-start | bytes 393224 | tf_op jit(solution)/shard_map/ppermute | solution.py:302
  23.9 3.4 %collective-permute-start.3 = (f32[2,32,512]{2,1,0:T(8,128)S(1)}, f32[2,32,512]{2,1,0:T(8,128)S(1)}, u32[]{:S(2)}, u32[]{:S(2)}) collective-permute-start(f32[2,32,512]{2,1,0:T(8,128)S(1)} %get-tuple-element.14), channel_id=1, source_target_pairs={{16,32},{48,64},{80,96},{112,128},{144,160},{176,192},{208,224},{2... | collective-permute-start | bytes 393224 | tf_op jit(solution)/shard_map/ppermute | solution.py:302
  27.4 0.1 pad_add_fusion.refs_0_
  27.4 0.0 copy-start.4
  27.5 0.0 collective-permute-done.n_first
  27.5 0.0 collective-permute-done.1.n_second
  27.5 0.0 copy-done.2
  27.5 0.0 copy-done.3
  27.5 0.0 copy-done.5
  27.5 0.5 shard_map.78
  28.0 0.0 collective-permute-done.2.x_first
  28.0 2.5 %collective-permute-done.3.x_second = f32[2,32,512]{2,1,0:T(8,128)S(1)} collective-permute-done((f32[2,32,512]{2,1,0:T(8,128)S(1)}, f32[2,32,512]{2,1,0:T(8,128)S(1)}, u32[]{:S(2)}, u32[]{:S(2)}) %collective-permute-start.3) | collective-permute-done | bytes 131104 | tf_op jit(solution)/shard_map/ppermute | solution.py:302
  30.5 0.0 copy-done.4
  30.5 0.9 shard_map.80
  31.4 48.5 %all_to_all.22 = f32[16,4,128]{2,1,0:T(4,128)S(1)} all-to-all(f32[16,4,128]{2,1,0:T(4,128)S(1)} %bitcast.18), channel_id=1, replica_groups=mesh['wide'=64,'narrow'=16] {'narrow'}, dimensions={0} | all-to-all | bytes 65536 | tf_op jit(solution)/shard_map/all_to_all | solution.py:306
  79.9 0.1 copy.8
  79.9 28.2 %all_to_all.23 = f32[64,1,256]{2,1,0:T(1,128)S(1)} all-to-all(f32[64,1,256]{2,1,0:T(1,128)S(1)} %copy.8), channel_id=1, replica_groups=mesh['wide'=64,'narrow'=16] {'wide'}, dimensions={0} | all-to-all | bytes 131072 | tf_op jit(solution)/shard_map/all_to_all | solution.py:306
  108.1 1.1 shard_map.81
  109.2 0.1 copy.9
  109.3 17.7 %all_to_all.24 = f32[64,1,256]{2,1,0:T(1,128)S(1)} all-to-all(f32[64,1,256]{2,1,0:T(1,128)S(1)} %copy.9), channel_id=1, replica_groups=mesh['wide'=64,'narrow'=16] {'wide'}, dimensions={0} | all-to-all | bytes 131072 | tf_op jit(solution)/shard_map/all_to_all | solution.py:306
  126.9 0.1 shard_map.83
  127.0 2.3 %collective-permute-start.4 = (f32[48,128]{1,0:T(8,128)S(1)}, f32[48,128]{1,0:T(8,128)S(1)}, u32[]{:S(2)}, u32[]{:S(2)}) collective-permute-start(f32[48,128]{1,0:T(8,128)S(1)} %get-tuple-element.18), channel_id=1, source_target_pairs={{0,1},{2,3},{4,5},{6,7},{8,9},{10,11},{12,13},{14,15},{1,0},{3,2},... | collective-permute-start | bytes 73736 | tf_op jit(solution)/shard_map/ppermute | solution.py:302
  129.4 0.7 collective-permute-start.5
  130.1 1.0 shard_map.82
  131.0 13.0 %collective-permute-done.4.first = f32[48,128]{1,0:T(8,128)S(1)} collective-permute-done((f32[48,128]{1,0:T(8,128)S(1)}, f32[48,128]{1,0:T(8,128)S(1)}, u32[]{:S(2)}, u32[]{:S(2)}) %collective-permute-start.4) | collective-permute-done | bytes 24608 | tf_op jit(solution)/shard_map/ppermute | solution.py:302
  144.1 0.0 collective-permute-done.5.second
  144.1 1.2 shard_map.84
  (5 shorter events, 0.0 us)
Async XLA Ops:
  0.6 18.8 %copy-start = (f32[4,32,512]{2,1,0:T(8,128)S(1)}, f32[4,32,512]{2,1,0:T(8,128)}, u32[]{:S(2)}) copy-start(f32[4,32,512]{2,1,0:T(8,128)} %kirchhoff.3) | copy-start | bytes 786436
  0.6 18.8 %copy-start.1 = (f32[4,32,512]{2,1,0:T(8,128)S(1)}, f32[4,32,512]{2,1,0:T(8,128)}, u32[]{:S(2)}) copy-start(f32[4,32,512]{2,1,0:T(8,128)} %adjoint.3) | copy-start | bytes 786436
  2.3 25.1 %collective-permute-start = (f32[40,256]{1,0:T(8,128)}, f32[40,256]{1,0:T(8,128)S(1)}, u32[]{:S(2)}, u32[]{:S(2)}) collective-permute-start(f32[40,256]{1,0:T(8,128)} %get-tuple-element.11._), channel_id=1, source_target_pairs={{0,1},{2,3},{4,5},{6,7},{8,9},{10,11},{12,13},{14,15},{1,0},{3,2},... | collective-permute-start | bytes 122888 | tf_op jit(solution)/shard_map/ppermute | solution.py:302
  18.6 8.9 %copy-start.2 = (s32[16,2,256]{2,1,0:T(2,128)S(1)}, s32[16,2,256]{2,1,0:T(2,128)}, u32[]{:S(2)}) copy-start(s32[16,2,256]{2,1,0:T(2,128)} %solid.5) | copy-start | bytes 98308
  18.6 8.9 %copy-start.3 = (s32[16,2,256]{2,1,0:T(2,128)S(1)}, s32[16,2,256]{2,1,0:T(2,128)}, u32[]{:S(2)}) copy-start(s32[16,2,256]{2,1,0:T(2,128)} %void.5) | copy-start | bytes 98308
  18.6 8.9 %copy-start.5 = (f32[16,2,256]{2,1,0:T(2,128)S(1)}, f32[16,2,256]{2,1,0:T(2,128)}, u32[]{:S(2)}) copy-start(f32[16,2,256]{2,1,0:T(2,128)} %design.3) | copy-start | bytes 98308
  18.6 8.8 %collective-permute-start.1 = (f32[40,256]{1,0:T(8,128)}, f32[40,256]{1,0:T(8,128)S(1)}, u32[]{:S(2)}, u32[]{:S(2)}) collective-permute-start(f32[40,256]{1,0:T(8,128)} %get-tuple-element.12.__), channel_id=1, source_target_pairs={{1,2},{3,4},{5,6},{7,8},{9,10},{11,12},{13,14},{2,1},{4,3},{6,5},{... | collective-permute-start | bytes 122888 | tf_op jit(solution)/shard_map/ppermute | solution.py:302
  19.5 0.8 copy-start.6
  20.2 0.8 copy-start.7
  21.0 6.9 %collective-permute-start.2 = (f32[2,32,512]{2,1,0:T(8,128)S(1)}, f32[2,32,512]{2,1,0:T(8,128)S(1)}, u32[]{:S(2)}, u32[]{:S(2)}) collective-permute-start(f32[2,32,512]{2,1,0:T(8,128)S(1)} %get-tuple-element.13), channel_id=1, source_target_pairs={{0,16},{32,48},{64,80},{96,112},{128,144},{160,176},{192,208},{224... | collective-permute-start | bytes 393224 | tf_op jit(solution)/shard_map/ppermute | solution.py:302
  23.9 6.6 %collective-permute-start.3 = (f32[2,32,512]{2,1,0:T(8,128)S(1)}, f32[2,32,512]{2,1,0:T(8,128)S(1)}, u32[]{:S(2)}, u32[]{:S(2)}) collective-permute-start(f32[2,32,512]{2,1,0:T(8,128)S(1)} %get-tuple-element.14), channel_id=1, source_target_pairs={{16,32},{48,64},{80,96},{112,128},{144,160},{176,192},{208,224},{2... | collective-permute-start | bytes 393224 | tf_op jit(solution)/shard_map/ppermute | solution.py:302
  27.4 3.1 %copy-start.4 = (bf16[4,32,512]{2,1,0:T(8,128)(2,1)S(1)}, bf16[4,32,512]{2,1,0:T(8,128)(2,1)}, u32[]{:S(2)}) copy-start(bf16[4,32,512]{2,1,0:T(8,128)(2,1)} %slope.1) | copy-start | bytes 393220
  127.0 17.0 %collective-permute-start.4 = (f32[48,128]{1,0:T(8,128)S(1)}, f32[48,128]{1,0:T(8,128)S(1)}, u32[]{:S(2)}, u32[]{:S(2)}) collective-permute-start(f32[48,128]{1,0:T(8,128)S(1)} %get-tuple-element.18), channel_id=1, source_target_pairs={{0,1},{2,3},{4,5},{6,7},{8,9},{10,11},{12,13},{14,15},{1,0},{3,2},... | collective-permute-start | bytes 73736 | tf_op jit(solution)/shard_map/ppermute | solution.py:302
  129.4 14.7 %collective-permute-start.5 = (f32[48,128]{1,0:T(8,128)S(1)}, f32[48,128]{1,0:T(8,128)S(1)}, u32[]{:S(2)}, u32[]{:S(2)}) collective-permute-start(f32[48,128]{1,0:T(8,128)S(1)} %get-tuple-element.19), channel_id=1, source_target_pairs={{1,2},{3,4},{5,6},{7,8},{9,10},{11,12},{13,14},{2,1},{4,3},{6,5},{... | collective-permute-start | bytes 73736 | tf_op jit(solution)/shard_map/ppermute | solution.py:302

commit v9 on v8

--- a/solution.py
+++ b/solution.py
@@ -90,11 +90,11 @@
         put(slice(at, at + RADIUS), planes[:RADIUS], planes[ZC - RADIUS :])
 
 
-def pack_wide_kernel(kirchhoff, adjoint, _, __, to_first, to_second):
+def pack_wide_kernel(k_low, k_high, a_low, a_high, _, __, to_first, to_second):
     even = is_even("wide")
-    for f, field in enumerate((kirchhoff, adjoint)):
-        to_first[f] = jnp.where(even, field[field.shape[0] - 1], field[0])
-        to_second[f] = jnp.where(even, field[0], field[field.shape[0] - 1])
+    for f, (low, high) in enumerate(((k_low, k_high), (a_low, a_high))):
+        to_first[f] = jnp.where(even, high[0], low[0])
+        to_second[f] = jnp.where(even, low[0], high[0])
 
 
 def restrict_kernel(kirchhoff, adjoint, slope, x_first, x_second, n_first, n_second, out):
@@ -295,6 +295,21 @@
     )(kirchhoff, kirchhoff, adjoint, adjoint, design)
 
 
+def pack_wide(kirchhoff, adjoint, packed, shape):
+    x_fine = kirchhoff.shape[0]
+    low = pl.BlockSpec((1, *shape[1:]), lambda i: (0, 0, 0))
+    high = pl.BlockSpec((1, *shape[1:]), lambda i: (x_fine - 1, 0, 0))
+    out, unread = pl.BlockSpec(shape, lambda i: (0, 0, 0)), pl.BlockSpec(memory_space=pl.ANY)
+    return pl.pallas_call(
+        pack_wide_kernel,
+        grid=(1,),
+        out_shape=[jax.ShapeDtypeStruct(shape, F32)] * 2,
+        in_specs=[low, high, low, high, unread, unread],
+        out_specs=[out, out],
+        cost_estimate=pl.CostEstimate(flops=1 << 30, bytes_accessed=1 << 16, transcendentals=0),
+    )(kirchhoff, kirchhoff, adjoint, adjoint, *packed)
+
+
 def swap(to_first, to_second, axis):
     count = lax.axis_size(axis)
     pairs = [[(i, i + 1) for i in range(start, count - 1, 2)] for start in (0, 1)]
@@ -320,7 +335,7 @@
     packed = pack_narrow(kirchhoff, adjoint, design, packed)
     n_first, n_second = swap(*packed, "narrow")
     layers = (2, *kirchhoff.shape[1:])
-    layers = call(pack_wide_kernel, (layers, layers), flops=1 << 30)(kirchhoff, adjoint, *packed)
+    layers = pack_wide(kirchhoff, adjoint, packed, layers)
     x_first, x_second = swap(*layers, "wide")
     coarse = call(restrict_kernel, (YW * narrow, LANES))(
         kirchhoff, adjoint, penalty_slope, x_first, x_second, n_first, n_second

time: 146 us -> 146 us (level)
  Pallas kernels: 6.44 us -> 8.02 us
  local copies, waits for them, and re-layouts: 1.75 us -> 0.2 us
    pallas_call x0 -> x1, Pallas kernels: none -> 1.67 us  [pack_wide(): pl.pallas_call(pack_wide_kernel, grid=(1,), out_shape=[jax.ShapeDtypeStru...]
    unnamed x18 -> x14, local copies, waits for them, and re-layouts: 1.59 us -> 0.04 us
    pallas_call x7 -> x6, Pallas kernels: 4.75 us -> 4.73 us  [run(): pl.pallas_call(kernel, out_shape=out_shape, in_specs=specs, out_specs=jax...]
  transfers between devices with their start and end apart: 6 -> 6, of which waited for: 2 -> 2; matrix products, arithmetic and copies ran while one was open for 0% -> 0% of each run, Pallas kernels for 1% -> 2%
where the time goes in v9:
time: 146 us; the launch traced here: 145 us
  blocking collectives  94.1 us (64%)
  starting transfers between devices  26.4 us (18%)
  waiting for transfers between devices  15.7 us (11%)
  Pallas kernels  8.02 us (5%)
    all_to_all x3, blocking collectives, exchange(): return lax.all_to_all(values, axis, split_axis=0, concat_axis=0, tiled=True)  94.1 us
    ppermute x3, starting transfers between devices, swap(): lax.ppermute(to_first, axis, both[0])  21.5 us
    ppermute x3, waiting for transfers between devices, swap(): lax.ppermute(to_first, axis, both[0])  13 us
    ppermute x3, starting transfers between devices, swap(): lax.ppermute(to_second, axis, both[1])  4.9 us
    pallas_call x6, Pallas kernels, run(): pl.pallas_call(kernel, out_shape=out_shape, in_specs=specs, out_specs=jax...  4.73 us
  transfers between devices with their start and end apart: 6, of which 2 were waited for; matrix products, arithmetic and copies ran while one was open for 0% of the time, Pallas kernels for 2%

profile of v9, /device:TPU:1, one launch (start us, length us, event | category | flops | bytes accessed | tf_op | source)
XLA Modules:
  0.0 145.3 jit_solution(9059596560669769742)
XLA Ops:
  0.6 1.6 %shard_map.77 = (f32[40,256]{1,0:T(8,128)}, f32[40,256]{1,0:T(8,128)}) custom-call(f32[4,32,512]{2,1,0:T(8,128)} %kirchhoff.1, f32[4,32,512]{2,1,0:T(8,128)} %kirchhoff.1, f32[4,32,512]{2,1,0:T(8,128)} %adjoint.1, f32[4,32,512]{2,1,0:T(8,128)} %adjoint.1, f32[16,2,256]{2,1,0:T(2,128)} %design.3), custom_call_target="tpu_custom_call" | custom-call | tf_op jit(solution)/shard_map/pallas_call | solution.py:289
  2.3 16.3 %collective-permute-start = (f32[40,256]{1,0:T(8,128)}, f32[40,256]{1,0:T(8,128)S(1)}, u32[]{:S(2)}, u32[]{:S(2)}) collective-permute-start(f32[40,256]{1,0:T(8,128)} %get-tuple-element.11._), channel_id=1, source_target_pairs={{0,1},{2,3},{4,5},{6,7},{8,9},{10,11},{12,13},{14,15},{1,0},{3,2},... | collective-permute-start | bytes 122888 | tf_op jit(solution)/shard_map/ppermute | solution.py:317
  18.5 0.0 copy-start.2
  18.5 0.0 copy-start.3
  18.5 0.0 copy-start.5
  18.6 0.8 collective-permute-start.1
  19.4 1.7 %shard_map.79 = (f32[2,32,512]{2,1,0:T(8,128)}, f32[2,32,512]{2,1,0:T(8,128)}) custom-call(f32[4,32,512]{2,1,0:T(8,128)} %kirchhoff.1, f32[4,32,512]{2,1,0:T(8,128)} %kirchhoff.1, f32[4,32,512]{2,1,0:T(8,128)} %adjoint.1, f32[4,32,512]{2,1,0:T(8,128)} %adjoint.1, f32[40,256]{1,0:T(8,128)} %get-tuple-element.11._, f32[40,256]{1,0:T(8,128)} %get-tuple-element.12.__), custom_call_target="tpu_custom_call" | custom-call | flops 1073741824 | bytes 65536 | tf_op jit(solution)/shard_map/pallas_call | solution.py:303
  21.0 2.9 %collective-permute-start.2 = (f32[2,32,512]{2,1,0:T(8,128)}, f32[2,32,512]{2,1,0:T(8,128)S(1)}, u32[]{:S(2)}, u32[]{:S(2)}) collective-permute-start(f32[2,32,512]{2,1,0:T(8,128)} %get-tuple-element.13), channel_id=1, source_target_pairs={{0,16},{32,48},{64,80},{96,112},{128,144},{160,176},{192,208},{224... | collective-permute-start | bytes 393224 | tf_op jit(solution)/shard_map/ppermute | solution.py:317
  23.9 3.4 %collective-permute-start.3 = (f32[2,32,512]{2,1,0:T(8,128)}, f32[2,32,512]{2,1,0:T(8,128)S(1)}, u32[]{:S(2)}, u32[]{:S(2)}) collective-permute-start(f32[2,32,512]{2,1,0:T(8,128)} %get-tuple-element.14), channel_id=1, source_target_pairs={{16,32},{48,64},{80,96},{112,128},{144,160},{176,192},{208,224},{2... | collective-permute-start | bytes 393224 | tf_op jit(solution)/shard_map/ppermute | solution.py:317
  27.3 0.1 pad_add_fusion.refs_0_
  27.4 0.0 copy-start
  27.4 0.0 copy-start.1
  27.4 0.0 copy-start.4
  27.4 0.0 collective-permute-done.n_first
  27.4 0.0 collective-permute-done.1.n_second
  27.4 0.0 copy-done.2
  27.4 0.0 copy-done.3
  27.5 0.0 copy-done.5
  27.5 0.5 shard_map.78
  28.0 0.0 collective-permute-done.2.x_first
  28.0 2.7 %collective-permute-done.3.x_second = f32[2,32,512]{2,1,0:T(8,128)S(1)} collective-permute-done((f32[2,32,512]{2,1,0:T(8,128)}, f32[2,32,512]{2,1,0:T(8,128)S(1)}, u32[]{:S(2)}, u32[]{:S(2)}) %collective-permute-start.3) | collective-permute-done | bytes 131104 | tf_op jit(solution)/shard_map/ppermute | solution.py:317
  30.7 0.0 copy-done
  30.7 0.0 copy-done.1
  30.7 0.0 copy-done.4
  30.7 0.9 shard_map.80
  31.6 48.4 %all_to_all.22 = f32[16,4,128]{2,1,0:T(4,128)S(1)} all-to-all(f32[16,4,128]{2,1,0:T(4,128)S(1)} %bitcast.18), channel_id=1, replica_groups=mesh['wide'=64,'narrow'=16] {'narrow'}, dimensions={0} | all-to-all | bytes 65536 | tf_op jit(solution)/shard_map/all_to_all | solution.py:321
  80.0 0.1 copy.8
  80.1 28.0 %all_to_all.23 = f32[64,1,256]{2,1,0:T(1,128)S(1)} all-to-all(f32[64,1,256]{2,1,0:T(1,128)S(1)} %copy.8), channel_id=1, replica_groups=mesh['wide'=64,'narrow'=16] {'wide'}, dimensions={0} | all-to-all | bytes 131072 | tf_op jit(solution)/shard_map/all_to_all | solution.py:321
  108.1 1.1 shard_map.81
  109.2 0.1 copy.9
  109.3 17.7 %all_to_all.24 = f32[64,1,256]{2,1,0:T(1,128)S(1)} all-to-all(f32[64,1,256]{2,1,0:T(1,128)S(1)} %copy.9), channel_id=1, replica_groups=mesh['wide'=64,'narrow'=16] {'wide'}, dimensions={0} | all-to-all | bytes 131072 | tf_op jit(solution)/shard_map/all_to_all | solution.py:321
  126.9 0.1 shard_map.83
  127.0 2.4 %collective-permute-start.4 = (f32[48,128]{1,0:T(8,128)S(1)}, f32[48,128]{1,0:T(8,128)S(1)}, u32[]{:S(2)}, u32[]{:S(2)}) collective-permute-start(f32[48,128]{1,0:T(8,128)S(1)} %get-tuple-element.18), channel_id=1, source_target_pairs={{0,1},{2,3},{4,5},{6,7},{8,9},{10,11},{12,13},{14,15},{1,0},{3,2},... | collective-permute-start | bytes 73736 | tf_op jit(solution)/shard_map/ppermute | solution.py:317
  129.4 0.7 collective-permute-start.5
  130.1 1.0 shard_map.82
  131.1 13.0 %collective-permute-done.4.first = f32[48,128]{1,0:T(8,128)S(1)} collective-permute-done((f32[48,128]{1,0:T(8,128)S(1)}, f32[48,128]{1,0:T(8,128)S(1)}, u32[]{:S(2)}, u32[]{:S(2)}) %collective-permute-start.4) | collective-permute-done | bytes 24608 | tf_op jit(solution)/shard_map/ppermute | solution.py:317
  144.1 0.0 collective-permute-done.5.second
  144.1 1.2 shard_map.84
  (4 shorter events, 0.0 us)
Async XLA Ops:
  2.3 25.2 %collective-permute-start = (f32[40,256]{1,0:T(8,128)}, f32[40,256]{1,0:T(8,128)S(1)}, u32[]{:S(2)}, u32[]{:S(2)}) collective-permute-start(f32[40,256]{1,0:T(8,128)} %get-tuple-element.11._), channel_id=1, source_target_pairs={{0,1},{2,3},{4,5},{6,7},{8,9},{10,11},{12,13},{14,15},{1,0},{3,2},... | collective-permute-start | bytes 122888 | tf_op jit(solution)/shard_map/ppermute | solution.py:317
  18.5 8.9 %copy-start.2 = (s32[16,2,256]{2,1,0:T(2,128)S(1)}, s32[16,2,256]{2,1,0:T(2,128)}, u32[]{:S(2)}) copy-start(s32[16,2,256]{2,1,0:T(2,128)} %solid.5) | copy-start | bytes 98308
  18.5 8.9 %copy-start.3 = (s32[16,2,256]{2,1,0:T(2,128)S(1)}, s32[16,2,256]{2,1,0:T(2,128)}, u32[]{:S(2)}) copy-start(s32[16,2,256]{2,1,0:T(2,128)} %void.5) | copy-start | bytes 98308
  18.5 8.9 %copy-start.5 = (f32[16,2,256]{2,1,0:T(2,128)S(1)}, f32[16,2,256]{2,1,0:T(2,128)}, u32[]{:S(2)}) copy-start(f32[16,2,256]{2,1,0:T(2,128)} %design.3) | copy-start | bytes 98308
  18.6 8.9 %collective-permute-start.1 = (f32[40,256]{1,0:T(8,128)}, f32[40,256]{1,0:T(8,128)S(1)}, u32[]{:S(2)}, u32[]{:S(2)}) collective-permute-start(f32[40,256]{1,0:T(8,128)} %get-tuple-element.12.__), channel_id=1, source_target_pairs={{1,2},{3,4},{5,6},{7,8},{9,10},{11,12},{13,14},{2,1},{4,3},{6,5},{... | collective-permute-start | bytes 122888 | tf_op jit(solution)/shard_map/ppermute | solution.py:317
  21.0 6.9 %collective-permute-start.2 = (f32[2,32,512]{2,1,0:T(8,128)}, f32[2,32,512]{2,1,0:T(8,128)S(1)}, u32[]{:S(2)}, u32[]{:S(2)}) collective-permute-start(f32[2,32,512]{2,1,0:T(8,128)} %get-tuple-element.13), channel_id=1, source_target_pairs={{0,16},{32,48},{64,80},{96,112},{128,144},{160,176},{192,208},{224... | collective-permute-start | bytes 393224 | tf_op jit(solution)/shard_map/ppermute | solution.py:317
  23.9 6.8 %collective-permute-start.3 = (f32[2,32,512]{2,1,0:T(8,128)}, f32[2,32,512]{2,1,0:T(8,128)S(1)}, u32[]{:S(2)}, u32[]{:S(2)}) collective-permute-start(f32[2,32,512]{2,1,0:T(8,128)} %get-tuple-element.14), channel_id=1, source_target_pairs={{16,32},{48,64},{80,96},{112,128},{144,160},{176,192},{208,224},{2... | collective-permute-start | bytes 393224 | tf_op jit(solution)/shard_map/ppermute | solution.py:317
  27.4 3.3 %copy-start = (f32[4,32,512]{2,1,0:T(8,128)S(1)}, f32[4,32,512]{2,1,0:T(8,128)}, u32[]{:S(2)}) copy-start(f32[4,32,512]{2,1,0:T(8,128)} %kirchhoff.1) | copy-start | bytes 786436
  27.4 3.3 %copy-start.1 = (f32[4,32,512]{2,1,0:T(8,128)S(1)}, f32[4,32,512]{2,1,0:T(8,128)}, u32[]{:S(2)}) copy-start(f32[4,32,512]{2,1,0:T(8,128)} %adjoint.1) | copy-start | bytes 786436
  27.4 3.3 %copy-start.4 = (bf16[4,32,512]{2,1,0:T(8,128)(2,1)S(1)}, bf16[4,32,512]{2,1,0:T(8,128)(2,1)}, u32[]{:S(2)}) copy-start(bf16[4,32,512]{2,1,0:T(8,128)(2,1)} %slope.1) | copy-start | bytes 393220
  127.0 17.0 %collective-permute-start.4 = (f32[48,128]{1,0:T(8,128)S(1)}, f32[48,128]{1,0:T(8,128)S(1)}, u32[]{:S(2)}, u32[]{:S(2)}) collective-permute-start(f32[48,128]{1,0:T(8,128)S(1)} %get-tuple-element.18), channel_id=1, source_target_pairs={{0,1},{2,3},{4,5},{6,7},{8,9},{10,11},{12,13},{14,15},{1,0},{3,2},... | collective-permute-start | bytes 73736 | tf_op jit(solution)/shard_map/ppermute | solution.py:317
  129.4 14.7 %collective-permute-start.5 = (f32[48,128]{1,0:T(8,128)S(1)}, f32[48,128]{1,0:T(8,128)S(1)}, u32[]{:S(2)}, u32[]{:S(2)}) collective-permute-start(f32[48,128]{1,0:T(8,128)S(1)} %get-tuple-element.19), channel_id=1, source_target_pairs={{1,2},{3,4},{5,6},{7,8},{9,10},{11,12},{13,14},{2,1},{4,3},{6,5},{... | collective-permute-start | bytes 73736 | tf_op jit(solution)/shard_map/ppermute | solution.py:317
